TPU v7x, 512 devices: a whole 4x4x16 slice. The times are simulated.
512 devices in a mesh: grp: 16 (over z_lo, y), dev: 32 (over x, z_hi, core).
Axes of the slice: x: 4, y: 4, z: 16 (z_hi: 4, z_lo: 4; z = z_hi * 4 + z_lo), core: 2. Of those that a mesh axis runs over, the one named last changes fastest.
Arguments:
- embedding: bfloat16 [524288, 256], P(('grp', 'dev')), may hold values from -6 to 6
- cotangent: bfloat16 [524288, 256], P(('grp', 'dev')), may hold values from -6 to 6
- fractional: bfloat16 [3, 524288], P(None, ('grp', 'dev')), may hold values from 0 to 1
- wave_index: int32 [3, 512], replicated, may hold values from -8 to 8
- tile_pairs: int32 [12288, 2], P(('grp', 'dev')), may hold values from 0 to 15, as said below
- counts: int32 [512], P(('grp', 'dev')), may hold values from 3 to 24, as said below
- wave_filter: float32 [512, 256], replicated, may hold values from -0.25 to 0.25
- short_weight: bfloat16 [256, 256], replicated, may hold values from -0.375 to 0.375
Outputs:
- message: bfloat16 [524288, 256], P(('grp', 'dev'))
- embedding_grad: bfloat16 [524288, 256], P(('grp', 'dev'))
Inputs may be any that keep to these rules, and one draw needn't show every extreme that they name: `tile_pairs`: in each block's 24 rows, column 0 is one of the block's 8 tiles and column 1 one of 16 tiles: the block's own, then the next block's. The first row of every block names a tile of the next block. `counts`: some block has exactly 24 live rows in every draw.
All inputs are finite; a program needn't handle non-finite values.
Results may differ from a plain program's by a relative error of at most 0.0059.
Values may be sent and summed in bfloat16 or wider, within the bound.
No kernel may reach another device: no remote copies, remote signals or barrier semaphores. Data moves between devices by JAX's collectives and lax.ppermute only.
A program may use at most 64 MiB of HBM per device.

v0:
```python
import math

import jax
import jax.numpy as jnp
from jax import lax
from jax.sharding import PartitionSpec as P

TILE = 128


two_pi = 2.0 * math.pi


def shifted(value, axis, by):
    size = lax.axis_size(axis)
    return lax.ppermute(value, axis, [(i, (i + by) % size) for i in range(size)])


def trig_table(places, wave_index):
    phase = two_pi * jnp.dot(
        places.astype(jnp.float32).T,
        wave_index.astype(jnp.float32),
        precision=lax.Precision.HIGHEST,
    )
    return jnp.concatenate([jnp.cos(phase), jnp.sin(phase)], axis=1).astype(jnp.bfloat16)


def pair_kernel(left_places, right_places):
    left = left_places.astype(jnp.float32)
    right = right_places.astype(jnp.float32)
    wave = jnp.sin(math.pi * (left[:, :, None] - right[:, None, :]))
    spread = jnp.exp(-2.0 * jnp.sum(wave * wave, axis=0))
    return (spread / math.sqrt(left.shape[1])).astype(jnp.bfloat16)


def pair_kernels(place_tiles, firsts, seconds):
    return jax.vmap(pair_kernel)(place_tiles[firsts], place_tiles[seconds])


def one_hot_rows(indices, keep, width):
    hits = (indices[:, None] == jnp.arange(width, dtype=jnp.int32)[None, :]) & keep[:, None]
    return hits.astype(jnp.float32)


def collect(hot, terms):
    return jnp.einsum("pt,pic->tic", hot, terms, precision=lax.Precision.HIGHEST)


def body(
    embedding, cotangent, fractional, wave_index, tile_pairs, counts, wave_filter, short_weight
):
    atom_rows, channels = embedding.shape
    wave_count = wave_index.shape[1]
    tile_count = atom_rows // TILE
    pair_rows = tile_pairs.shape[0]
    blocks = lax.axis_size("grp") * lax.axis_size("dev")
    inv_root = 1.0 / math.sqrt(atom_rows * blocks)
    table = trig_table(fractional, wave_index)
    joined = jnp.concatenate([embedding, cotangent], axis=1)
    rows = 2 * wave_count // blocks
    columns = table
    summed = lax.psum_scatter(
        lax.dot_general(
            columns, joined, (((0,), (0,)), ((), ())), preferred_element_type=jnp.float32
        ),
        ("grp", "dev"),
        scatter_dimension=0,
        tiled=True,
    )
    local = lax.dynamic_slice_in_dim(
        wave_filter, lax.axis_index(("grp", "dev")) * rows % wave_count, summed.shape[0], 0
    )
    tiled = jnp.concatenate([local, local], axis=1)
    coeffs = (summed * tiled * inv_root).astype(jnp.bfloat16)
    columns = table
    long_range = jnp.dot(
        columns,
        lax.all_gather(coeffs, ("grp", "dev"), axis=0, tiled=True),
        preferred_element_type=jnp.float32,
    )
    projected = jnp.dot(embedding, short_weight, preferred_element_type=jnp.float32).astype(
        jnp.bfloat16
    )
    above_projected, above_places = shifted((projected, fractional), ("grp", "dev"), -1)
    near_projected = jnp.concatenate([projected, above_projected], axis=0).reshape(
        2 * tile_count, TILE, channels
    )
    near_places = (
        jnp.concatenate([fractional, above_places], axis=1)
        .reshape(3, 2 * tile_count, TILE)
        .transpose(1, 0, 2)
    )
    cotangent_tiles = cotangent.reshape(tile_count, TILE, channels)
    firsts = tile_pairs[:, 0]
    seconds = tile_pairs[:, 1]
    live = jnp.arange(pair_rows, dtype=jnp.int32) < counts[0]
    kernels = pair_kernels(near_places, firsts, seconds)
    ahead = jnp.einsum(
        "pij,pjc->pic", kernels, near_projected[seconds], preferred_element_type=jnp.float32
    )
    behind = jnp.einsum(
        "pij,pic->pjc", kernels, cotangent_tiles[firsts], preferred_element_type=jnp.float32
    )
    forward = collect(one_hot_rows(firsts, live, tile_count), ahead)
    backward = collect(one_hot_rows(seconds, live, 2 * tile_count), behind)
    below = shifted(backward[tile_count:].astype(jnp.bfloat16), ("grp", "dev"), 1).astype(
        jnp.float32
    )
    own_back = backward[:tile_count]
    near_grad = (own_back + below).reshape(atom_rows, channels).astype(jnp.bfloat16)
    message = (long_range[:, :channels] + forward.reshape(atom_rows, channels)).astype(jnp.bfloat16)
    mixed = lax.dot_general(
        near_grad, short_weight, (((1,), (1,)), ((), ())), preferred_element_type=jnp.float32
    )
    embedding_grad = (long_range[:, channels:] + mixed).astype(jnp.bfloat16)
    return (message, embedding_grad)


def solution(mesh):
    in_specs = (
        P(("grp", "dev"), None),
        P(("grp", "dev"), None),
        P(None, ("grp", "dev")),
        P(),
        P(("grp", "dev"), None),
        P(("grp", "dev")),
        P(),
        P(),
    )
    out_specs = (P(("grp", "dev"), None), P(("grp", "dev"), None))
    return jax.shard_map(body, mesh=mesh, in_specs=in_specs, out_specs=out_specs, check_vma=False)
```

profile of v0, /device:TPU:1, one launch (start us, length us, event | category | flops | bytes accessed | tf_op | source)
XLA Modules:
  0.0 1305.8 jit_solution(4090141184728938035)
XLA Ops:
  7.2 8.9 collective-permute-start
  16.1 10.5 cosine_convert_fusion
  26.6 1.0 copy-done.8
  27.6 3.8 fusion.5
  31.4 0.0 all-gather.3.cloned.1.call-start
  31.5 0.8 copy-done.10
  32.3 0.3 convolution_convert_fusion
  32.6 10.1 collective-permute-start.1
  43.5 0.6 gather_fusion.3
  44.2 0.6 gather_fusion
  44.8 0.6 gather_fusion.1
  45.5 468.8 %all-reduce.3.cloned.1.call-done = f32[1024,512]{1,0:T(8,128)} async-done(((f32[1024,512]{1,0:T(8,128)}), f32[1024,512]{1,0:T(8,128)}) %all-reduce.3.cloned.1.call-update) | async-done | bytes 2097168
  514.3 1.2 fusion.28
  515.6 16.7 %multiply_reduce_fusion = f32[24,128,128]{2,1,0:T(8,128)S(1)} fusion(f32[24,3,128]{2,1,0:T(4,128)S(1)} %convert_element_type.49, f32[24,3,128]{2,1,0:T(4,128)S(1)} %convert_element_type.48), kind=kLoop, calls=%fused_computation.4 | loop fusion | flops 4325376 | bytes 1646592 | tf_op jit(solution)/shard_map/vmap()/reduce_sum | solution.py:32
  532.3 0.6 fusion.12
  532.9 0.5 copy-done.3
  533.4 3.1 fusion
  536.6 0.9 slice.50
  537.5 3.8 collective-permute-start.2
  541.4 1.1 pad_maximum_fusion.3
  542.5 1.9 gather_fusion.2
  544.4 2.0 fusion.13
  546.4 2.9 fusion.2
  549.2 0.3 copy.21
  549.6 15.1 %collective-permute-done.2 = bf16[8,128,256]{2,0,1:T(8,128)(2,1)} collective-permute-done((bf16[8,128,256]{2,0,1:T(8,128)(2,1)}, bf16[8,128,256]{2,0,1:T(8,128)(2,1)}, u32[]{:S(2)}, u32[]{:S(2)}) %collective-permute-start.2) | collective-permute-done | bytes 524320 | tf_op jit(solution)/shard_map/ppermute | solution.py:16
  564.7 1.2 fusion.7
  565.9 0.1 copy.24
  566.0 725.6 %all-gather.3.cloned.1.call-done = bf16[512,2,512]{2,1,0:T(2,128)(2,1)} async-done(((bf16[1,2,512]{2,1,0:T(2,128)(2,1)}), bf16[512,2,512]{2,1,0:T(2,128)(2,1)}) %all-gather.3.cloned.1.call-update) | async-done | bytes 1048592 | tf_op jit(solution)/shard_map/all_gather | solution.py:78
  1291.7 2.2 reshape.65
  1293.9 2.8 fusion.4
  1296.8 1.0 fusion.8
  1297.8 1.1 fusion.6
  (39 shorter events, 0.2 us)
Async XLA Ops:
  7.2 36.3 %copy-start = (f32[512,256]{1,0:T(8,128)S(1)}, f32[512,256]{1,0:T(8,128)}, u32[]{:S(2)}) copy-start(f32[512,256]{1,0:T(8,128)} %param.14) | copy-start | bytes 1572868
  7.2 20.4 %copy-start.5 = (bf16[1024,256]{1,0:T(8,128)(2,1)S(1)}, bf16[1024,256]{1,0:T(8,128)(2,1)}, u32[]{:S(2)}) copy-start(bf16[1024,256]{1,0:T(8,128)(2,1)} %param.9) | copy-start | bytes 1572868
  7.2 20.4 %copy-start.11 = (bf16[1024,256]{1,0:T(8,128)(2,1)S(1)}, bf16[1024,256]{1,0:T(8,128)(2,1)}, u32[]{:S(2)}) copy-start(bf16[1024,256]{1,0:T(8,128)(2,1)} %param.8) | copy-start | bytes 1572868
  7.2 507.1 %all-reduce.3.cloned.1.call-start = ((), (), s32[]{:S(2)}) async-start(), calls=%async_computation.1 | async-start | bytes 4194304
  7.2 36.9 %collective-permute-start = (bf16[3,1024]{1,0:T(4,128)(2,1)}, bf16[3,1024]{1,0:T(4,128)(2,1)S(1)}, u32[]{:S(2)}, u32[]{:S(2)}) collective-permute-start(bf16[3,1024]{1,0:T(4,128)(2,1)} %param.10), channel_id=1, source_target_pairs={{0,511},{1,0},{2,1},{3,2},{4,3},{5,4},{6,5},{7,6},{8,7},{9,8},{10,... | collective-permute-start | bytes 18440 | tf_op jit(solution)/shard_map/ppermute | solution.py:16
  26.6 1.0 copy-start.8
  31.4 0.9 copy-start.10
  31.4 12.1 copy-start.13
  31.4 12.8 copy-start.12
  31.4 1260.3 %all-gather.3.cloned.1.call-start = ((), (), s32[]{:S(2)}) async-start(), calls=%async_computation | async-start | bytes 1050624 | tf_op jit(solution)/shard_map/all_gather | solution.py:78
  32.6 499.7 %copy-start.6 = (bf16[1024,256]{1,0:T(8,128)(2,1)}, bf16[1024,256]{1,0:T(8,128)(2,1)S(1)}, u32[]{:S(2)}) copy-start(bf16[1024,256]{1,0:T(8,128)(2,1)S(1)} %convolution_convert_fusion) | copy-start | bytes 1572868
  32.6 508.8 %collective-permute-start.1 = (bf16[1024,256]{1,0:T(8,128)(2,1)S(1)}, bf16[1024,256]{1,0:T(8,128)(2,1)}, u32[]{:S(2)}, u32[]{:S(2)}) collective-permute-start(bf16[1024,256]{1,0:T(8,128)(2,1)S(1)} %convolution_convert_fusion), channel_id=1, source_target_pairs={{0,511},{1,0},{2,1},{3,2},{4,3},{5,4},{6,5},{7,6},{8,7},{9,8},{10,... | collective-permute-start | bytes 1572872 | tf_op jit(solution)/shard_map/ppermute | solution.py:16
  532.3 1.1 copy-start.3
  533.4 7.9 copy-start.7
  536.6 4.8 copy-start.1
  537.5 27.2 %collective-permute-start.2 = (bf16[8,128,256]{2,0,1:T(8,128)(2,1)}, bf16[8,128,256]{2,0,1:T(8,128)(2,1)}, u32[]{:S(2)}, u32[]{:S(2)}) collective-permute-start(bf16[8,128,256]{2,0,1:T(8,128)(2,1)} %slice.50), channel_id=1, source_target_pairs={{0,1},{1,2},{2,3},{3,4},{4,5},{5,6},{6,7},{7,8},{8,9},{9,10},{10,1... | collective-permute-start | bytes 1572872 | tf_op jit(solution)/shard_map/ppermute | solution.py:16
  542.5 1.9 copy-start.4
  549.2 15.5 %copy-start.2 = (f32[16,128,256]{2,0,1:T(8,128)S(1)}, f32[16,128,256]{2,0,1:T(8,128)}, u32[]{:S(2)}) copy-start(f32[16,128,256]{2,0,1:T(8,128)} %copy-done.1) | copy-start | bytes 6291460
  565.9 728.0 %copy-start.9 = (bf16[1024,512]{0,1:T(8,128)(2,1)S(1)}, bf16[1024,512]{0,1:T(8,128)(2,1)}, u32[]{:S(2)}) copy-start(bf16[1024,512]{0,1:T(8,128)(2,1)} %copy-done.8) | copy-start | bytes 3145732
Sparse Core Ops, SparseCore 0:
  31.5 482.7 all-reduce.2
  516.4 775.2 all-gather.2
where the time goes:
time: 1310 us
  waiting for transfers between devices  1210 us (92%)
  matrix products  27.1 us (2%)
  starting transfers between devices  22.9 us (2%)
  other arithmetic  21.4 us (2%)
  between operations  15 us (1%)
    all_gather x1, waiting for transfers between devices, body(): lax.all_gather(coeffs, ('grp', 'dev'), axis=0, tiled=True)  726 us
    unnamed x3, waiting for transfers between devices  469 us
  transfers between devices with their start and end apart: 5, of which 3 were waited for; matrix products, arithmetic and copies ran while one was open for 4% of the time, Pallas kernels for 0%

commit v1 on v0

v1 whole, which is shorter than its diff:
```python
import functools
import math

import jax
import jax.numpy as jnp
from jax import lax
from jax.experimental import pallas as pl
from jax.experimental.pallas import tpu as pltpu
from jax.sharding import Mesh
from jax.sharding import PartitionSpec as P


TILE = 128
FINE = ("z_lo", "y", "x", "z_hi", "core")
ALONG_Z = ("z_lo", "z_hi")
F32, BF16 = jnp.float32, jnp.bfloat16
VMEM = pl.BlockSpec(memory_space=pltpu.VMEM)
SMEM = pl.BlockSpec(memory_space=pltpu.SMEM)

COS = (
    0.9999999889445764,
    -19.73920446657614,
    64.93911592834654,
    -85.45011342750612,
    60.167429791960785,
    -25.966884612677454,
    6.527705963152031,
)
SIN = (
    6.283185302468581,
    -41.34170039298386,
    81.60513081114435,
    -76.70300555818746,
    42.02585148963868,
    -14.899578436725896,
    3.2377800860428168,
)


def cos_sin(turns):
    r = turns - jnp.floor(turns + 0.5)
    u = r * r
    c, s = COS[-1], SIN[-1]
    for k in COS[-2::-1]:
        c = c * u + k
    for k in SIN[-2::-1]:
        s = s * u + k
    return c, s * r


def dot(a, b, dims=((1,), (0,))):
    return lax.dot_general(a, b, (dims, ((), ())), preferred_element_type=F32)


def padded(rows):
    rows = rows.astype(F32)
    return jnp.concatenate([rows, jnp.zeros((5, rows.shape[1]), F32)], axis=0)


def sums_kernel(seat, waves_far, places_far, left_far, right_far, out, waves, places, left, right, turns, table, sems):
    half, atoms = turns.shape
    mine = pl.ds(pl.multiple_of(seat[0] * half, half), half)
    loads = [
        pltpu.make_async_copy(waves_far.at[:, mine], waves, sems.at[0]),
        pltpu.make_async_copy(places_far, places, sems.at[1]),
        pltpu.make_async_copy(left_far, left, sems.at[2]),
        pltpu.make_async_copy(right_far, right, sems.at[3]),
    ]
    for load in loads:
        load.start()
    loads[0].wait()
    loads[1].wait()
    turns[...] = dot(padded(waves[...]).astype(BF16), padded(places[...]).astype(BF16), ((0,), (0,)))

    @pl.loop(0, half // 16)
    def _(i):
        top = pl.ds(pl.multiple_of(i * 16, 16), 16)
        low = pl.ds(pl.multiple_of(half + i * 16, 16), 16)
        for j in range(atoms // 256):
            cols = pl.ds(j * 256, 256)
            c, s = cos_sin(turns[top, cols])
            table[top, cols] = c.astype(BF16)
            table[low, cols] = s.astype(BF16)

    for side, ref in enumerate((left, right)):
        loads[2 + side].wait()
        for block in range(2):
            part = dot(table[block * half : block * half + half, :], ref[...])
            for r in range(half // 8):
                i, k = divmod(block * (half // 8) + r, 4)
                for q in range(2):
                    out[i, k * 4 + side * 2 + q] = part[8 * r : 8 * r + 8, 128 * q : 128 * q + 128]


def partial_sums(seat, waves, places, left, right):
    half, atoms = waves.shape[1] // 2, places.shape[1]
    return pl.pallas_call(
        sums_kernel,
        out_shape=jax.ShapeDtypeStruct((16, 16, 8, 128), F32),
        in_specs=[SMEM] + [pl.BlockSpec(memory_space=pltpu.HBM)] * 4,
        out_specs=VMEM,
        scratch_shapes=[
            pltpu.VMEM((3, half), waves.dtype),
            pltpu.VMEM(places.shape, BF16),
            pltpu.VMEM(left.shape, BF16),
            pltpu.VMEM(right.shape, BF16),
            pltpu.VMEM((half, atoms), F32),
            pltpu.VMEM((2 * half, atoms), BF16),
            pltpu.SemaphoreType.DMA((4,)),
        ],
        compiler_params=pltpu.CompilerParams(vmem_limit_bytes=12 << 20),
        cost_estimate=pl.CostEstimate(
            flops=4 * half * atoms * 512, bytes_accessed=2 << 20, transcendentals=0
        ),
        name="sums",
    )(seat, *(pltpu.with_memory_space_constraint(v, pltpu.HBM) for v in (waves, places, left, right)))


def add_kernel(a, b, out):
    @pl.loop(0, a.shape[0])
    def _(i):
        out[i] = a[i] + b[i]


def add(a, b):
    return pl.pallas_call(
        add_kernel,
        out_shape=jax.ShapeDtypeStruct(a.shape, F32),
        in_specs=[VMEM] * 2,
        out_specs=VMEM,
        compiler_params=pltpu.CompilerParams(vmem_limit_bytes=4 << 20),
        name="add",
    )(a, b)


def gather_sum_kernel(a, out):
    @pl.loop(0, out.shape[0])
    def _(i):
        total = a[0, i]
        for k in range(1, a.shape[0]):
            total = total + a[k, i]
        out[i] = total


def gather_sum(a):
    return pl.pallas_call(
        gather_sum_kernel,
        out_shape=jax.ShapeDtypeStruct(a.shape[1:], F32),
        in_specs=[VMEM],
        out_specs=VMEM,
        compiler_params=pltpu.CompilerParams(vmem_limit_bytes=4 << 20),
        name="plane_sum",
    )(a)


def coefficients_kernel(a, scale, out):
    total = a[0]
    for k in range(1, a.shape[0]):
        total = total + a[k]
    mine = (total * scale[...]).astype(BF16)

    @pl.loop(0, out.shape[0] // 8)
    def _(i):
        for k in range(8):
            out[i * 8 + k] = mine


def coefficients(a, scale):
    return pl.pallas_call(
        coefficients_kernel,
        out_shape=jax.ShapeDtypeStruct((256, 8, 128), BF16),
        in_specs=[VMEM] * 2,
        out_specs=VMEM,
        compiler_params=pltpu.CompilerParams(vmem_limit_bytes=4 << 20),
        name="coefficients",
    )(a, scale)


def table_kernel(seat, waves, places, wave_filter, table, scale, turns, *, atoms_all):
    atoms, count = turns.shape
    half = count // 2
    turns[...] = dot(padded(places[...]).astype(BF16), padded(waves[...]).astype(BF16), ((0,), (0,)))

    @pl.loop(0, atoms // 16)
    def _(i):
        rows = pl.ds(pl.multiple_of(i * 16, 16), 16)
        for j in range(2):
            c, s = cos_sin(turns[rows, j * half : j * half + half])
            table[rows, 2 * j * half : (2 * j + 1) * half] = c.astype(BF16)
            table[rows, (2 * j + 1) * half : (2 * j + 2) * half] = s.astype(BF16)

    row, col = seat[1], seat[2]
    tile = wave_filter[pl.ds(pl.multiple_of(row * 8, 8), 8), pl.ds(pl.multiple_of(col * 128, 128), 128)]
    scale[...] = tile * (1.0 / math.sqrt(atoms_all))


def tables(seat, waves, places, wave_filter, atoms_all):
    atoms, count = places.shape[1], waves.shape[1]
    return pl.pallas_call(
        functools.partial(table_kernel, atoms_all=atoms_all),
        out_shape=(
            jax.ShapeDtypeStruct((atoms, 2 * count), BF16),
            jax.ShapeDtypeStruct((8, 128), F32),
        ),
        in_specs=[SMEM] + [VMEM] * 3,
        out_specs=(VMEM, VMEM),
        scratch_shapes=[pltpu.VMEM((atoms, count), F32)],
        compiler_params=pltpu.CompilerParams(vmem_limit_bytes=12 << 20),
        cost_estimate=pl.CostEstimate(flops=6 << 30, bytes_accessed=2 << 20, transcendentals=0),
        name="table",
    )(seat, waves, places, wave_filter)


def thirds(value):
    a = value.astype(BF16).astype(F32)
    b = (value - a).astype(BF16).astype(F32)
    return a, b, value - a - b


def features(places):
    coords = padded(places)
    live = lax.broadcasted_iota(jnp.int32, coords.shape, 0) < 3
    parts = [thirds(jnp.where(live, v, 0.0)) for v in cos_sin(coords)]
    left = jnp.concatenate([p[k] for k in (0, 0, 1, 1, 0, 2) for p in parts], axis=0)
    right = jnp.concatenate([p[k] for k in (0, 1, 0, 1, 2, 0) for p in parts], axis=0)
    return left, right


GROUP = 4


def near_kernel(
    pairs, count, embedding, embedding_above, cotangent, places, places_above, weight,
    ahead, behind, behind_next,
    projected, back, lefts, rights,
):
    atoms = embedding.shape[0]
    tiles = atoms // TILE
    projected[pl.ds(0, atoms), :] = dot(embedding[...], weight[...]).astype(BF16)
    projected[pl.ds(atoms, atoms), :] = dot(embedding_above[...], weight[...]).astype(BF16)
    left, right = features(places[...])
    _, right_above = features(places_above[...])
    lefts[...] = left.T.astype(BF16)
    for t in range(tiles):
        cut = slice(t * TILE, t * TILE + TILE)
        rights[t] = right[:, cut].astype(BF16)
        rights[tiles + t] = right_above[:, cut].astype(BF16)
    ahead[...] = jnp.zeros_like(ahead)
    back[...] = jnp.zeros_like(back)
    shift = -3.0 - 0.5 * math.log(TILE)

    def rows(t):
        return pl.ds(pl.multiple_of(t * TILE, TILE), TILE)

    @pl.loop(0, pairs.shape[0] // (2 * GROUP))
    def _(g):
        first, second, fore, rear = [], [], [], []
        for j in range(GROUP):
            p = g * GROUP + j
            u, v = pairs[2 * p], pairs[2 * p + 1]
            k = jnp.exp(dot(lefts[rows(u), :], rights[v]) + shift)
            k = jnp.where(p < count[0], k, 0.0)
            first.append(u)
            second.append(v)
            fore.append(dot(k.astype(BF16), projected[rows(v), :]))
            rear.append(dot(k.T.astype(BF16), cotangent[rows(u), :]))
        for u, v, f, r in zip(first, second, fore, rear, strict=True):
            ahead[rows(u), :] += f
            back[rows(v), :] += r

    behind[...] = back[pl.ds(0, atoms), :]
    behind_next[...] = back[pl.ds(atoms, atoms), :].astype(BF16)


def near(pairs, count, embedding, embedding_above, cotangent, places, places_above, weight):
    atoms, channels = embedding.shape
    tiles = atoms // TILE
    return pl.pallas_call(
        near_kernel,
        out_shape=(
            jax.ShapeDtypeStruct((atoms, channels), F32),
            jax.ShapeDtypeStruct((atoms, channels), F32),
            jax.ShapeDtypeStruct((atoms, channels), BF16),
        ),
        in_specs=[SMEM] * 2 + [VMEM] * 6,
        out_specs=(VMEM, VMEM, VMEM),
        scratch_shapes=[
            pltpu.VMEM((2 * atoms, channels), BF16),
            pltpu.VMEM((2 * atoms, channels), F32),
            pltpu.VMEM((atoms, 96), BF16),
            pltpu.VMEM((2 * tiles, 96, TILE), BF16),
        ],
        compiler_params=pltpu.CompilerParams(vmem_limit_bytes=16 << 20),
        cost_estimate=pl.CostEstimate(flops=10 << 30, bytes_accessed=4 << 20, transcendentals=0),
        name="near",
    )(pairs, count, embedding, embedding_above, cotangent, places, places_above, weight)


def mixed_kernel(own, below, weight, out):
    grad = (own[...] + below[...].astype(F32)).astype(BF16)
    out[...] = dot(grad, weight[...], ((1,), (1,)))


def mixing(own, below, weight):
    return pl.pallas_call(
        mixed_kernel,
        out_shape=jax.ShapeDtypeStruct(own.shape, F32),
        in_specs=[VMEM] * 3,
        out_specs=VMEM,
        compiler_params=pltpu.CompilerParams(vmem_limit_bytes=8 << 20),
        cost_estimate=pl.CostEstimate(flops=1 << 28, bytes_accessed=2 << 20, transcendentals=0),
        name="mixed",
    )(own, below, weight)


def final_kernel(order, seat, own, other, table, ahead, mixed, message, grad, matrix):
    channels = message.shape[1]

    @pl.when(pl.program_id(0) == 0)
    def _():
        for half, ref in ((seat[0], own), (1 - seat[0], other)):
            for r in range(0, 64, 2):
                rows = pl.ds(pl.multiple_of(half * 512 + 8 * r, 16), 16)
                for q in range(4):
                    pair = [ref[order[(r + d) * 4 + q]].astype(F32) for d in range(2)]
                    matrix[rows, 128 * q : 128 * q + 128] = jnp.concatenate(pair, axis=0).astype(BF16)

    message[...] = (dot(table[...], matrix[:, :channels]) + ahead[...]).astype(BF16)
    grad[...] = (dot(table[...], matrix[:, channels:]) + mixed[...]).astype(BF16)


def final(order, seat, own, other, table, ahead, mixed, steps=4):
    atoms, channels = ahead.shape
    rows = atoms // steps
    block = pl.BlockSpec((rows, channels), lambda i: (i, 0))
    whole = pl.BlockSpec(own.shape, lambda i: (0, 0, 0), pipeline_mode=pl.Buffered(1))
    return pl.pallas_call(
        functools.partial(final_kernel, order),
        grid=(steps,),
        out_shape=(jax.ShapeDtypeStruct((atoms, channels), BF16),) * 2,
        in_specs=[
            SMEM,
            whole,
            whole,
            pl.BlockSpec((rows, table.shape[1]), lambda i: (i, 0)),
            block,
            block,
        ],
        out_specs=(block, block),
        scratch_shapes=[pltpu.VMEM((table.shape[1], 2 * channels), BF16)],
        compiler_params=pltpu.CompilerParams(vmem_limit_bytes=16 << 20),
        cost_estimate=pl.CostEstimate(flops=1 << 30, bytes_accessed=4 << 20, transcendentals=0),
        name="final",
    )(seat, own, other, table, ahead, mixed)


def order_of_tiles():
    out = []
    for tile in range(256):
        y, x, z_lo, z_hi = tile // 64, tile // 16 % 4, tile // 4 % 4, tile % 4
        out.append(((z_lo * 4 + y) * 4 + x) * 4 + z_hi)
    return tuple(out)


def body(
    embedding, cotangent, fractional, wave_index, tile_pairs, counts, wave_filter, short_weight
):
    devices = math.prod(lax.axis_size(name) for name in FINE)
    atoms_all = embedding.shape[0] * devices
    core, x, y = (lax.axis_index(name).astype(jnp.int32) for name in ("core", "x", "y"))
    z_lo, z_hi = lax.axis_index("z_lo").astype(jnp.int32), lax.axis_index("z_hi").astype(jnp.int32)
    seat = jnp.stack([core, core * 32 + (y & 1) * 16 + x * 4 + z_lo, z_hi & 1])
    swap = [(0, 1), (1, 0)]

    given = lax.ppermute(
        partial_sums(1 - seat[:1], wave_index, fractional, embedding, cotangent), "core", swap
    )
    kept = partial_sums(seat[:1], wave_index, fractional, embedding, cotangent)
    chip = lax.all_to_all(add(kept, given), ("y", "x"), 0, 0, tiled=True)
    embedding_above = shifted(embedding, -1)
    places_above = shifted(fractional, -1)
    table, scale = tables(seat, wave_index, fractional, wave_filter, atoms_all)
    summed = gather_sum(chip)
    parts = lax.all_to_all(summed, ALONG_Z, 0, 0, tiled=True)
    ahead, behind, behind_next = near(
        tile_pairs.reshape(-1), counts, embedding, embedding_above, cotangent, fractional, places_above,
        short_weight,
    )
    below = shifted(behind_next, 1)
    mixed = mixing(behind, below, short_weight)
    spread = coefficients(parts, scale)
    coeffs = lax.all_to_all(spread, FINE[:4], 0, 0, tiled=True)
    other = lax.ppermute(coeffs, "core", swap)
    return final(order_of_tiles(), seat, coeffs, other, table, ahead, mixed)


def shifted(value, by):
    size = math.prod(lax.axis_size(name) for name in FINE)
    return lax.ppermute(value, FINE, [(i, (i + by) % size) for i in range(size)])


def solution(mesh):
    fine = Mesh(mesh.devices.reshape(4, 4, 4, 4, 2), FINE)
    rows, places, one = P(FINE, None), P(None, FINE), P(FINE)
    return jax.shard_map(
        body,
        mesh=fine,
        in_specs=(rows, rows, places, P(), rows, one, P(), P()),
        out_specs=(rows, rows),
        check_vma=False,
    )
```

time: 1310 us -> 162 us (0.12)
  the two profiles are of different devices: /device:TPU:1 before, /device:TPU:120 now
where the time goes in v1:
time: 162 us
  waiting for transfers between devices  73 us (45%)
  starting transfers between devices  57 us (35%)
  Pallas kernels  24.1 us (15%)
  local copies, waits for them, and re-layouts  6.09 us (4%)
    ppermute x3, waiting for transfers between devices, shifted(): lax.ppermute(value, FINE, [(i, (i + by) % size) for i in range(size)])  51.2 us
    ppermute x3, starting transfers between devices, shifted(): lax.ppermute(value, FINE, [(i, (i + by) % size) for i in range(size)])  16.4 us
    all_to_all x1, waiting for transfers between devices, body(): chip = lax.all_to_all(add(kept, given), ('y', 'x'), 0, 0, tiled=True)  16 us
    all_to_all x1, starting transfers between devices, body(): coeffs = lax.all_to_all(spread, FINE[:4], 0, 0, tiled=True)  15.1 us
    all_to_all x1, starting transfers between devices, body(): parts = lax.all_to_all(summed, ALONG_Z, 0, 0, tiled=True)  14.3 us
    pallas_call x1, Pallas kernels, near(): pl.pallas_call(near_kernel, out_shape=(jax.ShapeDtypeStruct((atoms, chann...  7.57 us
    all_to_all x1, starting transfers between devices, body(): chip = lax.all_to_all(add(kept, given), ('y', 'x'), 0, 0, tiled=True)  7.31 us
    pallas_call x2, Pallas kernels, partial_sums(): pl.pallas_call(sums_kernel, out_shape=jax.ShapeDtypeStruct((16, 16, 8, 12...  6.28 us
  transfers between devices with their start and end apart: 8, of which 4 were waited for; matrix products, arithmetic and copies ran while one was open for 0% of the time, Pallas kernels for 9%

profile of v1, /device:TPU:120, one launch (start us, length us, event | category | flops | bytes accessed | tf_op | source)
XLA Modules:
  0.0 161.7 jit_solution(9540380920130456088)
XLA Ops:
  0.6 3.1 %sums.3 = f32[16,16,8,128]{3,2,1,0:T(8,128)S(1)} custom-call(s32[1]{0:T(128)S(6)} %sub.3.seat, s32[3,512]{1,0:T(4,128)} %waves.1, bf16[3,1024]{1,0:T(4,128)(2,1)} %places.3, bf16[1024,256]{1,0:T(8,128)(2,1)} %embedding.1, bf16[1024,256]{1,0:T(8,128)(2,1)} %cotangent.1), custom_call_target="tpu_custom_call" | custom-call | flops 536870912 | bytes 2097152 | tf_op jit(solution)/shard_map/sums/pallas_call | solution.py:97
  3.8 1.9 %collective-permute-start = (f32[16,16,8,128]{3,2,1,0:T(8,128)S(1)}, f32[16,16,8,128]{3,2,1,0:T(8,128)S(1)}, u32[]{:S(2)}, u32[]{:S(2)}) collective-permute-start(f32[16,16,8,128]{3,2,1,0:T(8,128)S(1)} %sums.3), channel_id=1, source_target_pairs={{0,1},{1,0},{2,3},{3,2},{4,5},{5,4},{6,7},{7,6},{8,9},{9,8},{10,11... | collective-permute-start | bytes 3145736 | tf_op jit(solution)/shard_map/ppermute | solution.py:375
  5.7 3.1 %sums.2.a = f32[16,16,8,128]{3,2,1,0:T(8,128)S(1)} custom-call(s32[1]{0:T(128)} %bitcast.seat, s32[3,512]{1,0:T(4,128)} %waves.1, bf16[3,1024]{1,0:T(4,128)(2,1)} %places.3, bf16[1024,256]{1,0:T(8,128)(2,1)} %embedding.1, bf16[1024,256]{1,0:T(8,128)(2,1)} %cotangent.1), custom_call_target="tpu_custom_call" | custom-call | flops 536870912 | bytes 2097152 | tf_op jit(solution)/shard_map/sums/pallas_call | solution.py:97
  8.9 1.2 add.17
  10.0 7.3 %all-to-all-start = ((f32[16,16,8,128]{3,2,1,0:T(8,128)}), f32[16,16,8,128]{3,2,1,0:T(8,128)S(1)}, u32[]{:S(2)}, u32[]{:S(2)}) async-start(f32[16,16,8,128]{3,2,1,0:T(8,128)} %add.17), calls=%async_computation | async-start | bytes 2097152 | tf_op jit(solution)/shard_map/all_to_all | solution.py:379
  17.3 0.1 pad_add_fusion.seat
  17.4 16.0 %all-to-all-done.a = f32[16,16,8,128]{3,2,1,0:T(8,128)S(1)} async-done(((f32[16,16,8,128]{3,2,1,0:T(8,128)}), f32[16,16,8,128]{3,2,1,0:T(8,128)S(1)}, u32[]{:S(2)}, u32[]{:S(2)}) %all-to-all-start) | async-done | bytes 1048608 | tf_op jit(solution)/shard_map/all_to_all | solution.py:379
  33.4 0.9 plane_sum.1
  34.3 14.3 %all-to-all-start.1 = ((f32[16,8,128]{2,1,0:T(8,128)}), f32[16,8,128]{2,1,0:T(8,128)S(1)}, u32[]{:S(2)}, u32[]{:S(2)}) async-start(f32[16,8,128]{2,1,0:T(8,128)} %plane_sum.1), calls=%async_computation.1 | async-start | bytes 131072 | tf_op jit(solution)/shard_map/all_to_all | solution.py:384
  48.6 0.0 copy-start.10
  48.6 1.0 copy-done.10
  49.7 3.6 %table.1 = (bf16[1024,1024]{1,0:T(8,128)(2,1)S(1)}, f32[8,128]{1,0:T(8,128)S(1)}) custom-call(s32[3]{0:T(128)S(1)} %pad_add_fusion.seat, s32[3,512]{1,0:T(4,128)S(1)} %copy-done.8, bf16[3,1024]{1,0:T(4,128)(2,1)S(1)} %copy-done.9, f32[512,256]{1,0:T(8,128)S(1)} %copy-done.10), custom_call_target="tpu_custom_call" | custom-call | flops 6442450944 | bytes 2097152 | tf_op jit(solution)/shard_map/table/pallas_call | solution.py:199
  53.3 5.9 %all-to-all-done.1.a = f32[16,8,128]{2,1,0:T(8,128)S(1)} async-done(((f32[16,8,128]{2,1,0:T(8,128)}), f32[16,8,128]{2,1,0:T(8,128)S(1)}, u32[]{:S(2)}, u32[]{:S(2)}) %all-to-all-start.1) | async-done | bytes 65568 | tf_op jit(solution)/shard_map/all_to_all | solution.py:384
  59.2 0.2 coefficients.1
  59.4 0.0 copy-start.2
  59.4 0.8 copy-done.2
  60.2 15.1 %all-to-all-start.2 = ((bf16[256,8,128]{2,1,0:T(8,128)(2,1)}), bf16[256,8,128]{2,1,0:T(8,128)(2,1)}, u32[]{:S(2)}, u32[]{:S(2)}) async-start(bf16[256,8,128]{2,1,0:T(8,128)(2,1)} %copy-done.2), calls=%async_computation.2 | async-start | bytes 1048576 | tf_op jit(solution)/shard_map/all_to_all | solution.py:392
  75.3 5.1 %collective-permute-start.2 = (bf16[1024,256]{1,0:T(8,128)(2,1)S(1)}, bf16[1024,256]{1,0:T(8,128)(2,1)}, u32[]{:S(2)}, u32[]{:S(2)}) collective-permute-start(bf16[1024,256]{1,0:T(8,128)(2,1)S(1)} %copy-done), channel_id=1, source_target_pairs={{0,511},{1,0},{2,1},{3,2},{4,3},{5,4},{6,5},{7,6},{8,7},{9,8},{10,... | collective-permute-start | bytes 1572872 | tf_op jit(solution)/shard_map/ppermute | solution.py:399
  80.4 3.9 %collective-permute-start.3 = (bf16[3,1024]{1,0:T(4,128)(2,1)S(1)}, bf16[3,1024]{1,0:T(4,128)(2,1)S(1)}, u32[]{:S(2)}, u32[]{:S(2)}) collective-permute-start(bf16[3,1024]{1,0:T(4,128)(2,1)S(1)} %copy-done.9), channel_id=1, source_target_pairs={{0,511},{1,0},{2,1},{3,2},{4,3},{5,4},{6,5},{7,6},{8,7},{9,8},{10,... | collective-permute-start | bytes 18440 | tf_op jit(solution)/shard_map/ppermute | solution.py:399
  85.0 0.1 copy.11
  85.1 0.1 reshape.7.pairs
  85.2 31.7 %collective-permute-done.3.places_above = bf16[3,1024]{1,0:T(4,128)(2,1)S(1)} collective-permute-done((bf16[3,1024]{1,0:T(4,128)(2,1)S(1)}, bf16[3,1024]{1,0:T(4,128)(2,1)S(1)}, u32[]{:S(2)}, u32[]{:S(2)}) %collective-permute-start.3) | collective-permute-done | bytes 6176 | tf_op jit(solution)/shard_map/ppermute | solution.py:399
  116.8 7.6 %near.1 = (f32[1024,256]{1,0:T(8,128)S(1)}, f32[1024,256]{1,0:T(8,128)S(1)}, bf16[1024,256]{1,0:T(8,128)(2,1)}) custom-call(s32[48]{0:T(128)S(1)} %reshape.7.pairs, s32[1]{0:T(128)S(6)} %copy.12.count, bf16[1024,256]{1,0:T(8,128)(2,1)S(1)} %copy-done, bf16[1024,256]{1,0:T(8,128)(2,1)} %collective-permute-done.2.embedding_above, ...), custom_call_target="tpu_custom_call" | custom-call | flops 10737418240 | bytes 4194304 | tf_op jit(solution)/shard_map/near/pallas_call | solution.py:278
  124.4 1.0 copy-done.3
  125.4 1.0 copy-done.5
  126.4 7.4 %collective-permute-start.4 = (bf16[1024,256]{1,0:T(8,128)(2,1)}, bf16[1024,256]{1,0:T(8,128)(2,1)S(1)}, u32[]{:S(2)}, u32[]{:S(2)}) collective-permute-start(bf16[1024,256]{1,0:T(8,128)(2,1)} %get-tuple-element.11), channel_id=1, source_target_pairs={{0,1},{1,2},{2,3},{3,4},{4,5},{5,6},{6,7},{7,8},{8,9},{9,10},{10,1... | collective-permute-start | bytes 1572872 | tf_op jit(solution)/shard_map/ppermute | solution.py:399
  133.8 1.9 %collective-permute-start.1 = (bf16[256,8,128]{2,1,0:T(8,128)(2,1)}, bf16[256,8,128]{2,1,0:T(8,128)(2,1)S(1)}, u32[]{:S(2)}, u32[]{:S(2)}) collective-permute-start(bf16[256,8,128]{2,1,0:T(8,128)(2,1)} %all-to-all-done.2.own), channel_id=1, source_target_pairs={{0,1},{1,0},{2,3},{3,2},{4,5},{5,4},{6,7},{7,6},{8,9},{9,8},{10,11... | collective-permute-start | bytes 1572872 | tf_op jit(solution)/shard_map/ppermute | solution.py:393
  135.7 19.5 %collective-permute-done.4.below = bf16[1024,256]{1,0:T(8,128)(2,1)S(1)} collective-permute-done((bf16[1024,256]{1,0:T(8,128)(2,1)}, bf16[1024,256]{1,0:T(8,128)(2,1)S(1)}, u32[]{:S(2)}, u32[]{:S(2)}) %collective-permute-start.4) | collective-permute-done | bytes 524320 | tf_op jit(solution)/shard_map/ppermute | solution.py:399
  155.2 1.2 copy-done.4
  156.4 0.3 mixed.1
  156.8 0.9 copy-done.6
  157.6 4.0 %final.1 = (bf16[1024,256]{1,0:T(8,128)(2,1)}, bf16[1024,256]{1,0:T(8,128)(2,1)}) custom-call(s32[3]{0:T(128)S(1)} %pad_add_fusion.seat, bf16[256,8,128]{2,1,0:T(8,128)(2,1)} %all-to-all-done.2.own, bf16[256,8,128]{2,1,0:T(8,128)(2,1)S(1)} %collective-permute-done.1.other, bf16[1024,1024]{1,0:T(8,128)(2,1)S(1)} %get-tuple-element.8.table, ...), custom_call_target="tpu_custom_call" | custom-call | flops 1073741824 | bytes 4194304 | tf_op jit(solution)/shard_map/final/pallas_call | solution.py:337
  (20 shorter events, 0.0 us)
Async XLA Ops:
  3.8 5.1 %collective-permute-start = (f32[16,16,8,128]{3,2,1,0:T(8,128)S(1)}, f32[16,16,8,128]{3,2,1,0:T(8,128)S(1)}, u32[]{:S(2)}, u32[]{:S(2)}) collective-permute-start(f32[16,16,8,128]{3,2,1,0:T(8,128)S(1)} %sums.3), channel_id=1, source_target_pairs={{0,1},{1,0},{2,3},{3,2},{4,5},{5,4},{6,7},{7,6},{8,9},{9,8},{10,11... | collective-permute-start | bytes 3145736 | tf_op jit(solution)/shard_map/ppermute | solution.py:375
  10.0 38.6 %copy-start.8 = (s32[3,512]{1,0:T(4,128)S(1)}, s32[3,512]{1,0:T(4,128)}, u32[]{:S(2)}) copy-start(s32[3,512]{1,0:T(4,128)} %waves.1) | copy-start | bytes 18436
  10.0 38.6 %copy-start.9 = (bf16[3,1024]{1,0:T(4,128)(2,1)S(1)}, bf16[3,1024]{1,0:T(4,128)(2,1)}, u32[]{:S(2)}) copy-start(bf16[3,1024]{1,0:T(4,128)(2,1)} %places.3) | copy-start | bytes 18436
  10.0 23.4 %all-to-all-start = ((f32[16,16,8,128]{3,2,1,0:T(8,128)}), f32[16,16,8,128]{3,2,1,0:T(8,128)S(1)}, u32[]{:S(2)}, u32[]{:S(2)}) async-start(f32[16,16,8,128]{3,2,1,0:T(8,128)} %add.17), calls=%async_computation | async-start | bytes 2097152 | tf_op jit(solution)/shard_map/all_to_all | solution.py:379
  34.3 24.9 %all-to-all-start.1 = ((f32[16,8,128]{2,1,0:T(8,128)}), f32[16,8,128]{2,1,0:T(8,128)S(1)}, u32[]{:S(2)}, u32[]{:S(2)}) async-start(f32[16,8,128]{2,1,0:T(8,128)} %plane_sum.1), calls=%async_computation.1 | async-start | bytes 131072 | tf_op jit(solution)/shard_map/all_to_all | solution.py:384
  48.6 1.0 copy-start.10
  49.7 25.6 %copy-start = (bf16[1024,256]{1,0:T(8,128)(2,1)S(1)}, bf16[1024,256]{1,0:T(8,128)(2,1)}, u32[]{:S(2)}) copy-start(bf16[1024,256]{1,0:T(8,128)(2,1)} %embedding.1) | copy-start | bytes 1572868
  49.7 35.3 %copy-start.11 = (s32[24,2]{0,1:T(2,128)S(1)}, s32[24,2]{0,1:T(2,128)}, u32[]{:S(2)}) copy-start(s32[24,2]{0,1:T(2,128)} %param.12) | copy-start | bytes 580
  49.7 67.2 %copy-start.1 = (bf16[1024,256]{1,0:T(8,128)(2,1)S(1)}, bf16[1024,256]{1,0:T(8,128)(2,1)}, u32[]{:S(2)}) copy-start(bf16[1024,256]{1,0:T(8,128)(2,1)} %cotangent.1) | copy-start | bytes 1572868
  49.7 67.2 %copy-start.7 = (bf16[256,256]{1,0:T(8,128)(2,1)S(1)}, bf16[256,256]{1,0:T(8,128)(2,1)}, u32[]{:S(2)}) copy-start(bf16[256,256]{1,0:T(8,128)(2,1)} %weight.3) | copy-start | bytes 393220
  59.4 0.8 copy-start.2
  60.2 73.6 %all-to-all-start.2 = ((bf16[256,8,128]{2,1,0:T(8,128)(2,1)}), bf16[256,8,128]{2,1,0:T(8,128)(2,1)}, u32[]{:S(2)}, u32[]{:S(2)}) async-start(bf16[256,8,128]{2,1,0:T(8,128)(2,1)} %copy-done.2), calls=%async_computation.2 | async-start | bytes 1048576 | tf_op jit(solution)/shard_map/all_to_all | solution.py:392
  75.3 41.5 %collective-permute-start.2 = (bf16[1024,256]{1,0:T(8,128)(2,1)S(1)}, bf16[1024,256]{1,0:T(8,128)(2,1)}, u32[]{:S(2)}, u32[]{:S(2)}) collective-permute-start(bf16[1024,256]{1,0:T(8,128)(2,1)S(1)} %copy-done), channel_id=1, source_target_pairs={{0,511},{1,0},{2,1},{3,2},{4,3},{5,4},{6,5},{7,6},{8,7},{9,8},{10,... | collective-permute-start | bytes 1572872 | tf_op jit(solution)/shard_map/ppermute | solution.py:399
  80.4 36.4 %collective-permute-start.3 = (bf16[3,1024]{1,0:T(4,128)(2,1)S(1)}, bf16[3,1024]{1,0:T(4,128)(2,1)S(1)}, u32[]{:S(2)}, u32[]{:S(2)}) collective-permute-start(bf16[3,1024]{1,0:T(4,128)(2,1)S(1)} %copy-done.9), channel_id=1, source_target_pairs={{0,511},{1,0},{2,1},{3,2},{4,3},{5,4},{6,5},{7,6},{8,7},{9,8},{10,... | collective-permute-start | bytes 18440 | tf_op jit(solution)/shard_map/ppermute | solution.py:399
  124.4 1.0 copy-start.3
  125.4 1.0 copy-start.5
  126.4 28.8 %collective-permute-start.4 = (bf16[1024,256]{1,0:T(8,128)(2,1)}, bf16[1024,256]{1,0:T(8,128)(2,1)S(1)}, u32[]{:S(2)}, u32[]{:S(2)}) collective-permute-start(bf16[1024,256]{1,0:T(8,128)(2,1)} %get-tuple-element.11), channel_id=1, source_target_pairs={{0,1},{1,2},{2,3},{3,4},{4,5},{5,6},{6,7},{7,8},{8,9},{9,10},{10,1... | collective-permute-start | bytes 1572872 | tf_op jit(solution)/shard_map/ppermute | solution.py:399
  133.8 23.0 %collective-permute-start.1 = (bf16[256,8,128]{2,1,0:T(8,128)(2,1)}, bf16[256,8,128]{2,1,0:T(8,128)(2,1)S(1)}, u32[]{:S(2)}, u32[]{:S(2)}) collective-permute-start(bf16[256,8,128]{2,1,0:T(8,128)(2,1)} %all-to-all-done.2.own), channel_id=1, source_target_pairs={{0,1},{1,0},{2,3},{3,2},{4,5},{5,4},{6,7},{7,6},{8,9},{9,8},{10,11... | collective-permute-start | bytes 1572872 | tf_op jit(solution)/shard_map/ppermute | solution.py:393
  155.2 1.2 copy-start.4
  156.4 1.2 copy-start.6

commit v2 on v1

--- a/solution.py
+++ b/solution.py
@@ -113,7 +113,7 @@
             flops=4 * half * atoms * 512, bytes_accessed=2 << 20, transcendentals=0
         ),
         name="sums",
-    )(seat, *(pltpu.with_memory_space_constraint(v, pltpu.HBM) for v in (waves, places, left, right)))
+    )(seat, *map(in_hbm, (waves, places, left, right)))
 
 
 def add_kernel(a, b, out):
@@ -226,21 +226,73 @@
     return left, right
 
 
+PLACES, PAIRS, LIVE, ABOVE_ROWS, BELOW_ROWS = 1024, 1040, 1064, 1040, 1072
+
+
+def pack_kernel(embedding, cotangent, places, pairs, count, above, below, sems):
+    atoms = embedding.shape[0]
+    loads = [
+        pltpu.make_async_copy(embedding, above.at[pl.ds(0, atoms)], sems.at[0]),
+        pltpu.make_async_copy(cotangent, below.at[pl.ds(0, atoms)], sems.at[1]),
+    ]
+    for load in loads:
+        load.start()
+    width = above.shape[1]
+    coords = places[...].astype(F32)
+    rows = [coords[d : d + 1, k * width : k * width + width] for d in range(3) for k in range(4)]
+    rows = jnp.concatenate([*rows, jnp.zeros((4, width), F32)], axis=0).astype(BF16)
+    above[PLACES : PLACES + 16, :] = rows
+    below[PLACES : PLACES + 16, :] = rows
+    tail = jnp.where(lax.broadcasted_iota(jnp.int32, (32, width), 0) >= LIVE - PAIRS, count[0], 0)
+    below[PAIRS:BELOW_ROWS, :] = tail.astype(F32).astype(BF16)
+    below[PAIRS:LIVE, 0:2] = pairs[...].astype(F32).astype(BF16)
+    for load in loads:
+        load.wait()
+
+
+def pack(embedding, cotangent, places, pairs, count):
+    width = embedding.shape[1]
+    hbm = pl.BlockSpec(memory_space=pltpu.HBM)
+    return pl.pallas_call(
+        pack_kernel,
+        out_shape=(
+            jax.ShapeDtypeStruct((ABOVE_ROWS, width), BF16),
+            jax.ShapeDtypeStruct((BELOW_ROWS, width), BF16),
+        ),
+        in_specs=[hbm, hbm, VMEM, VMEM, SMEM],
+        out_specs=(VMEM, VMEM),
+        scratch_shapes=[pltpu.SemaphoreType.DMA((2,))],
+        compiler_params=pltpu.CompilerParams(vmem_limit_bytes=4 << 20),
+        name="pack",
+    )(in_hbm(embedding), in_hbm(cotangent), places, pairs, count)
+
+
+def in_hbm(value):
+    return pltpu.with_memory_space_constraint(value, pltpu.HBM)
+
+
 GROUP = 4
 
 
 def near_kernel(
-    pairs, count, embedding, embedding_above, cotangent, places, places_above, weight,
-    ahead, behind, behind_next,
-    projected, back, lefts, rights,
+    pairs, count, pairs_below, count_below, embedding, above, cotangent, below, places, weight,
+    ahead, mixed,
+    projected, back, lefts, lefts_below, rights, far_places,
 ):
-    atoms = embedding.shape[0]
+    atoms, width = embedding.shape
     tiles = atoms // TILE
     projected[pl.ds(0, atoms), :] = dot(embedding[...], weight[...]).astype(BF16)
-    projected[pl.ds(atoms, atoms), :] = dot(embedding_above[...], weight[...]).astype(BF16)
+    projected[pl.ds(atoms, atoms), :] = dot(above[pl.ds(0, atoms), :], weight[...]).astype(BF16)
+    for side, ref in enumerate((above, below)):
+        rows = ref[PLACES : PLACES + 16, :].astype(F32)
+        for d in range(3):
+            for k in range(4):
+                far_places[side, d : d + 1, k * width : k * width + width] = rows[4 * d + k : 4 * d + k + 1]
     left, right = features(places[...])
-    _, right_above = features(places_above[...])
+    _, right_above = features(far_places[0])
+    left_below, _ = features(far_places[1])
     lefts[...] = left.T.astype(BF16)
+    lefts_below[...] = left_below.T.astype(BF16)
     for t in range(tiles):
         cut = slice(t * TILE, t * TILE + TILE)
         rights[t] = right[:, cut].astype(BF16)
@@ -249,68 +301,54 @@
     back[...] = jnp.zeros_like(back)
     shift = -3.0 - 0.5 * math.log(TILE)
 
-    def rows(t):
+    def rows_of(t):
         return pl.ds(pl.multiple_of(t * TILE, TILE), TILE)
 
     @pl.loop(0, pairs.shape[0] // (2 * GROUP))
     def _(g):
-        first, second, fore, rear = [], [], [], []
+        fore, rear = [], []
         for j in range(GROUP):
             p = g * GROUP + j
             u, v = pairs[2 * p], pairs[2 * p + 1]
-            k = jnp.exp(dot(lefts[rows(u), :], rights[v]) + shift)
+            k = jnp.exp(dot(lefts[rows_of(u), :], rights[v]) + shift)
             k = jnp.where(p < count[0], k, 0.0)
-            first.append(u)
-            second.append(v)
-            fore.append(dot(k.astype(BF16), projected[rows(v), :]))
-            rear.append(dot(k.T.astype(BF16), cotangent[rows(u), :]))
-        for u, v, f, r in zip(first, second, fore, rear, strict=True):
-            ahead[rows(u), :] += f
-            back[rows(v), :] += r
-
-    behind[...] = back[pl.ds(0, atoms), :]
-    behind_next[...] = back[pl.ds(atoms, atoms), :].astype(BF16)
-
-
-def near(pairs, count, embedding, embedding_above, cotangent, places, places_above, weight):
+            fore.append((u, dot(k.astype(BF16), projected[rows_of(v), :])))
+            k = jnp.where(v < tiles, k, 0.0)
+            own = jnp.where(v < tiles, v, v - tiles)
+            rear.append((own, dot(k.T.astype(BF16), cotangent[rows_of(u), :])))
+            u, v = pairs_below[2 * p], pairs_below[2 * p + 1]
+            own = jnp.where(v < tiles, v, v - tiles)
+            k = jnp.exp(dot(lefts_below[rows_of(u), :], rights[own]) + shift)
+            k = jnp.where((p < count_below[0]) & (v >= tiles), k, 0.0)
+            rear.append((own, dot(k.T.astype(BF16), below[rows_of(u), :])))
+        for t, part in fore:
+            ahead[rows_of(t), :] += part
+        for t, part in rear:
+            back[rows_of(t), :] += part
+
+    mixed[...] = dot(back[...].astype(BF16), weight[...], ((1,), (1,)))
+
+
+def near(pairs, count, pairs_below, count_below, embedding, above, cotangent, below, places, weight):
     atoms, channels = embedding.shape
     tiles = atoms // TILE
     return pl.pallas_call(
         near_kernel,
-        out_shape=(
-            jax.ShapeDtypeStruct((atoms, channels), F32),
-            jax.ShapeDtypeStruct((atoms, channels), F32),
-            jax.ShapeDtypeStruct((atoms, channels), BF16),
-        ),
-        in_specs=[SMEM] * 2 + [VMEM] * 6,
-        out_specs=(VMEM, VMEM, VMEM),
+        out_shape=(jax.ShapeDtypeStruct((atoms, channels), F32),) * 2,
+        in_specs=[SMEM] * 4 + [VMEM] * 6,
+        out_specs=(VMEM, VMEM),
         scratch_shapes=[
             pltpu.VMEM((2 * atoms, channels), BF16),
-            pltpu.VMEM((2 * atoms, channels), F32),
+            pltpu.VMEM((atoms, channels), F32),
+            pltpu.VMEM((atoms, 96), BF16),
             pltpu.VMEM((atoms, 96), BF16),
             pltpu.VMEM((2 * tiles, 96, TILE), BF16),
+            pltpu.VMEM((2, 3, atoms), F32),
         ],
         compiler_params=pltpu.CompilerParams(vmem_limit_bytes=16 << 20),
         cost_estimate=pl.CostEstimate(flops=10 << 30, bytes_accessed=4 << 20, transcendentals=0),
         name="near",
-    )(pairs, count, embedding, embedding_above, cotangent, places, places_above, weight)
-
-
-def mixed_kernel(own, below, weight, out):
-    grad = (own[...] + below[...].astype(F32)).astype(BF16)
-    out[...] = dot(grad, weight[...], ((1,), (1,)))
-
-
-def mixing(own, below, weight):
-    return pl.pallas_call(
-        mixed_kernel,
-        out_shape=jax.ShapeDtypeStruct(own.shape, F32),
-        in_specs=[VMEM] * 3,
-        out_specs=VMEM,
-        compiler_params=pltpu.CompilerParams(vmem_limit_bytes=8 << 20),
-        cost_estimate=pl.CostEstimate(flops=1 << 28, bytes_accessed=2 << 20, transcendentals=0),
-        name="mixed",
-    )(own, below, weight)
+    )(pairs, count, pairs_below, count_below, embedding, above, cotangent, below, places, weight)
 
 
 def final_kernel(order, seat, own, other, table, ahead, mixed, message, grad, matrix):
@@ -351,7 +389,7 @@
         compiler_params=pltpu.CompilerParams(vmem_limit_bytes=16 << 20),
         cost_estimate=pl.CostEstimate(flops=1 << 30, bytes_accessed=4 << 20, transcendentals=0),
         name="final",
-    )(seat, own, other, table, ahead, mixed)
+    )(seat, own, other, *map(in_hbm, (table, ahead, mixed)))
 
 
 def order_of_tiles():
@@ -372,24 +410,25 @@
     seat = jnp.stack([core, core * 32 + (y & 1) * 16 + x * 4 + z_lo, z_hi & 1])
     swap = [(0, 1), (1, 0)]
 
-    given = lax.ppermute(
-        partial_sums(1 - seat[:1], wave_index, fractional, embedding, cotangent), "core", swap
-    )
+    to_above, to_below = pack(embedding, cotangent, fractional, tile_pairs, counts)
+    above = shifted(to_above, -1)
+    below = shifted(to_below, 1)
+    given = partial_sums(1 - seat[:1], wave_index, fractional, embedding, cotangent)
+    given = lax.ppermute(given, "core", swap)
     kept = partial_sums(seat[:1], wave_index, fractional, embedding, cotangent)
-    chip = lax.all_to_all(add(kept, given), ("y", "x"), 0, 0, tiled=True)
-    embedding_above = shifted(embedding, -1)
-    places_above = shifted(fractional, -1)
+    total = add(kept, given)
+    chip = lax.all_to_all(total, ("y", "x"), 0, 0, tiled=True)
     table, scale = tables(seat, wave_index, fractional, wave_filter, atoms_all)
     summed = gather_sum(chip)
     parts = lax.all_to_all(summed, ALONG_Z, 0, 0, tiled=True)
-    ahead, behind, behind_next = near(
-        tile_pairs.reshape(-1), counts, embedding, embedding_above, cotangent, fractional, places_above,
-        short_weight,
-    )
-    below = shifted(behind_next, 1)
-    mixed = mixing(behind, below, short_weight)
     spread = coefficients(parts, scale)
     coeffs = lax.all_to_all(spread, FINE[:4], 0, 0, tiled=True)
+    pairs_below = below[PAIRS:LIVE, 0:2].astype(jnp.int32).reshape(-1)
+    count_below = below[LIVE, 0:1].astype(jnp.int32)
+    ahead, mixed = near(
+        tile_pairs.reshape(-1), counts, pairs_below, count_below, embedding, above, cotangent, below,
+        fractional, short_weight,
+    )
     other = lax.ppermute(coeffs, "core", swap)
     return final(order_of_tiles(), seat, coeffs, other, table, ahead, mixed)
 

time: 162 us -> 148 us (0.914)
  the two profiles are of different devices: /device:TPU:120 before, /device:TPU:1 now
where the time goes in v2:
time: 148 us; the launch traced here: 147 us
  starting transfers between devices  70.4 us (48%)
  waiting for transfers between devices  42.8 us (29%)
  Pallas kernels  27.5 us (19%)
  local copies, waits for them, and re-layouts  4.08 us (3%)
  between operations  2.17 us (1%)
    ppermute x1, starting transfers between devices, body(): other = lax.ppermute(coeffs, 'core', swap)  26.2 us
    all_to_all x1, waiting for transfers between devices, body(): chip = lax.all_to_all(total, ('y', 'x'), 0, 0, tiled=True)  18.7 us
    ppermute x2, waiting for transfers between devices, shifted(): lax.ppermute(value, FINE, [(i, (i + by) % size) for i in range(size)])  17.4 us
    all_to_all x1, starting transfers between devices, body(): coeffs = lax.all_to_all(spread, FINE[:4], 0, 0, tiled=True)  11.5 us
    all_to_all x1, starting transfers between devices, body(): parts = lax.all_to_all(summed, ALONG_Z, 0, 0, tiled=True)  11.2 us
    ppermute x2, starting transfers between devices, shifted(): lax.ppermute(value, FINE, [(i, (i + by) % size) for i in range(size)])  8.91 us
    ppermute x1, starting transfers between devices, body(): given = lax.ppermute(given, 'core', swap)  8.75 us
    pallas_call x1, Pallas kernels, near(): pl.pallas_call(near_kernel, out_shape=(jax.ShapeDtypeStruct((atoms, chann...  8.33 us
  transfers between devices with their start and end apart: 7, of which 3 were waited for; matrix products, arithmetic and copies ran while one was open for 1% of the time, Pallas kernels for 11%

profile of v2, /device:TPU:1, one launch (start us, length us, event | category | flops | bytes accessed | tf_op | source)
XLA Modules:
  0.0 147.0 jit_solution(1151478293018452038)
XLA Ops:
  0.6 3.1 %sums.3 = f32[16,16,8,128]{3,2,1,0:T(8,128)S(1)} custom-call(s32[1]{0:T(128)S(6)} %sub.3.seat, s32[3,512]{1,0:T(4,128)} %waves.1, bf16[3,1024]{1,0:T(4,128)(2,1)} %places.5, bf16[1024,256]{1,0:T(8,128)(2,1)} %embedding.3, bf16[1024,256]{1,0:T(8,128)(2,1)} %cotangent.3), custom_call_target="tpu_custom_call" | custom-call | flops 536870912 | bytes 2097152 | tf_op jit(solution)/shard_map/sums/pallas_call | solution.py:97
  3.8 8.7 %collective-permute-start = (f32[16,16,8,128]{3,2,1,0:T(8,128)S(1)}, f32[16,16,8,128]{3,2,1,0:T(8,128)S(1)}, u32[]{:S(2)}, u32[]{:S(2)}) collective-permute-start(f32[16,16,8,128]{3,2,1,0:T(8,128)S(1)} %sums.3), channel_id=1, source_target_pairs={{0,1},{1,0},{2,3},{3,2},{4,5},{5,4},{6,7},{7,6},{8,9},{9,8},{10,11... | collective-permute-start | bytes 3145736 | tf_op jit(solution)/shard_map/ppermute | solution.py:417
  12.5 3.1 %sums.2.a = f32[16,16,8,128]{3,2,1,0:T(8,128)S(1)} custom-call(s32[1]{0:T(128)} %bitcast.seat, s32[3,512]{1,0:T(4,128)} %waves.1, bf16[3,1024]{1,0:T(4,128)(2,1)} %places.5, bf16[1024,256]{1,0:T(8,128)(2,1)} %embedding.3, bf16[1024,256]{1,0:T(8,128)(2,1)} %cotangent.3), custom_call_target="tpu_custom_call" | custom-call | flops 536870912 | bytes 2097152 | tf_op jit(solution)/shard_map/sums/pallas_call | solution.py:97
  15.7 0.0 collective-permute-done.b
  15.7 1.2 add.17
  16.9 3.8 %all-to-all-start = ((f32[16,16,8,128]{3,2,1,0:T(8,128)}), f32[16,16,8,128]{3,2,1,0:T(8,128)S(1)}, u32[]{:S(2)}, u32[]{:S(2)}) async-start(f32[16,16,8,128]{3,2,1,0:T(8,128)} %add.17), calls=%async_computation | async-start | bytes 2097152 | tf_op jit(solution)/shard_map/all_to_all | solution.py:420
  20.7 0.1 pad_add_fusion.seat
  20.8 18.7 %all-to-all-done.a = f32[16,16,8,128]{3,2,1,0:T(8,128)S(1)} async-done(((f32[16,16,8,128]{3,2,1,0:T(8,128)}), f32[16,16,8,128]{3,2,1,0:T(8,128)S(1)}, u32[]{:S(2)}, u32[]{:S(2)}) %all-to-all-start) | async-done | bytes 1048608 | tf_op jit(solution)/shard_map/all_to_all | solution.py:420
  39.5 0.9 plane_sum.1
  40.4 11.2 %all-to-all-start.1 = ((f32[16,8,128]{2,1,0:T(8,128)}), f32[16,8,128]{2,1,0:T(8,128)S(1)}, u32[]{:S(2)}, u32[]{:S(2)}) async-start(f32[16,8,128]{2,1,0:T(8,128)} %plane_sum.1), calls=%async_computation.1 | async-start | bytes 131072 | tf_op jit(solution)/shard_map/all_to_all | solution.py:423
  51.6 0.0 copy-start.9
  51.6 3.6 %table.1 = (bf16[1024,1024]{1,0:T(8,128)(2,1)S(1)}, f32[8,128]{1,0:T(8,128)S(1)}) custom-call(s32[3]{0:T(128)S(1)} %pad_add_fusion.seat, s32[3,512]{1,0:T(4,128)S(1)} %copy-done.6, bf16[3,1024]{1,0:T(4,128)(2,1)S(1)} %copy-done.5, f32[512,256]{1,0:T(8,128)S(1)} %copy-done.7), custom_call_target="tpu_custom_call" | custom-call | flops 6442450944 | bytes 2097152 | tf_op jit(solution)/shard_map/table/pallas_call | solution.py:199
  55.3 1.3 copy-done.2
  56.6 6.7 %all-to-all-done.1.a = f32[16,8,128]{2,1,0:T(8,128)S(1)} async-done(((f32[16,8,128]{2,1,0:T(8,128)}), f32[16,8,128]{2,1,0:T(8,128)S(1)}, u32[]{:S(2)}, u32[]{:S(2)}) %all-to-all-start.1) | async-done | bytes 65568 | tf_op jit(solution)/shard_map/all_to_all | solution.py:423
  63.3 1.0 coefficients.1
  64.2 11.5 %all-to-all-start.2 = ((bf16[256,8,128]{2,1,0:T(8,128)(2,1)}), bf16[256,8,128]{2,1,0:T(8,128)(2,1)S(1)}, u32[]{:S(2)}, u32[]{:S(2)}) async-start(bf16[256,8,128]{2,1,0:T(8,128)(2,1)} %coefficients.1), calls=%async_computation.2 | async-start | bytes 1048576 | tf_op jit(solution)/shard_map/all_to_all | solution.py:425
  76.4 0.1 copy.12.pairs
  76.5 1.2 pack.1
  77.7 7.0 %collective-permute-start.2 = (bf16[1072,256]{1,0:T(8,128)(2,1)S(1)}, bf16[1072,256]{1,0:T(8,128)(2,1)S(1)}, u32[]{:S(2)}, u32[]{:S(2)}) collective-permute-start(bf16[1072,256]{1,0:T(8,128)(2,1)S(1)} %get-tuple-element.10), channel_id=1, source_target_pairs={{0,1},{1,2},{2,3},{3,4},{4,5},{5,6},{6,7},{7,8},{8,9},{9,10},{10,1... | collective-permute-start | bytes 1646600 | tf_op jit(solution)/shard_map/ppermute | solution.py:438
  84.7 1.9 %collective-permute-start.3 = (bf16[1040,256]{1,0:T(8,128)(2,1)S(1)}, bf16[1040,256]{1,0:T(8,128)(2,1)}, u32[]{:S(2)}, u32[]{:S(2)}) collective-permute-start(bf16[1040,256]{1,0:T(8,128)(2,1)S(1)} %get-tuple-element.11), channel_id=1, source_target_pairs={{0,511},{1,0},{2,1},{3,2},{4,3},{5,4},{6,5},{7,6},{8,7},{9,8},{10,... | collective-permute-start | bytes 1597448 | tf_op jit(solution)/shard_map/ppermute | solution.py:438
  86.6 0.1 reshape.14.pairs
  86.7 17.4 %collective-permute-done.2.below = bf16[1072,256]{1,0:T(8,128)(2,1)S(1)} collective-permute-done((bf16[1072,256]{1,0:T(8,128)(2,1)S(1)}, bf16[1072,256]{1,0:T(8,128)(2,1)S(1)}, u32[]{:S(2)}, u32[]{:S(2)}) %collective-permute-start.2) | collective-permute-done | bytes 548896 | tf_op jit(solution)/shard_map/ppermute | solution.py:438
  104.1 0.5 slice.9
  105.3 0.1 reshape.18.pairs_below
  105.4 0.0 all-to-all-done.2.own
  105.4 26.2 %collective-permute-start.1 = (bf16[256,8,128]{2,1,0:T(8,128)(2,1)S(1)}, bf16[256,8,128]{2,1,0:T(8,128)(2,1)S(1)}, u32[]{:S(2)}, u32[]{:S(2)}) collective-permute-start(bf16[256,8,128]{2,1,0:T(8,128)(2,1)S(1)} %all-to-all-done.2.own), channel_id=1, source_target_pairs={{0,1},{1,0},{2,3},{3,2},{4,5},{5,4},{6,7},{7,6},{8,9},{9,8},{10,11... | collective-permute-start | bytes 1572872 | tf_op jit(solution)/shard_map/ppermute | solution.py:432
  131.7 0.0 collective-permute-done.3.above
  131.7 8.3 %near.1 = (f32[1024,256]{1,0:T(8,128)S(1)}, f32[1024,256]{1,0:T(8,128)S(1)}) custom-call(s32[48]{0:T(128)S(1)} %reshape.14.pairs, s32[1]{0:T(128)S(6)} %copy.14.count, s32[48]{0:T(128)S(1)} %reshape.18.pairs_below, s32[1]{0:T(128)S(6)} %convert.2.count_below, bf16[1024,256]{1,0:T(8,128)(2,1)S(1)} %copy-done, bf16[1040,256]{1,0:T(8,128)(2,1)} %collective-permute-done.3.above, ...), custom_call_target="tpu_custom_call" | custom-call | flops 10737418240 | bytes 4194304 | tf_op jit(solution)/shard_map/near/pallas_call | solution.py:335
  140.1 1.0 copy-done.3
  141.0 1.0 copy-done.4
  142.0 0.0 collective-permute-done.1.other
  142.0 5.0 %final.1 = (bf16[1024,256]{1,0:T(8,128)(2,1)}, bf16[1024,256]{1,0:T(8,128)(2,1)}) custom-call(s32[3]{0:T(128)S(1)} %pad_add_fusion.seat, bf16[256,8,128]{2,1,0:T(8,128)(2,1)S(1)} %all-to-all-done.2.own, bf16[256,8,128]{2,1,0:T(8,128)(2,1)S(1)} %collective-permute-done.1.other, bf16[1024,1024]{1,0:T(8,128)(2,1)} %copy-done.2, f32[1024,256]{1,0:T(8,128)} %copy-done.3, ...), custom_call_target="tpu_custom_call" | custom-call | flops 1073741824 | bytes 4194304 | tf_op jit(solution)/shard_map/final/pallas_call | solution.py:375
  (17 shorter events, 0.0 us)
Async XLA Ops:
  3.8 11.9 %collective-permute-start = (f32[16,16,8,128]{3,2,1,0:T(8,128)S(1)}, f32[16,16,8,128]{3,2,1,0:T(8,128)S(1)}, u32[]{:S(2)}, u32[]{:S(2)}) collective-permute-start(f32[16,16,8,128]{3,2,1,0:T(8,128)S(1)} %sums.3), channel_id=1, source_target_pairs={{0,1},{1,0},{2,3},{3,2},{4,5},{5,4},{6,7},{7,6},{8,9},{9,8},{10,11... | collective-permute-start | bytes 3145736 | tf_op jit(solution)/shard_map/ppermute | solution.py:417
  16.9 34.7 %copy-start.5 = (bf16[3,1024]{1,0:T(4,128)(2,1)S(1)}, bf16[3,1024]{1,0:T(4,128)(2,1)}, u32[]{:S(2)}) copy-start(bf16[3,1024]{1,0:T(4,128)(2,1)} %places.5) | copy-start | bytes 18436
  16.9 34.7 %copy-start.6 = (s32[3,512]{1,0:T(4,128)S(1)}, s32[3,512]{1,0:T(4,128)}, u32[]{:S(2)}) copy-start(s32[3,512]{1,0:T(4,128)} %waves.1) | copy-start | bytes 18436
  16.9 34.7 %copy-start.7 = (f32[512,256]{1,0:T(8,128)S(1)}, f32[512,256]{1,0:T(8,128)}, u32[]{:S(2)}) copy-start(f32[512,256]{1,0:T(8,128)} %wave_filter.1) | copy-start | bytes 1572868
  16.9 22.6 %all-to-all-start = ((f32[16,16,8,128]{3,2,1,0:T(8,128)}), f32[16,16,8,128]{3,2,1,0:T(8,128)S(1)}, u32[]{:S(2)}, u32[]{:S(2)}) async-start(f32[16,16,8,128]{3,2,1,0:T(8,128)} %add.17), calls=%async_computation | async-start | bytes 2097152 | tf_op jit(solution)/shard_map/all_to_all | solution.py:420
  40.4 22.9 %all-to-all-start.1 = ((f32[16,8,128]{2,1,0:T(8,128)}), f32[16,8,128]{2,1,0:T(8,128)S(1)}, u32[]{:S(2)}, u32[]{:S(2)}) async-start(f32[16,8,128]{2,1,0:T(8,128)} %plane_sum.1), calls=%async_computation.1 | async-start | bytes 131072 | tf_op jit(solution)/shard_map/all_to_all | solution.py:423
  51.6 24.8 %copy-start.9 = (s32[24,2]{0,1:T(2,128)S(1)}, s32[24,2]{0,1:T(2,128)}, u32[]{:S(2)}) copy-start(s32[24,2]{0,1:T(2,128)} %param.12) | copy-start | bytes 580
  55.3 1.3 copy-start.2
  56.6 75.1 %copy-start = (bf16[1024,256]{1,0:T(8,128)(2,1)S(1)}, bf16[1024,256]{1,0:T(8,128)(2,1)}, u32[]{:S(2)}) copy-start(bf16[1024,256]{1,0:T(8,128)(2,1)} %embedding.3) | copy-start | bytes 1572868
  56.6 75.1 %copy-start.1 = (bf16[1024,256]{1,0:T(8,128)(2,1)S(1)}, bf16[1024,256]{1,0:T(8,128)(2,1)}, u32[]{:S(2)}) copy-start(bf16[1024,256]{1,0:T(8,128)(2,1)} %cotangent.3) | copy-start | bytes 1572868
  56.6 75.1 %copy-start.8 = (bf16[256,256]{1,0:T(8,128)(2,1)S(1)}, bf16[256,256]{1,0:T(8,128)(2,1)}, u32[]{:S(2)}) copy-start(bf16[256,256]{1,0:T(8,128)(2,1)} %weight.1) | copy-start | bytes 393220
  64.2 41.2 %all-to-all-start.2 = ((bf16[256,8,128]{2,1,0:T(8,128)(2,1)}), bf16[256,8,128]{2,1,0:T(8,128)(2,1)S(1)}, u32[]{:S(2)}, u32[]{:S(2)}) async-start(bf16[256,8,128]{2,1,0:T(8,128)(2,1)} %coefficients.1), calls=%async_computation.2 | async-start | bytes 1048576 | tf_op jit(solution)/shard_map/all_to_all | solution.py:425
  77.7 26.4 %collective-permute-start.2 = (bf16[1072,256]{1,0:T(8,128)(2,1)S(1)}, bf16[1072,256]{1,0:T(8,128)(2,1)S(1)}, u32[]{:S(2)}, u32[]{:S(2)}) collective-permute-start(bf16[1072,256]{1,0:T(8,128)(2,1)S(1)} %get-tuple-element.10), channel_id=1, source_target_pairs={{0,1},{1,2},{2,3},{3,4},{4,5},{5,6},{6,7},{7,8},{8,9},{9,10},{10,1... | collective-permute-start | bytes 1646600 | tf_op jit(solution)/shard_map/ppermute | solution.py:438
  84.7 47.0 %collective-permute-start.3 = (bf16[1040,256]{1,0:T(8,128)(2,1)S(1)}, bf16[1040,256]{1,0:T(8,128)(2,1)}, u32[]{:S(2)}, u32[]{:S(2)}) collective-permute-start(bf16[1040,256]{1,0:T(8,128)(2,1)S(1)} %get-tuple-element.11), channel_id=1, source_target_pairs={{0,511},{1,0},{2,1},{3,2},{4,3},{5,4},{6,5},{7,6},{8,7},{9,8},{10,... | collective-permute-start | bytes 1597448 | tf_op jit(solution)/shard_map/ppermute | solution.py:438
  105.4 36.6 %collective-permute-start.1 = (bf16[256,8,128]{2,1,0:T(8,128)(2,1)S(1)}, bf16[256,8,128]{2,1,0:T(8,128)(2,1)S(1)}, u32[]{:S(2)}, u32[]{:S(2)}) collective-permute-start(bf16[256,8,128]{2,1,0:T(8,128)(2,1)S(1)} %all-to-all-done.2.own), channel_id=1, source_target_pairs={{0,1},{1,0},{2,3},{3,2},{4,5},{5,4},{6,7},{7,6},{8,9},{9,8},{10,11... | collective-permute-start | bytes 1572872 | tf_op jit(solution)/shard_map/ppermute | solution.py:432
  140.0 1.0 copy-start.3
  141.0 1.0 copy-start.4

commit v3 on v2

--- a/solution.py
+++ b/solution.py
@@ -158,22 +158,39 @@
     for k in range(1, a.shape[0]):
         total = total + a[k]
     mine = (total * scale[...]).astype(BF16)
-
-    @pl.loop(0, out.shape[0] // 8)
-    def _(i):
-        for k in range(8):
-            out[i * 8 + k] = mine
+    for k in range(out.shape[0]):
+        out[k] = mine
 
 
 def coefficients(a, scale):
     return pl.pallas_call(
         coefficients_kernel,
-        out_shape=jax.ShapeDtypeStruct((256, 8, 128), BF16),
+        out_shape=jax.ShapeDtypeStruct(a.shape, BF16),
         in_specs=[VMEM] * 2,
         out_specs=VMEM,
         compiler_params=pltpu.CompilerParams(vmem_limit_bytes=4 << 20),
         name="coefficients",
     )(a, scale)
+
+
+def copies_kernel(a, out):
+    for k in range(a.shape[0]):
+        mine = a[k]
+
+        @pl.loop(0, out.shape[0], unroll=True)
+        def _(i):
+            out[i, k] = mine
+
+
+def copies(a):
+    return pl.pallas_call(
+        copies_kernel,
+        out_shape=jax.ShapeDtypeStruct((16, *a.shape), BF16),
+        in_specs=[VMEM],
+        out_specs=VMEM,
+        compiler_params=pltpu.CompilerParams(vmem_limit_bytes=4 << 20),
+        name="copies",
+    )(a)
 
 
 def table_kernel(seat, waves, places, wave_filter, table, scale, turns, *, atoms_all):
@@ -226,65 +243,84 @@
     return left, right
 
 
-PLACES, PAIRS, LIVE, ABOVE_ROWS, BELOW_ROWS = 1024, 1040, 1064, 1040, 1072
-
-
-def pack_kernel(embedding, cotangent, places, pairs, count, above, below, sems):
+PLACES, PAIRS, LIVE, ROWS = 1024, 1040, 1048, 1056
+
+
+def pack_kernel(seat, embedding, cotangent, places_far, pairs, count, far, close, places, sems):
     atoms = embedding.shape[0]
+    positions = pltpu.make_async_copy(places_far, places, sems.at[2])
+    positions.start()
+
+    def both(forward, backward):
+        a = pltpu.make_async_copy(embedding, backward.at[pl.ds(0, atoms)], sems.at[0])
+        b = pltpu.make_async_copy(cotangent, forward.at[pl.ds(0, atoms)], sems.at[1])
+        a.start()
+        b.start()
+        return a, b
+
+    @pl.when(seat[0] == 0)
+    def _():
+        both(close, far)
+
+    @pl.when(seat[0] != 0)
+    def _():
+        both(far, close)
+
+    width = far.shape[1]
+    positions.wait()
+    coords = places[...].astype(F32)
+    rows = [coords[d : d + 1, k * width : k * width + width] for d in range(3) for k in range(4)]
+    rows = jnp.concatenate([*rows, jnp.zeros((4, width), F32)], axis=0).astype(BF16)
+    listed = jnp.concatenate([pairs[...].astype(F32), jnp.zeros((2, width - pairs.shape[1]), F32)], axis=1)
+    listed = jnp.concatenate([listed, jnp.zeros((6, width), F32)], axis=0)
+    tail = jnp.concatenate([listed, jnp.full((8, width), count[0], jnp.int32).astype(F32)], axis=0).astype(BF16)
+    for ref in (far, close):
+        ref[PLACES:PAIRS, :] = rows
+        ref[PAIRS:ROWS, :] = tail
+    pltpu.make_async_copy(embedding, far.at[pl.ds(0, atoms)], sems.at[0]).wait()
+    pltpu.make_async_copy(cotangent, close.at[pl.ds(0, atoms)], sems.at[1]).wait()
+
+
+def pack(seat, embedding, cotangent, places, pairs, count):
+    hbm = pl.BlockSpec(memory_space=pltpu.HBM)
+    return pl.pallas_call(
+        pack_kernel,
+        out_shape=(jax.ShapeDtypeStruct((ROWS, embedding.shape[1]), BF16),) * 2,
+        in_specs=[SMEM, hbm, hbm, hbm, VMEM, SMEM],
+        out_specs=(VMEM, VMEM),
+        scratch_shapes=[pltpu.VMEM(places.shape, BF16), pltpu.SemaphoreType.DMA((3,))],
+        compiler_params=pltpu.CompilerParams(vmem_limit_bytes=4 << 20),
+        name="pack",
+    )(seat, *map(in_hbm, (embedding, cotangent, places)), pairs, count)
+
+
+def in_hbm(value):
+    return pltpu.with_memory_space_constraint(value, pltpu.HBM)
+
+
+GROUP = 4
+
+
+def near_kernel(
+    seat, pairs, count, pairs_below, count_below, embedding, cotangent, far, close, places, weight,
+    ahead, mixed,
+    around, projected, back, lefts, lefts_below, rights, far_places, sems,
+):
+    atoms, width = embedding.shape
+    tiles = atoms // TILE
     loads = [
-        pltpu.make_async_copy(embedding, above.at[pl.ds(0, atoms)], sems.at[0]),
-        pltpu.make_async_copy(cotangent, below.at[pl.ds(0, atoms)], sems.at[1]),
+        pltpu.make_async_copy(close, around.at[seat[0]], sems.at[0]),
+        pltpu.make_async_copy(far, around.at[1 - seat[0]], sems.at[1]),
     ]
     for load in loads:
         load.start()
-    width = above.shape[1]
-    coords = places[...].astype(F32)
-    rows = [coords[d : d + 1, k * width : k * width + width] for d in range(3) for k in range(4)]
-    rows = jnp.concatenate([*rows, jnp.zeros((4, width), F32)], axis=0).astype(BF16)
-    above[PLACES : PLACES + 16, :] = rows
-    below[PLACES : PLACES + 16, :] = rows
-    tail = jnp.where(lax.broadcasted_iota(jnp.int32, (32, width), 0) >= LIVE - PAIRS, count[0], 0)
-    below[PAIRS:BELOW_ROWS, :] = tail.astype(F32).astype(BF16)
-    below[PAIRS:LIVE, 0:2] = pairs[...].astype(F32).astype(BF16)
+    projected[pl.ds(0, atoms), :] = dot(embedding[...], weight[...]).astype(BF16)
     for load in loads:
         load.wait()
-
-
-def pack(embedding, cotangent, places, pairs, count):
-    width = embedding.shape[1]
-    hbm = pl.BlockSpec(memory_space=pltpu.HBM)
-    return pl.pallas_call(
-        pack_kernel,
-        out_shape=(
-            jax.ShapeDtypeStruct((ABOVE_ROWS, width), BF16),
-            jax.ShapeDtypeStruct((BELOW_ROWS, width), BF16),
-        ),
-        in_specs=[hbm, hbm, VMEM, VMEM, SMEM],
-        out_specs=(VMEM, VMEM),
-        scratch_shapes=[pltpu.SemaphoreType.DMA((2,))],
-        compiler_params=pltpu.CompilerParams(vmem_limit_bytes=4 << 20),
-        name="pack",
-    )(in_hbm(embedding), in_hbm(cotangent), places, pairs, count)
-
-
-def in_hbm(value):
-    return pltpu.with_memory_space_constraint(value, pltpu.HBM)
-
-
-GROUP = 4
-
-
-def near_kernel(
-    pairs, count, pairs_below, count_below, embedding, above, cotangent, below, places, weight,
-    ahead, mixed,
-    projected, back, lefts, lefts_below, rights, far_places,
-):
-    atoms, width = embedding.shape
-    tiles = atoms // TILE
-    projected[pl.ds(0, atoms), :] = dot(embedding[...], weight[...]).astype(BF16)
+    above, below = around.at[0], around.at[1]
     projected[pl.ds(atoms, atoms), :] = dot(above[pl.ds(0, atoms), :], weight[...]).astype(BF16)
     for side, ref in enumerate((above, below)):
-        rows = ref[PLACES : PLACES + 16, :].astype(F32)
+        rows = ref[PLACES:PAIRS, :].astype(F32)
         for d in range(3):
             for k in range(4):
                 far_places[side, d : d + 1, k * width : k * width + width] = rows[4 * d + k : 4 * d + k + 1]
@@ -304,19 +340,19 @@
     def rows_of(t):
         return pl.ds(pl.multiple_of(t * TILE, TILE), TILE)
 
-    @pl.loop(0, pairs.shape[0] // (2 * GROUP))
+    @pl.loop(0, pairs.shape[1] // GROUP)
     def _(g):
         fore, rear = [], []
         for j in range(GROUP):
             p = g * GROUP + j
-            u, v = pairs[2 * p], pairs[2 * p + 1]
+            u, v = pairs[0, p], pairs[1, p]
             k = jnp.exp(dot(lefts[rows_of(u), :], rights[v]) + shift)
             k = jnp.where(p < count[0], k, 0.0)
             fore.append((u, dot(k.astype(BF16), projected[rows_of(v), :])))
             k = jnp.where(v < tiles, k, 0.0)
             own = jnp.where(v < tiles, v, v - tiles)
             rear.append((own, dot(k.T.astype(BF16), cotangent[rows_of(u), :])))
-            u, v = pairs_below[2 * p], pairs_below[2 * p + 1]
+            u, v = pairs_below[0, p], pairs_below[1, p]
             own = jnp.where(v < tiles, v, v - tiles)
             k = jnp.exp(dot(lefts_below[rows_of(u), :], rights[own]) + shift)
             k = jnp.where((p < count_below[0]) & (v >= tiles), k, 0.0)
@@ -329,29 +365,34 @@
     mixed[...] = dot(back[...].astype(BF16), weight[...], ((1,), (1,)))
 
 
-def near(pairs, count, pairs_below, count_below, embedding, above, cotangent, below, places, weight):
+def near(seat, pairs, count, pairs_below, count_below, embedding, cotangent, far, close, places, weight):
     atoms, channels = embedding.shape
     tiles = atoms // TILE
+    hbm = pl.BlockSpec(memory_space=pltpu.HBM)
     return pl.pallas_call(
         near_kernel,
         out_shape=(jax.ShapeDtypeStruct((atoms, channels), F32),) * 2,
-        in_specs=[SMEM] * 4 + [VMEM] * 6,
+        in_specs=[SMEM] * 5 + [VMEM] * 2 + [hbm] * 2 + [VMEM] * 2,
         out_specs=(VMEM, VMEM),
         scratch_shapes=[
+            pltpu.VMEM((2, ROWS, channels), BF16),
             pltpu.VMEM((2 * atoms, channels), BF16),
             pltpu.VMEM((atoms, channels), F32),
             pltpu.VMEM((atoms, 96), BF16),
             pltpu.VMEM((atoms, 96), BF16),
             pltpu.VMEM((2 * tiles, 96, TILE), BF16),
             pltpu.VMEM((2, 3, atoms), F32),
+            pltpu.SemaphoreType.DMA((2,)),
         ],
         compiler_params=pltpu.CompilerParams(vmem_limit_bytes=16 << 20),
         cost_estimate=pl.CostEstimate(flops=10 << 30, bytes_accessed=4 << 20, transcendentals=0),
         name="near",
-    )(pairs, count, pairs_below, count_below, embedding, above, cotangent, below, places, weight)
-
-
-def final_kernel(order, seat, own, other, table, ahead, mixed, message, grad, matrix):
+    )(
+        seat, pairs, count, pairs_below, count_below, embedding, cotangent, in_hbm(far), in_hbm(close), places, weight
+    )
+
+
+def final_kernel(seat, own, other, table, ahead, mixed, message, grad, matrix):
     channels = message.shape[1]
 
     @pl.when(pl.program_id(0) == 0)
@@ -360,20 +401,20 @@
             for r in range(0, 64, 2):
                 rows = pl.ds(pl.multiple_of(half * 512 + 8 * r, 16), 16)
                 for q in range(4):
-                    pair = [ref[order[(r + d) * 4 + q]].astype(F32) for d in range(2)]
+                    pair = [ref[(r + d) * 4 + q].astype(F32) for d in range(2)]
                     matrix[rows, 128 * q : 128 * q + 128] = jnp.concatenate(pair, axis=0).astype(BF16)
 
     message[...] = (dot(table[...], matrix[:, :channels]) + ahead[...]).astype(BF16)
     grad[...] = (dot(table[...], matrix[:, channels:]) + mixed[...]).astype(BF16)
 
 
-def final(order, seat, own, other, table, ahead, mixed, steps=4):
+def final(seat, own, other, table, ahead, mixed, steps=4):
     atoms, channels = ahead.shape
     rows = atoms // steps
     block = pl.BlockSpec((rows, channels), lambda i: (i, 0))
     whole = pl.BlockSpec(own.shape, lambda i: (0, 0, 0), pipeline_mode=pl.Buffered(1))
     return pl.pallas_call(
-        functools.partial(final_kernel, order),
+        final_kernel,
         grid=(steps,),
         out_shape=(jax.ShapeDtypeStruct((atoms, channels), BF16),) * 2,
         in_specs=[
@@ -392,14 +433,6 @@
     )(seat, own, other, *map(in_hbm, (table, ahead, mixed)))
 
 
-def order_of_tiles():
-    out = []
-    for tile in range(256):
-        y, x, z_lo, z_hi = tile // 64, tile // 16 % 4, tile // 4 % 4, tile % 4
-        out.append(((z_lo * 4 + y) * 4 + x) * 4 + z_hi)
-    return tuple(out)
-
-
 def body(
     embedding, cotangent, fractional, wave_index, tile_pairs, counts, wave_filter, short_weight
 ):
@@ -410,32 +443,29 @@
     seat = jnp.stack([core, core * 32 + (y & 1) * 16 + x * 4 + z_lo, z_hi & 1])
     swap = [(0, 1), (1, 0)]
 
-    to_above, to_below = pack(embedding, cotangent, fractional, tile_pairs, counts)
-    above = shifted(to_above, -1)
-    below = shifted(to_below, 1)
+    listed = tile_pairs.T
+    to_far, to_close = pack(seat[:1], embedding, cotangent, fractional, listed, counts)
+    size = math.prod(lax.axis_size(name) for name in FINE)
+    far = lax.ppermute(to_far, FINE, [(i, (i + (1 if i % 2 else -1)) % size) for i in range(size)])
     given = partial_sums(1 - seat[:1], wave_index, fractional, embedding, cotangent)
     given = lax.ppermute(given, "core", swap)
     kept = partial_sums(seat[:1], wave_index, fractional, embedding, cotangent)
     total = add(kept, given)
     chip = lax.all_to_all(total, ("y", "x"), 0, 0, tiled=True)
+    close = lax.ppermute(to_close, "core", swap)
     table, scale = tables(seat, wave_index, fractional, wave_filter, atoms_all)
     summed = gather_sum(chip)
     parts = lax.all_to_all(summed, ALONG_Z, 0, 0, tiled=True)
-    spread = coefficients(parts, scale)
-    coeffs = lax.all_to_all(spread, FINE[:4], 0, 0, tiled=True)
-    pairs_below = below[PAIRS:LIVE, 0:2].astype(jnp.int32).reshape(-1)
-    count_below = below[LIVE, 0:1].astype(jnp.int32)
+    tail = jnp.where(seat[0] == 0, far[PAIRS:ROWS, :TILE], close[PAIRS:ROWS, :TILE]).astype(jnp.int32)
+    pairs_below, count_below = tail[0:2, : listed.shape[1]], tail[LIVE - PAIRS, 0:1]
+    mine = lax.all_to_all(coefficients(parts, scale), ALONG_Z, 0, 0, tiled=True)
     ahead, mixed = near(
-        tile_pairs.reshape(-1), counts, pairs_below, count_below, embedding, above, cotangent, below,
-        fractional, short_weight,
+        seat[:1], listed, counts, pairs_below, count_below, embedding, cotangent, far, close, fractional,
+        short_weight,
     )
+    coeffs = lax.all_to_all(copies(mine), ("y", "x"), 0, 0, tiled=True).reshape(256, 8, 128)
     other = lax.ppermute(coeffs, "core", swap)
-    return final(order_of_tiles(), seat, coeffs, other, table, ahead, mixed)
-
-
-def shifted(value, by):
-    size = math.prod(lax.axis_size(name) for name in FINE)
-    return lax.ppermute(value, FINE, [(i, (i + by) % size) for i in range(size)])
+    return final(seat, coeffs, other, table, ahead, mixed)
 
 
 def solution(mesh):

time: 148 us -> 122 us (0.82)
  starting transfers between devices: 70.4 us -> 46 us
  waiting for transfers between devices: 42.8 us -> 20 us
  blocking collectives: 0 us -> 20.6 us
    all_to_all x0 -> x1, blocking collectives: none -> 20.6 us  [body(): mine = lax.all_to_all(coefficients(parts, scale), ALONG_Z, 0, 0, tiled=True)]
    ppermute x1, starting transfers between devices: 26.2 us -> 7.1 us  [body(): other = lax.ppermute(coeffs, 'core', swap)]
    ppermute x2, waiting for transfers between devices: 17.4 us -> 0.01 us  [the longest x1 0.01 us: body(): lax.ppermute(to_far, FINE, [(i, (i + (1 if i % 2 else -1)) % size) for i...]
    all_to_all x1, waiting for transfers between devices: 18.7 us -> 5.43 us  [body(): chip = lax.all_to_all(total, ('y', 'x'), 0, 0, tiled=True)]
    all_to_all x1, starting transfers between devices: 11.5 us -> 3.57 us  [body(): lax.all_to_all(copies(mine), ('y', 'x'), 0, 0, tiled=True)]
    all_to_all x1, waiting for transfers between devices: 0.01 us -> 7.82 us  [body(): lax.all_to_all(copies(mine), ('y', 'x'), 0, 0, tiled=True)]
    ppermute x2, starting transfers between devices: 8.91 us -> 15.6 us  [the longest x1 8.85 us: body(): close = lax.ppermute(to_close, 'core', swap)]
    all_to_all x1, starting transfers between devices: 11.2 us -> 7.21 us  [body(): parts = lax.all_to_all(summed, ALONG_Z, 0, 0, tiled=True)]
  transfers between devices with their start and end apart: 7 -> 7, of which waited for: 3 -> 3; matrix products, arithmetic and copies ran while one was open for 1% -> 1% of each run, Pallas kernels for 11% -> 16%
where the time goes in v3:
time: 122 us; the launch traced here: 121 us
  starting transfers between devices  46 us (38%)
  Pallas kernels  28.6 us (23%)
  blocking collectives  20.6 us (17%)
  waiting for transfers between devices  20 us (16%)
  local copies, waits for them, and re-layouts  3.79 us (3%)
  between operations  1.53 us (1%)
    all_to_all x1, blocking collectives, body(): mine = lax.all_to_all(coefficients(parts, scale), ALONG_Z, 0, 0, tiled=True)  20.6 us
    pallas_call x1, Pallas kernels, near(): pl.pallas_call(near_kernel, out_shape=(jax.ShapeDtypeStruct((atoms, chann...  9.54 us
    ppermute x1, starting transfers between devices, body(): close = lax.ppermute(to_close, 'core', swap)  8.85 us
    ppermute x1, starting transfers between devices, body(): given = lax.ppermute(given, 'core', swap)  8.75 us
    all_to_all x1, waiting for transfers between devices, body(): lax.all_to_all(copies(mine), ('y', 'x'), 0, 0, tiled=True)  7.82 us
    all_to_all x1, starting transfers between devices, body(): parts = lax.all_to_all(summed, ALONG_Z, 0, 0, tiled=True)  7.21 us
    ppermute x1, starting transfers between devices, body(): other = lax.ppermute(coeffs, 'core', swap)  7.1 us
    all_to_all x1, waiting for transfers between devices, body(): parts = lax.all_to_all(summed, ALONG_Z, 0, 0, tiled=True)  6.76 us
  transfers between devices with their start and end apart: 7, of which 3 were waited for; matrix products, arithmetic and copies ran while one was open for 1% of the time, Pallas kernels for 16%

profile of v3, /device:TPU:1, one launch (start us, length us, event | category | flops | bytes accessed | tf_op | source)
XLA Modules:
  0.0 121.3 jit_solution(12166875209897222722)
XLA Ops:
  0.6 3.1 %sums.3 = f32[16,16,8,128]{3,2,1,0:T(8,128)S(1)} custom-call(s32[1]{0:T(128)S(6)} %sub.3.seat, s32[3,512]{1,0:T(4,128)} %waves.1, bf16[3,1024]{1,0:T(4,128)(2,1)} %places.3, bf16[1024,256]{1,0:T(8,128)(2,1)} %embedding.3, bf16[1024,256]{1,0:T(8,128)(2,1)} %cotangent.3), custom_call_target="tpu_custom_call" | custom-call | flops 536870912 | bytes 2097152 | tf_op jit(solution)/shard_map/sums/pallas_call | solution.py:97
  3.8 8.7 %collective-permute-start = (f32[16,16,8,128]{3,2,1,0:T(8,128)S(1)}, f32[16,16,8,128]{3,2,1,0:T(8,128)S(1)}, u32[]{:S(2)}, u32[]{:S(2)}) collective-permute-start(f32[16,16,8,128]{3,2,1,0:T(8,128)S(1)} %sums.3), channel_id=1, source_target_pairs={{0,1},{1,0},{2,3},{3,2},{4,5},{5,4},{6,7},{7,6},{8,9},{9,8},{10,11... | collective-permute-start | bytes 3145736 | tf_op jit(solution)/shard_map/ppermute | solution.py:451
  12.5 3.1 %sums.2.a = f32[16,16,8,128]{3,2,1,0:T(8,128)S(1)} custom-call(s32[1]{0:T(128)} %bitcast.seat, s32[3,512]{1,0:T(4,128)} %waves.1, bf16[3,1024]{1,0:T(4,128)(2,1)} %places.3, bf16[1024,256]{1,0:T(8,128)(2,1)} %embedding.3, bf16[1024,256]{1,0:T(8,128)(2,1)} %cotangent.3), custom_call_target="tpu_custom_call" | custom-call | flops 536870912 | bytes 2097152 | tf_op jit(solution)/shard_map/sums/pallas_call | solution.py:97
  15.7 0.0 copy-start.7
  15.7 0.0 collective-permute-done.b
  15.7 1.2 add.17
  16.9 3.8 %all-to-all-start = ((f32[16,16,8,128]{3,2,1,0:T(8,128)}), f32[16,16,8,128]{3,2,1,0:T(8,128)S(1)}, u32[]{:S(2)}, u32[]{:S(2)}) async-start(f32[16,16,8,128]{3,2,1,0:T(8,128)} %add.17), calls=%async_computation | async-start | bytes 2097152 | tf_op jit(solution)/shard_map/all_to_all | solution.py:454
  21.3 1.2 %pack.1 = (bf16[1056,256]{1,0:T(8,128)(2,1)S(1)}, bf16[1056,256]{1,0:T(8,128)(2,1)S(1)}) custom-call(s32[1]{0:T(128)} %bitcast.seat, bf16[1024,256]{1,0:T(8,128)(2,1)} %embedding.3, bf16[1024,256]{1,0:T(8,128)(2,1)} %cotangent.3, bf16[3,1024]{1,0:T(4,128)(2,1)} %places.3, s32[2,24]{1,0:T(2,128)S(1)} %bitcast.8, s32[1]{0:T(128)S(6)} %copy.10.count), custom_call_target="tpu_custom_call" | custom-call | tf_op jit(solution)/shard_map/pack/pallas_call | solution.py:286
  22.6 6.8 %collective-permute-start.2 = (bf16[1056,256]{1,0:T(8,128)(2,1)S(1)}, bf16[1056,256]{1,0:T(8,128)(2,1)}, u32[]{:S(2)}, u32[]{:S(2)}) collective-permute-start(bf16[1056,256]{1,0:T(8,128)(2,1)S(1)} %get-tuple-element.10), channel_id=1, source_target_pairs={{0,511},{1,2},{2,1},{3,4},{4,3},{5,6},{6,5},{7,8},{8,7},{9,10},{10... | collective-permute-start | bytes 1622024 | tf_op jit(solution)/shard_map/ppermute | solution.py:449
  29.3 8.9 %collective-permute-start.3 = (bf16[1056,256]{1,0:T(8,128)(2,1)S(1)}, bf16[1056,256]{1,0:T(8,128)(2,1)}, u32[]{:S(2)}, u32[]{:S(2)}) collective-permute-start(bf16[1056,256]{1,0:T(8,128)(2,1)S(1)} %get-tuple-element.11), channel_id=1, source_target_pairs={{0,1},{1,0},{2,3},{3,2},{4,5},{5,4},{6,7},{7,6},{8,9},{9,8},{10,11... | collective-permute-start | bytes 1622024 | tf_op jit(solution)/shard_map/ppermute | solution.py:455
  38.2 0.1 pad_add_fusion.seat
  38.3 5.4 %all-to-all-done.a = f32[16,16,8,128]{3,2,1,0:T(8,128)S(1)} async-done(((f32[16,16,8,128]{3,2,1,0:T(8,128)}), f32[16,16,8,128]{3,2,1,0:T(8,128)S(1)}, u32[]{:S(2)}, u32[]{:S(2)}) %all-to-all-start) | async-done | bytes 1048608 | tf_op jit(solution)/shard_map/all_to_all | solution.py:454
  43.7 0.9 plane_sum.1
  44.6 7.2 %all-to-all-start.1 = ((f32[16,8,128]{2,1,0:T(8,128)}), f32[16,8,128]{2,1,0:T(8,128)S(1)}, u32[]{:S(2)}, u32[]{:S(2)}) async-start(f32[16,8,128]{2,1,0:T(8,128)} %plane_sum.1), calls=%async_computation.1 | async-start | bytes 131072 | tf_op jit(solution)/shard_map/all_to_all | solution.py:458
  51.9 0.0 copy-start
  51.9 0.0 copy-start.1
  51.9 0.0 copy-start.9
  51.9 3.6 %table.1 = (bf16[1024,1024]{1,0:T(8,128)(2,1)S(1)}, f32[8,128]{1,0:T(8,128)S(1)}) custom-call(s32[3]{0:T(128)S(1)} %pad_add_fusion.seat, s32[3,512]{1,0:T(4,128)S(1)} %copy-done.6, bf16[3,1024]{1,0:T(4,128)(2,1)S(1)} %copy-done.5, f32[512,256]{1,0:T(8,128)S(1)} %copy-done.8), custom_call_target="tpu_custom_call" | custom-call | flops 6442450944 | bytes 2097152 | tf_op jit(solution)/shard_map/table/pallas_call | solution.py:216
  55.6 1.3 %copy-done.2 = bf16[1024,1024]{1,0:T(8,128)(2,1)} copy-done((bf16[1024,1024]{1,0:T(8,128)(2,1)}, bf16[1024,1024]{1,0:T(8,128)(2,1)S(1)}, u32[]{:S(2)}) %copy-start.2) | copy-done | bytes 2097176
  56.9 6.8 %all-to-all-done.1.a = f32[16,8,128]{2,1,0:T(8,128)S(1)} async-done(((f32[16,8,128]{2,1,0:T(8,128)}), f32[16,8,128]{2,1,0:T(8,128)S(1)}, u32[]{:S(2)}, u32[]{:S(2)}) %all-to-all-start.1) | async-done | bytes 65568 | tf_op jit(solution)/shard_map/all_to_all | solution.py:458
  63.7 20.6 %all_to_all.20.a = bf16[16,8,128]{2,1,0:T(8,128)(2,1)S(1)} all-to-all(bf16[16,8,128]{2,1,0:T(8,128)(2,1)S(1)} %coefficients.1), channel_id=1, replica_groups=mesh['z_lo'=4,'y'=4,'x'=4,'z_hi'=4,'core'=2] {'z_lo','z_hi'}, dimensions={0} | all-to-all | bytes 65536 | tf_op jit(solution)/shard_map/all_to_all | solution.py:461
  84.2 0.9 copies.1
  85.1 3.6 %all-to-all-start.3 = ((bf16[16,16,8,128]{3,2,1,0:T(8,128)(2,1)}), bf16[16,16,8,128]{3,2,1,0:T(8,128)(2,1)S(1)}, u32[]{:S(2)}, u32[]{:S(2)}) async-start(bf16[16,16,8,128]{3,2,1,0:T(8,128)(2,1)} %copies.1), calls=%async_computation.3 | async-start | bytes 1048576 | tf_op jit(solution)/shard_map/all_to_all | solution.py:466
  88.7 0.0 collective-permute-done.2.far
  88.7 0.7 fusion
  89.4 0.5 slice.19
  89.9 7.8 %all-to-all-done.3 = bf16[16,16,8,128]{3,2,1,0:T(8,128)(2,1)S(1)} async-done(((bf16[16,16,8,128]{3,2,1,0:T(8,128)(2,1)}), bf16[16,16,8,128]{3,2,1,0:T(8,128)(2,1)S(1)}, u32[]{:S(2)}, u32[]{:S(2)}) %all-to-all-start.3) | async-done | bytes 524320 | tf_op jit(solution)/shard_map/all_to_all | solution.py:466
  97.7 7.1 %collective-permute-start.1 = (bf16[256,8,128]{2,1,0:T(8,128)(2,1)S(1)}, bf16[256,8,128]{2,1,0:T(8,128)(2,1)S(1)}, u32[]{:S(2)}, u32[]{:S(2)}) collective-permute-start(bf16[256,8,128]{2,1,0:T(8,128)(2,1)S(1)} %bitcast.6), channel_id=1, source_target_pairs={{0,1},{1,0},{2,3},{3,2},{4,5},{5,4},{6,7},{7,6},{8,9},{9,8},{10,11... | collective-permute-start | bytes 1572872 | tf_op jit(solution)/shard_map/ppermute | solution.py:467
  104.9 9.5 %near.1 = (f32[1024,256]{1,0:T(8,128)S(1)}, f32[1024,256]{1,0:T(8,128)S(1)}) custom-call(s32[1]{0:T(128)} %bitcast.seat, s32[2,24]{1,0:T(2,128)S(1)} %bitcast.9, s32[1]{0:T(128)S(6)} %copy.10.count, s32[2,24]{1,0:T(2,128)S(1)} %slice.18.pairs_below, s32[1]{0:T(128)} %bitcast.5.count_below, bf16[1024,256]{1,0:T(8,128)(2,1)S(1)} %copy-done, ...), custom_call_target="tpu_custom_call" | custom-call | flops 10737418240 | bytes 4194304 | tf_op jit(solution)/shard_map/near/pallas_call | solution.py:372
  114.4 1.0 copy-done.3
  115.4 1.0 copy-done.4
  116.4 5.0 %final.1 = (bf16[1024,256]{1,0:T(8,128)(2,1)}, bf16[1024,256]{1,0:T(8,128)(2,1)}) custom-call(s32[3]{0:T(128)S(1)} %pad_add_fusion.seat, bf16[256,8,128]{2,1,0:T(8,128)(2,1)S(1)} %bitcast.7, bf16[256,8,128]{2,1,0:T(8,128)(2,1)S(1)} %collective-permute-done.1.other, bf16[1024,1024]{1,0:T(8,128)(2,1)} %copy-done.2, f32[1024,256]{1,0:T(8,128)} %copy-done.3, ...), custom_call_target="tpu_custom_call" | custom-call | flops 1073741824 | bytes 4194304 | tf_op jit(solution)/shard_map/final/pallas_call | solution.py:416
  (17 shorter events, 0.1 us)
Async XLA Ops:
  3.8 11.9 %collective-permute-start = (f32[16,16,8,128]{3,2,1,0:T(8,128)S(1)}, f32[16,16,8,128]{3,2,1,0:T(8,128)S(1)}, u32[]{:S(2)}, u32[]{:S(2)}) collective-permute-start(f32[16,16,8,128]{3,2,1,0:T(8,128)S(1)} %sums.3), channel_id=1, source_target_pairs={{0,1},{1,0},{2,3},{3,2},{4,5},{5,4},{6,7},{7,6},{8,9},{9,8},{10,11... | collective-permute-start | bytes 3145736 | tf_op jit(solution)/shard_map/ppermute | solution.py:451
  15.7 5.6 %copy-start.7 = (s32[24,2]{0,1:T(2,128)S(1)}, s32[24,2]{0,1:T(2,128)}, u32[]{:S(2)}) copy-start(s32[24,2]{0,1:T(2,128)} %param.12) | copy-start | bytes 580
  16.9 35.0 %copy-start.5 = (bf16[3,1024]{1,0:T(4,128)(2,1)S(1)}, bf16[3,1024]{1,0:T(4,128)(2,1)}, u32[]{:S(2)}) copy-start(bf16[3,1024]{1,0:T(4,128)(2,1)} %places.3) | copy-start | bytes 18436
  16.9 35.0 %copy-start.6 = (s32[3,512]{1,0:T(4,128)S(1)}, s32[3,512]{1,0:T(4,128)}, u32[]{:S(2)}) copy-start(s32[3,512]{1,0:T(4,128)} %waves.1) | copy-start | bytes 18436
  16.9 35.0 %copy-start.8 = (f32[512,256]{1,0:T(8,128)S(1)}, f32[512,256]{1,0:T(8,128)}, u32[]{:S(2)}) copy-start(f32[512,256]{1,0:T(8,128)} %wave_filter.1) | copy-start | bytes 1572868
  16.9 26.8 %all-to-all-start = ((f32[16,16,8,128]{3,2,1,0:T(8,128)}), f32[16,16,8,128]{3,2,1,0:T(8,128)S(1)}, u32[]{:S(2)}, u32[]{:S(2)}) async-start(f32[16,16,8,128]{3,2,1,0:T(8,128)} %add.17), calls=%async_computation | async-start | bytes 2097152 | tf_op jit(solution)/shard_map/all_to_all | solution.py:454
  22.6 66.1 %collective-permute-start.2 = (bf16[1056,256]{1,0:T(8,128)(2,1)S(1)}, bf16[1056,256]{1,0:T(8,128)(2,1)}, u32[]{:S(2)}, u32[]{:S(2)}) collective-permute-start(bf16[1056,256]{1,0:T(8,128)(2,1)S(1)} %get-tuple-element.10), channel_id=1, source_target_pairs={{0,511},{1,2},{2,1},{3,4},{4,3},{5,6},{6,5},{7,8},{8,7},{9,10},{10... | collective-permute-start | bytes 1622024 | tf_op jit(solution)/shard_map/ppermute | solution.py:449
  29.3 59.4 %collective-permute-start.3 = (bf16[1056,256]{1,0:T(8,128)(2,1)S(1)}, bf16[1056,256]{1,0:T(8,128)(2,1)}, u32[]{:S(2)}, u32[]{:S(2)}) collective-permute-start(bf16[1056,256]{1,0:T(8,128)(2,1)S(1)} %get-tuple-element.11), channel_id=1, source_target_pairs={{0,1},{1,0},{2,3},{3,2},{4,5},{5,4},{6,7},{7,6},{8,9},{9,8},{10,11... | collective-permute-start | bytes 1622024 | tf_op jit(solution)/shard_map/ppermute | solution.py:455
  44.6 19.0 %all-to-all-start.1 = ((f32[16,8,128]{2,1,0:T(8,128)}), f32[16,8,128]{2,1,0:T(8,128)S(1)}, u32[]{:S(2)}, u32[]{:S(2)}) async-start(f32[16,8,128]{2,1,0:T(8,128)} %plane_sum.1), calls=%async_computation.1 | async-start | bytes 131072 | tf_op jit(solution)/shard_map/all_to_all | solution.py:458
  51.9 53.0 %copy-start = (bf16[1024,256]{1,0:T(8,128)(2,1)S(1)}, bf16[1024,256]{1,0:T(8,128)(2,1)}, u32[]{:S(2)}) copy-start(bf16[1024,256]{1,0:T(8,128)(2,1)} %embedding.3) | copy-start | bytes 1572868
  51.9 53.0 %copy-start.1 = (bf16[1024,256]{1,0:T(8,128)(2,1)S(1)}, bf16[1024,256]{1,0:T(8,128)(2,1)}, u32[]{:S(2)}) copy-start(bf16[1024,256]{1,0:T(8,128)(2,1)} %cotangent.3) | copy-start | bytes 1572868
  51.9 53.0 %copy-start.9 = (bf16[256,256]{1,0:T(8,128)(2,1)S(1)}, bf16[256,256]{1,0:T(8,128)(2,1)}, u32[]{:S(2)}) copy-start(bf16[256,256]{1,0:T(8,128)(2,1)} %weight.1) | copy-start | bytes 393220
  55.5 1.3 %copy-start.2 = (bf16[1024,1024]{1,0:T(8,128)(2,1)}, bf16[1024,1024]{1,0:T(8,128)(2,1)S(1)}, u32[]{:S(2)}) copy-start(bf16[1024,1024]{1,0:T(8,128)(2,1)S(1)} %get-tuple-element.9.table) | copy-start | bytes 6291460
  85.1 12.6 %all-to-all-start.3 = ((bf16[16,16,8,128]{3,2,1,0:T(8,128)(2,1)}), bf16[16,16,8,128]{3,2,1,0:T(8,128)(2,1)S(1)}, u32[]{:S(2)}, u32[]{:S(2)}) async-start(bf16[16,16,8,128]{3,2,1,0:T(8,128)(2,1)} %copies.1), calls=%async_computation.3 | async-start | bytes 1048576 | tf_op jit(solution)/shard_map/all_to_all | solution.py:466
  97.7 18.6 %collective-permute-start.1 = (bf16[256,8,128]{2,1,0:T(8,128)(2,1)S(1)}, bf16[256,8,128]{2,1,0:T(8,128)(2,1)S(1)}, u32[]{:S(2)}, u32[]{:S(2)}) collective-permute-start(bf16[256,8,128]{2,1,0:T(8,128)(2,1)S(1)} %bitcast.6), channel_id=1, source_target_pairs={{0,1},{1,0},{2,3},{3,2},{4,5},{5,4},{6,7},{7,6},{8,9},{9,8},{10,11... | collective-permute-start | bytes 1572872 | tf_op jit(solution)/shard_map/ppermute | solution.py:467
  114.4 1.0 copy-start.3
  115.4 1.0 copy-start.4

commit v4 on v3

--- a/solution.py
+++ b/solution.py
@@ -92,12 +92,12 @@
                     out[i, k * 4 + side * 2 + q] = part[8 * r : 8 * r + 8, 128 * q : 128 * q + 128]
 
 
-def partial_sums(seat, waves, places, left, right):
+def partial_sums(seat, waves, places, left, right, first):
     half, atoms = waves.shape[1] // 2, places.shape[1]
     return pl.pallas_call(
         sums_kernel,
         out_shape=jax.ShapeDtypeStruct((16, 16, 8, 128), F32),
-        in_specs=[SMEM] + [pl.BlockSpec(memory_space=pltpu.HBM)] * 4,
+        in_specs=[SMEM] + [pl.BlockSpec(memory_space=pl.ANY)] * 4,
         out_specs=VMEM,
         scratch_shapes=[
             pltpu.VMEM((3, half), waves.dtype),
@@ -113,19 +113,19 @@
             flops=4 * half * atoms * 512, bytes_accessed=2 << 20, transcendentals=0
         ),
         name="sums",
-    )(seat, *map(in_hbm, (waves, places, left, right)))
+    )(seat, *(map(in_hbm, (waves, places)) if first else (waves, places)), in_hbm(left), in_hbm(right))
 
 
 def add_kernel(a, b, out):
     @pl.loop(0, a.shape[0])
     def _(i):
-        out[i] = a[i] + b[i]
+        out[i] = (a[i] + b[i]).astype(BF16)
 
 
 def add(a, b):
     return pl.pallas_call(
         add_kernel,
-        out_shape=jax.ShapeDtypeStruct(a.shape, F32),
+        out_shape=jax.ShapeDtypeStruct(a.shape, BF16),
         in_specs=[VMEM] * 2,
         out_specs=VMEM,
         compiler_params=pltpu.CompilerParams(vmem_limit_bytes=4 << 20),
@@ -136,9 +136,9 @@
 def gather_sum_kernel(a, out):
     @pl.loop(0, out.shape[0])
     def _(i):
-        total = a[0, i]
+        total = a[0, i].astype(F32)
         for k in range(1, a.shape[0]):
-            total = total + a[k, i]
+            total = total + a[k, i].astype(F32)
         out[i] = total
 
 
@@ -246,10 +246,14 @@
 PLACES, PAIRS, LIVE, ROWS = 1024, 1040, 1048, 1056
 
 
-def pack_kernel(seat, embedding, cotangent, places_far, pairs, count, far, close, places, sems):
+def pack_kernel(seat, embedding, cotangent, places_far, pairs_far, count, far, close, places, pairs, sems):
     atoms = embedding.shape[0]
-    positions = pltpu.make_async_copy(places_far, places, sems.at[2])
-    positions.start()
+    small = [
+        pltpu.make_async_copy(places_far, places, sems.at[2]),
+        pltpu.make_async_copy(pairs_far, pairs, sems.at[3]),
+    ]
+    for load in small:
+        load.start()
 
     def both(forward, backward):
         a = pltpu.make_async_copy(embedding, backward.at[pl.ds(0, atoms)], sems.at[0])
@@ -267,7 +271,8 @@
         both(far, close)
 
     width = far.shape[1]
-    positions.wait()
+    for load in small:
+        load.wait()
     coords = places[...].astype(F32)
     rows = [coords[d : d + 1, k * width : k * width + width] for d in range(3) for k in range(4)]
     rows = jnp.concatenate([*rows, jnp.zeros((4, width), F32)], axis=0).astype(BF16)
@@ -286,12 +291,16 @@
     return pl.pallas_call(
         pack_kernel,
         out_shape=(jax.ShapeDtypeStruct((ROWS, embedding.shape[1]), BF16),) * 2,
-        in_specs=[SMEM, hbm, hbm, hbm, VMEM, SMEM],
+        in_specs=[SMEM, hbm, hbm, hbm, hbm, SMEM],
         out_specs=(VMEM, VMEM),
-        scratch_shapes=[pltpu.VMEM(places.shape, BF16), pltpu.SemaphoreType.DMA((3,))],
+        scratch_shapes=[
+            pltpu.VMEM(places.shape, BF16),
+            pltpu.VMEM(pairs.shape, pairs.dtype),
+            pltpu.SemaphoreType.DMA((4,)),
+        ],
         compiler_params=pltpu.CompilerParams(vmem_limit_bytes=4 << 20),
         name="pack",
-    )(seat, *map(in_hbm, (embedding, cotangent, places)), pairs, count)
+    )(seat, *map(in_hbm, (embedding, cotangent, places, pairs)), count)
 
 
 def in_hbm(value):
@@ -299,97 +308,155 @@
 
 
 GROUP = 4
-
-
-def near_kernel(
-    seat, pairs, count, pairs_below, count_below, embedding, cotangent, far, close, places, weight,
-    ahead, mixed,
-    around, projected, back, lefts, lefts_below, rights, far_places, sems,
+SHIFT = -3.0 - 0.5 * math.log(TILE)
+
+
+def rows_of(t):
+    return pl.ds(pl.multiple_of(t * TILE, TILE), TILE)
+
+
+def unpack_places(packed, places):
+    width = packed.shape[1]
+    rows = packed[PLACES:PAIRS, :].astype(F32)
+    for d in range(3):
+        for k in range(4):
+            places[d : d + 1, k * width : k * width + width] = rows[4 * d + k : 4 * d + k + 1]
+
+
+def store_tiles(rights, first, right):
+    for t in range(right.shape[1] // TILE):
+        rights[first + t] = right[:, t * TILE : t * TILE + TILE].astype(BF16)
+
+
+def ahead_kernel(
+    seat, pairs, count, embedding, far, close, places, weight, ahead, above, projected, lefts, rights, far_places, sem
 ):
-    atoms, width = embedding.shape
-    tiles = atoms // TILE
-    loads = [
-        pltpu.make_async_copy(close, around.at[seat[0]], sems.at[0]),
-        pltpu.make_async_copy(far, around.at[1 - seat[0]], sems.at[1]),
-    ]
-    for load in loads:
-        load.start()
+    atoms = embedding.shape[0]
+
+    @pl.when(seat[0] == 0)
+    def _():
+        pltpu.make_async_copy(close, above, sem).start()
+
+    @pl.when(seat[0] != 0)
+    def _():
+        pltpu.make_async_copy(far, above, sem).start()
+
     projected[pl.ds(0, atoms), :] = dot(embedding[...], weight[...]).astype(BF16)
-    for load in loads:
-        load.wait()
-    above, below = around.at[0], around.at[1]
+    left, right = features(places[...])
+    lefts[...] = left.T.astype(BF16)
+    store_tiles(rights, 0, right)
+    ahead[...] = jnp.zeros_like(ahead)
+    pltpu.make_async_copy(far, above, sem).wait()
     projected[pl.ds(atoms, atoms), :] = dot(above[pl.ds(0, atoms), :], weight[...]).astype(BF16)
-    for side, ref in enumerate((above, below)):
-        rows = ref[PLACES:PAIRS, :].astype(F32)
-        for d in range(3):
-            for k in range(4):
-                far_places[side, d : d + 1, k * width : k * width + width] = rows[4 * d + k : 4 * d + k + 1]
-    left, right = features(places[...])
-    _, right_above = features(far_places[0])
-    left_below, _ = features(far_places[1])
-    lefts[...] = left.T.astype(BF16)
-    lefts_below[...] = left_below.T.astype(BF16)
-    for t in range(tiles):
-        cut = slice(t * TILE, t * TILE + TILE)
-        rights[t] = right[:, cut].astype(BF16)
-        rights[tiles + t] = right_above[:, cut].astype(BF16)
-    ahead[...] = jnp.zeros_like(ahead)
-    back[...] = jnp.zeros_like(back)
-    shift = -3.0 - 0.5 * math.log(TILE)
-
-    def rows_of(t):
-        return pl.ds(pl.multiple_of(t * TILE, TILE), TILE)
+    unpack_places(above, far_places)
+    _, right = features(far_places[...])
+    store_tiles(rights, atoms // TILE, right)
 
     @pl.loop(0, pairs.shape[1] // GROUP)
     def _(g):
-        fore, rear = [], []
+        parts = []
         for j in range(GROUP):
             p = g * GROUP + j
             u, v = pairs[0, p], pairs[1, p]
-            k = jnp.exp(dot(lefts[rows_of(u), :], rights[v]) + shift)
-            k = jnp.where(p < count[0], k, 0.0)
-            fore.append((u, dot(k.astype(BF16), projected[rows_of(v), :])))
-            k = jnp.where(v < tiles, k, 0.0)
-            own = jnp.where(v < tiles, v, v - tiles)
-            rear.append((own, dot(k.T.astype(BF16), cotangent[rows_of(u), :])))
+            k = jnp.exp(dot(lefts[rows_of(u), :], rights[v]) + SHIFT)
+            k = jnp.where(p < count[0], k, 0.0).astype(BF16)
+            parts.append((u, dot(k, projected[rows_of(v), :])))
+        for t, part in parts:
+            ahead[rows_of(t), :] += part
+
+
+def behind_kernel(
+    seat, pairs, count, pairs_below, count_below, cotangent, far, close, places, weight,
+    mixed,
+    below, back, lefts, lefts_below, rights, far_places, sem,
+):
+    atoms = cotangent.shape[0]
+    tiles = atoms // TILE
+
+    @pl.when(seat[0] == 0)
+    def _():
+        pltpu.make_async_copy(far, below, sem).start()
+
+    @pl.when(seat[0] != 0)
+    def _():
+        pltpu.make_async_copy(close, below, sem).start()
+
+    left, right = features(places[...])
+    lefts[...] = left.T.astype(BF16)
+    store_tiles(rights, 0, right)
+    back[...] = jnp.zeros_like(back)
+    pltpu.make_async_copy(far, below, sem).wait()
+    unpack_places(below, far_places)
+    left, _ = features(far_places[...])
+    lefts_below[...] = left.T.astype(BF16)
+
+    def own_of(v):
+        return jnp.where(v < tiles, v, v - tiles)
+
+    @pl.loop(0, pairs.shape[1] // GROUP)
+    def _(g):
+        parts = []
+        for j in range(GROUP):
+            p = g * GROUP + j
+            u, v = pairs[0, p], pairs[1, p]
+            k = jnp.exp(dot(lefts[rows_of(u), :], rights[own_of(v)]) + SHIFT)
+            k = jnp.where((p < count[0]) & (v < tiles), k, 0.0)
+            parts.append((own_of(v), dot(k.T.astype(BF16), cotangent[rows_of(u), :])))
             u, v = pairs_below[0, p], pairs_below[1, p]
-            own = jnp.where(v < tiles, v, v - tiles)
-            k = jnp.exp(dot(lefts_below[rows_of(u), :], rights[own]) + shift)
+            k = jnp.exp(dot(lefts_below[rows_of(u), :], rights[own_of(v)]) + SHIFT)
             k = jnp.where((p < count_below[0]) & (v >= tiles), k, 0.0)
-            rear.append((own, dot(k.T.astype(BF16), below[rows_of(u), :])))
-        for t, part in fore:
-            ahead[rows_of(t), :] += part
-        for t, part in rear:
+            parts.append((own_of(v), dot(k.T.astype(BF16), below[rows_of(u), :])))
+        for t, part in parts:
             back[rows_of(t), :] += part
 
     mixed[...] = dot(back[...].astype(BF16), weight[...], ((1,), (1,)))
 
 
-def near(seat, pairs, count, pairs_below, count_below, embedding, cotangent, far, close, places, weight):
+def near_ahead(seat, pairs, count, embedding, far, close, places, weight):
     atoms, channels = embedding.shape
     tiles = atoms // TILE
     hbm = pl.BlockSpec(memory_space=pltpu.HBM)
     return pl.pallas_call(
-        near_kernel,
-        out_shape=(jax.ShapeDtypeStruct((atoms, channels), F32),) * 2,
-        in_specs=[SMEM] * 5 + [VMEM] * 2 + [hbm] * 2 + [VMEM] * 2,
-        out_specs=(VMEM, VMEM),
+        ahead_kernel,
+        out_shape=jax.ShapeDtypeStruct((atoms, channels), F32),
+        in_specs=[SMEM] * 3 + [VMEM, hbm, hbm, VMEM, VMEM],
+        out_specs=VMEM,
         scratch_shapes=[
-            pltpu.VMEM((2, ROWS, channels), BF16),
+            pltpu.VMEM((ROWS, channels), BF16),
             pltpu.VMEM((2 * atoms, channels), BF16),
+            pltpu.VMEM((atoms, 96), BF16),
+            pltpu.VMEM((2 * tiles, 96, TILE), BF16),
+            pltpu.VMEM((3, atoms), F32),
+            pltpu.SemaphoreType.DMA(()),
+        ],
+        compiler_params=pltpu.CompilerParams(vmem_limit_bytes=12 << 20),
+        cost_estimate=pl.CostEstimate(flops=5 << 30, bytes_accessed=2 << 20, transcendentals=0),
+        name="near_ahead",
+    )(seat, pairs, count, embedding, in_hbm(far), in_hbm(close), places, weight)
+
+
+def near_behind(seat, pairs, count, pairs_below, count_below, cotangent, far, close, places, weight):
+    atoms, channels = cotangent.shape
+    tiles = atoms // TILE
+    hbm = pl.BlockSpec(memory_space=pltpu.HBM)
+    return pl.pallas_call(
+        behind_kernel,
+        out_shape=jax.ShapeDtypeStruct((atoms, channels), F32),
+        in_specs=[SMEM] * 5 + [VMEM, hbm, hbm, VMEM, VMEM],
+        out_specs=VMEM,
+        scratch_shapes=[
+            pltpu.VMEM((ROWS, channels), BF16),
             pltpu.VMEM((atoms, channels), F32),
             pltpu.VMEM((atoms, 96), BF16),
             pltpu.VMEM((atoms, 96), BF16),
-            pltpu.VMEM((2 * tiles, 96, TILE), BF16),
-            pltpu.VMEM((2, 3, atoms), F32),
-            pltpu.SemaphoreType.DMA((2,)),
+            pltpu.VMEM((tiles, 96, TILE), BF16),
+            pltpu.VMEM((3, atoms), F32),
+            pltpu.SemaphoreType.DMA(()),
         ],
-        compiler_params=pltpu.CompilerParams(vmem_limit_bytes=16 << 20),
-        cost_estimate=pl.CostEstimate(flops=10 << 30, bytes_accessed=4 << 20, transcendentals=0),
-        name="near",
-    )(
-        seat, pairs, count, pairs_below, count_below, embedding, cotangent, in_hbm(far), in_hbm(close), places, weight
-    )
+        compiler_params=pltpu.CompilerParams(vmem_limit_bytes=12 << 20),
+        cost_estimate=pl.CostEstimate(flops=5 << 30, bytes_accessed=2 << 20, transcendentals=0),
+        name="near_behind",
+    )(seat, pairs, count, pairs_below, count_below, cotangent, in_hbm(far), in_hbm(close), places, weight)
 
 
 def final_kernel(seat, own, other, table, ahead, mixed, message, grad, matrix):
@@ -408,7 +475,7 @@
     grad[...] = (dot(table[...], matrix[:, channels:]) + mixed[...]).astype(BF16)
 
 
-def final(seat, own, other, table, ahead, mixed, steps=4):
+def final(seat, own, other, table, ahead, mixed, steps=2):
     atoms, channels = ahead.shape
     rows = atoms // steps
     block = pl.BlockSpec((rows, channels), lambda i: (i, 0))
@@ -447,9 +514,9 @@
     to_far, to_close = pack(seat[:1], embedding, cotangent, fractional, listed, counts)
     size = math.prod(lax.axis_size(name) for name in FINE)
     far = lax.ppermute(to_far, FINE, [(i, (i + (1 if i % 2 else -1)) % size) for i in range(size)])
-    given = partial_sums(1 - seat[:1], wave_index, fractional, embedding, cotangent)
+    given = partial_sums(1 - seat[:1], wave_index, fractional, embedding, cotangent, True)
     given = lax.ppermute(given, "core", swap)
-    kept = partial_sums(seat[:1], wave_index, fractional, embedding, cotangent)
+    kept = partial_sums(seat[:1], wave_index, fractional, embedding, cotangent, False)
     total = add(kept, given)
     chip = lax.all_to_all(total, ("y", "x"), 0, 0, tiled=True)
     close = lax.ppermute(to_close, "core", swap)
@@ -459,9 +526,9 @@
     tail = jnp.where(seat[0] == 0, far[PAIRS:ROWS, :TILE], close[PAIRS:ROWS, :TILE]).astype(jnp.int32)
     pairs_below, count_below = tail[0:2, : listed.shape[1]], tail[LIVE - PAIRS, 0:1]
     mine = lax.all_to_all(coefficients(parts, scale), ALONG_Z, 0, 0, tiled=True)
-    ahead, mixed = near(
-        seat[:1], listed, counts, pairs_below, count_below, embedding, cotangent, far, close, fractional,
-        short_weight,
+    ahead = near_ahead(seat[:1], listed, counts, embedding, far, close, fractional, short_weight)
+    mixed = near_behind(
+        seat[:1], listed, counts, pairs_below, count_below, cotangent, far, close, fractional, short_weight
     )
     coeffs = lax.all_to_all(copies(mine), ("y", "x"), 0, 0, tiled=True).reshape(256, 8, 128)
     other = lax.ppermute(coeffs, "core", swap)

time: 122 us -> 121 us (level)
  blocking collectives: 20.6 us -> 0 us
  starting transfers between devices: 46 us -> 54.2 us
  waiting for transfers between devices: 20 us -> 26.4 us
  Pallas kernels: 28.6 us -> 32.8 us
    all_to_all x1 -> x0, blocking collectives: 20.6 us -> none  [body(): mine = lax.all_to_all(coefficients(parts, scale), ALONG_Z, 0, 0, tiled=True)]
    all_to_all x0 -> x1, waiting for transfers between devices: none -> 11.3 us  [body(): mine = lax.all_to_all(coefficients(parts, scale), ALONG_Z, 0, 0, tiled=True)]
    all_to_all x0 -> x1, starting transfers between devices: none -> 6.64 us  [body(): mine = lax.all_to_all(coefficients(parts, scale), ALONG_Z, 0, 0, tiled=True)]
    all_to_all x1, waiting for transfers between devices: 6.76 us -> 12.9 us  [body(): parts = lax.all_to_all(summed, ALONG_Z, 0, 0, tiled=True)]
    all_to_all x1, waiting for transfers between devices: 7.82 us -> 2.17 us  [body(): lax.all_to_all(copies(mine), ('y', 'x'), 0, 0, tiled=True)]
    all_to_all x1, waiting for transfers between devices: 5.43 us -> 0.01 us  [body(): chip = lax.all_to_all(total, ('y', 'x'), 0, 0, tiled=True)]
    pallas_call x2 -> x3, Pallas kernels: 10.7 us -> 15.9 us  [the longest x1 9.64 us: near_behind(): pl.pallas_call(behind_kernel, out_shape=jax.ShapeDtypeStruct((atoms, chan...]
    all_to_all x1, starting transfers between devices: 3.57 us -> 6.8 us  [body(): lax.all_to_all(copies(mine), ('y', 'x'), 0, 0, tiled=True)]
  transfers between devices with their start and end apart: 7 -> 8, of which waited for: 3 -> 3; matrix products, arithmetic and copies ran while one was open for 1% -> 1% of each run, Pallas kernels for 16% -> 21%
where the time goes in v4:
time: 121 us; the launch traced here: 120 us
  starting transfers between devices  54.2 us (45%)
  Pallas kernels  32.8 us (27%)
  waiting for transfers between devices  26.4 us (22%)
  local copies, waits for them, and re-layouts  4.6 us (4%)
  between operations  1.57 us (1%)
    all_to_all x1, waiting for transfers between devices, body(): parts = lax.all_to_all(summed, ALONG_Z, 0, 0, tiled=True)  12.9 us
    all_to_all x1, waiting for transfers between devices, body(): mine = lax.all_to_all(coefficients(parts, scale), ALONG_Z, 0, 0, tiled=True)  11.3 us
    pallas_call x1, Pallas kernels, near_behind(): pl.pallas_call(behind_kernel, out_shape=jax.ShapeDtypeStruct((atoms, chan...  9.64 us
    ppermute x1, starting transfers between devices, body(): given = lax.ppermute(given, 'core', swap)  8.75 us
    ppermute x1, starting transfers between devices, body(): close = lax.ppermute(to_close, 'core', swap)  8.74 us
    ppermute x1, starting transfers between devices, body(): lax.ppermute(to_far, FINE, [(i, (i + (1 if i % 2 else -1)) % size) for i...  6.94 us
    all_to_all x1, starting transfers between devices, body(): lax.all_to_all(copies(mine), ('y', 'x'), 0, 0, tiled=True)  6.8 us
    ppermute x1, starting transfers between devices, body(): other = lax.ppermute(coeffs, 'core', swap)  6.66 us
  transfers between devices with their start and end apart: 8, of which 3 were waited for; matrix products, arithmetic and copies ran while one was open for 1% of the time, Pallas kernels for 21%

profile of v4, /device:TPU:1, one launch (start us, length us, event | category | flops | bytes accessed | tf_op | source)
XLA Modules:
  0.0 120.4 jit_solution(16797613130580740641)
XLA Ops:
  0.6 0.0 copy-start.5
  0.7 3.2 %sums.3 = f32[16,16,8,128]{3,2,1,0:T(8,128)S(1)} custom-call(s32[1]{0:T(128)S(6)} %sub.3.seat, s32[3,512]{1,0:T(4,128)} %waves.1, bf16[3,1024]{1,0:T(4,128)(2,1)} %places.5, bf16[1024,256]{1,0:T(8,128)(2,1)} %embedding.3, bf16[1024,256]{1,0:T(8,128)(2,1)} %cotangent.3), custom_call_target="tpu_custom_call" | custom-call | flops 536870912 | bytes 2097152 | tf_op jit(solution)/shard_map/sums/pallas_call | solution.py:97
  3.8 8.7 %collective-permute-start = (f32[16,16,8,128]{3,2,1,0:T(8,128)S(1)}, f32[16,16,8,128]{3,2,1,0:T(8,128)S(1)}, u32[]{:S(2)}, u32[]{:S(2)}) collective-permute-start(f32[16,16,8,128]{3,2,1,0:T(8,128)S(1)} %sums.3), channel_id=1, source_target_pairs={{0,1},{1,0},{2,3},{3,2},{4,5},{5,4},{6,7},{7,6},{8,9},{9,8},{10,11... | collective-permute-start | bytes 3145736 | tf_op jit(solution)/shard_map/ppermute | solution.py:518
  12.6 2.5 %sums.2.a = f32[16,16,8,128]{3,2,1,0:T(8,128)S(1)} custom-call(s32[1]{0:T(128)} %bitcast.seat, s32[3,512]{1,0:T(4,128)S(1)} %copy-done.7, bf16[3,1024]{1,0:T(4,128)(2,1)S(1)} %copy-done.5, bf16[1024,256]{1,0:T(8,128)(2,1)} %embedding.3, bf16[1024,256]{1,0:T(8,128)(2,1)} %cotangent.3), custom_call_target="tpu_custom_call" | custom-call | flops 536870912 | bytes 2097152 | tf_op jit(solution)/shard_map/sums/pallas_call | solution.py:97
  15.1 0.0 copy-start.9
  15.1 1.0 add.17
  16.1 3.6 %all-to-all-start = ((bf16[16,16,8,128]{3,2,1,0:T(8,128)(2,1)}), bf16[16,16,8,128]{3,2,1,0:T(8,128)(2,1)S(1)}, u32[]{:S(2)}, u32[]{:S(2)}) async-start(bf16[16,16,8,128]{3,2,1,0:T(8,128)(2,1)} %add.17), calls=%async_computation | async-start | bytes 1048576 | tf_op jit(solution)/shard_map/all_to_all | solution.py:521
  20.3 1.3 %pack.1 = (bf16[1056,256]{1,0:T(8,128)(2,1)S(1)}, bf16[1056,256]{1,0:T(8,128)(2,1)S(1)}) custom-call(s32[1]{0:T(128)} %bitcast.seat, bf16[1024,256]{1,0:T(8,128)(2,1)} %embedding.3, bf16[1024,256]{1,0:T(8,128)(2,1)} %cotangent.3, bf16[3,1024]{1,0:T(4,128)(2,1)} %places.5, s32[2,24]{1,0:T(2,128)} %bitcast.8, s32[1]{0:T(128)S(6)} %copy.10.count), custom_call_target="tpu_custom_call" | custom-call | tf_op jit(solution)/shard_map/pack/pallas_call | solution.py:291
  21.6 6.9 %collective-permute-start.2 = (bf16[1056,256]{1,0:T(8,128)(2,1)S(1)}, bf16[1056,256]{1,0:T(8,128)(2,1)S(1)}, u32[]{:S(2)}, u32[]{:S(2)}) collective-permute-start(bf16[1056,256]{1,0:T(8,128)(2,1)S(1)} %get-tuple-element.8), channel_id=1, source_target_pairs={{0,511},{1,2},{2,1},{3,4},{4,3},{5,6},{6,5},{7,8},{8,7},{9,10},{10... | collective-permute-start | bytes 1622024 | tf_op jit(solution)/shard_map/ppermute | solution.py:516
  28.5 8.7 %collective-permute-start.3 = (bf16[1056,256]{1,0:T(8,128)(2,1)S(1)}, bf16[1056,256]{1,0:T(8,128)(2,1)}, u32[]{:S(2)}, u32[]{:S(2)}) collective-permute-start(bf16[1056,256]{1,0:T(8,128)(2,1)S(1)} %get-tuple-element.9), channel_id=1, source_target_pairs={{0,1},{1,0},{2,3},{3,2},{4,5},{5,4},{6,7},{7,6},{8,9},{9,8},{10,11... | collective-permute-start | bytes 1622024 | tf_op jit(solution)/shard_map/ppermute | solution.py:522
  37.3 0.1 pad_add_fusion.seat
  37.4 0.9 plane_sum.1
  38.3 6.1 %all-to-all-start.1 = ((f32[16,8,128]{2,1,0:T(8,128)}), f32[16,8,128]{2,1,0:T(8,128)S(1)}, u32[]{:S(2)}, u32[]{:S(2)}) async-start(f32[16,8,128]{2,1,0:T(8,128)} %plane_sum.1), calls=%async_computation.1 | async-start | bytes 131072 | tf_op jit(solution)/shard_map/all_to_all | solution.py:525
  44.4 0.0 copy-start.8
  44.5 3.6 %table.1 = (bf16[1024,1024]{1,0:T(8,128)(2,1)S(1)}, f32[8,128]{1,0:T(8,128)S(1)}) custom-call(s32[3]{0:T(128)S(1)} %pad_add_fusion.seat, s32[3,512]{1,0:T(4,128)S(1)} %copy-done.7, bf16[3,1024]{1,0:T(4,128)(2,1)S(1)} %copy-done.6, f32[512,256]{1,0:T(8,128)S(1)} %copy-done.9), custom_call_target="tpu_custom_call" | custom-call | flops 6442450944 | bytes 2097152 | tf_op jit(solution)/shard_map/table/pallas_call | solution.py:216
  48.1 1.3 %copy-done.2 = bf16[1024,1024]{1,0:T(8,128)(2,1)} copy-done((bf16[1024,1024]{1,0:T(8,128)(2,1)}, bf16[1024,1024]{1,0:T(8,128)(2,1)S(1)}, u32[]{:S(2)}) %copy-start.2) | copy-done | bytes 2097176
  49.4 12.9 %all-to-all-done.1.a = f32[16,8,128]{2,1,0:T(8,128)S(1)} async-done(((f32[16,8,128]{2,1,0:T(8,128)}), f32[16,8,128]{2,1,0:T(8,128)S(1)}, u32[]{:S(2)}, u32[]{:S(2)}) %all-to-all-start.1) | async-done | bytes 65568 | tf_op jit(solution)/shard_map/all_to_all | solution.py:525
  62.3 0.6 coefficients.1
  62.9 6.6 %all-to-all-start.2 = ((bf16[16,8,128]{2,1,0:T(8,128)(2,1)}), bf16[16,8,128]{2,1,0:T(8,128)(2,1)S(1)}, u32[]{:S(2)}, u32[]{:S(2)}) async-start(bf16[16,8,128]{2,1,0:T(8,128)(2,1)} %coefficients.1), calls=%async_computation.2 | async-start | bytes 65536 | tf_op jit(solution)/shard_map/all_to_all | solution.py:528
  69.6 11.3 %all-to-all-done.2.a = bf16[16,8,128]{2,1,0:T(8,128)(2,1)S(1)} async-done(((bf16[16,8,128]{2,1,0:T(8,128)(2,1)}), bf16[16,8,128]{2,1,0:T(8,128)(2,1)S(1)}, u32[]{:S(2)}, u32[]{:S(2)}) %all-to-all-start.2) | async-done | bytes 32800 | tf_op jit(solution)/shard_map/all_to_all | solution.py:528
  80.9 0.9 copies.1
  81.8 6.8 %all-to-all-start.3 = ((bf16[16,16,8,128]{3,2,1,0:T(8,128)(2,1)}), bf16[16,16,8,128]{3,2,1,0:T(8,128)(2,1)S(1)}, u32[]{:S(2)}, u32[]{:S(2)}) async-start(bf16[16,16,8,128]{3,2,1,0:T(8,128)(2,1)} %copies.1), calls=%async_computation.3 | async-start | bytes 1048576 | tf_op jit(solution)/shard_map/all_to_all | solution.py:533
  88.7 0.8 copy-done.11
  89.5 5.3 %near_ahead.1.ahead = f32[1024,256]{1,0:T(8,128)S(1)} custom-call(s32[1]{0:T(128)} %bitcast.seat, s32[2,24]{1,0:T(2,128)S(1)} %bitcast.9, s32[1]{0:T(128)S(6)} %copy.10.count, bf16[1024,256]{1,0:T(8,128)(2,1)S(1)} %copy-done, bf16[1056,256]{1,0:T(8,128)(2,1)} %copy-done.11, bf16[1056,256]{1,0:T(8,128)(2,1)} %collective-permute-done.3.close, ...), custom_call_target="tpu_custom_call" | custom-call | flops 5368709120 | bytes 2097152 | tf_op jit(solution)/shard_map/near_ahead/pallas_call | solution.py:419
  94.7 1.0 copy-done.3
  95.7 2.2 %all-to-all-done.3 = bf16[16,16,8,128]{3,2,1,0:T(8,128)(2,1)S(1)} async-done(((bf16[16,16,8,128]{3,2,1,0:T(8,128)(2,1)}), bf16[16,16,8,128]{3,2,1,0:T(8,128)(2,1)S(1)}, u32[]{:S(2)}, u32[]{:S(2)}) %all-to-all-start.3) | async-done | bytes 524320 | tf_op jit(solution)/shard_map/all_to_all | solution.py:533
  97.9 6.7 %collective-permute-start.1 = (bf16[256,8,128]{2,1,0:T(8,128)(2,1)S(1)}, bf16[256,8,128]{2,1,0:T(8,128)(2,1)S(1)}, u32[]{:S(2)}, u32[]{:S(2)}) collective-permute-start(bf16[256,8,128]{2,1,0:T(8,128)(2,1)S(1)} %bitcast.6), channel_id=1, source_target_pairs={{0,1},{1,0},{2,3},{3,2},{4,5},{5,4},{6,7},{7,6},{8,9},{9,8},{10,11... | collective-permute-start | bytes 1572872 | tf_op jit(solution)/shard_map/ppermute | solution.py:534
  104.6 0.7 fusion
  105.3 0.5 slice.19
  105.8 9.6 %near_behind.1.mixed = f32[1024,256]{1,0:T(8,128)S(1)} custom-call(s32[1]{0:T(128)} %bitcast.seat, s32[2,24]{1,0:T(2,128)S(1)} %bitcast.10, s32[1]{0:T(128)S(6)} %copy.10.count, s32[2,24]{1,0:T(2,128)S(1)} %slice.18.pairs_below, s32[1]{0:T(128)} %bitcast.5.count_below, bf16[1024,256]{1,0:T(8,128)(2,1)S(1)} %copy-done.1, bf16[1056,256]{1,0:T(8,128)(2,1)} %copy-done.11, ...), custom_call_target="tpu_custom_call" | custom-call | flops 5368709120 | bytes 2097152 | tf_op jit(solution)/shard_map/near_behind/pallas_call | solution.py:442
  115.4 1.0 copy-done.4
  116.4 4.0 %final.1 = (bf16[1024,256]{1,0:T(8,128)(2,1)}, bf16[1024,256]{1,0:T(8,128)(2,1)}) custom-call(s32[3]{0:T(128)S(1)} %pad_add_fusion.seat, bf16[256,8,128]{2,1,0:T(8,128)(2,1)S(1)} %bitcast.7, bf16[256,8,128]{2,1,0:T(8,128)(2,1)S(1)} %collective-permute-done.1.other, bf16[1024,1024]{1,0:T(8,128)(2,1)} %copy-done.2, f32[1024,256]{1,0:T(8,128)} %copy-done.3, ...), custom_call_target="tpu_custom_call" | custom-call | flops 1073741824 | bytes 4194304 | tf_op jit(solution)/shard_map/final/pallas_call | solution.py:483
  (23 shorter events, 0.1 us)
Async XLA Ops:
  0.6 12.0 %copy-start.5 = (bf16[3,1024]{1,0:T(4,128)(2,1)S(1)}, bf16[3,1024]{1,0:T(4,128)(2,1)}, u32[]{:S(2)}) copy-start(bf16[3,1024]{1,0:T(4,128)(2,1)} %places.5) | copy-start | bytes 18436
  0.6 12.0 %copy-start.7 = (s32[3,512]{1,0:T(4,128)S(1)}, s32[3,512]{1,0:T(4,128)}, u32[]{:S(2)}) copy-start(s32[3,512]{1,0:T(4,128)} %waves.1) | copy-start | bytes 18436
  3.8 11.3 %collective-permute-start = (f32[16,16,8,128]{3,2,1,0:T(8,128)S(1)}, f32[16,16,8,128]{3,2,1,0:T(8,128)S(1)}, u32[]{:S(2)}, u32[]{:S(2)}) collective-permute-start(f32[16,16,8,128]{3,2,1,0:T(8,128)S(1)} %sums.3), channel_id=1, source_target_pairs={{0,1},{1,0},{2,3},{3,2},{4,5},{5,4},{6,7},{7,6},{8,9},{9,8},{10,11... | collective-permute-start | bytes 3145736 | tf_op jit(solution)/shard_map/ppermute | solution.py:518
  15.1 29.3 %copy-start.6 = (bf16[3,1024]{1,0:T(4,128)(2,1)S(1)}, bf16[3,1024]{1,0:T(4,128)(2,1)}, u32[]{:S(2)}) copy-start(bf16[3,1024]{1,0:T(4,128)(2,1)} %places.5) | copy-start | bytes 18436
  15.1 29.3 %copy-start.9 = (f32[512,256]{1,0:T(8,128)S(1)}, f32[512,256]{1,0:T(8,128)}, u32[]{:S(2)}) copy-start(f32[512,256]{1,0:T(8,128)} %wave_filter.1) | copy-start | bytes 1572868
  16.1 21.3 %all-to-all-start = ((bf16[16,16,8,128]{3,2,1,0:T(8,128)(2,1)}), bf16[16,16,8,128]{3,2,1,0:T(8,128)(2,1)S(1)}, u32[]{:S(2)}, u32[]{:S(2)}) async-start(bf16[16,16,8,128]{3,2,1,0:T(8,128)(2,1)} %add.17), calls=%async_computation | async-start | bytes 1048576 | tf_op jit(solution)/shard_map/all_to_all | solution.py:521
  21.6 67.1 %collective-permute-start.2 = (bf16[1056,256]{1,0:T(8,128)(2,1)S(1)}, bf16[1056,256]{1,0:T(8,128)(2,1)S(1)}, u32[]{:S(2)}, u32[]{:S(2)}) collective-permute-start(bf16[1056,256]{1,0:T(8,128)(2,1)S(1)} %get-tuple-element.8), channel_id=1, source_target_pairs={{0,511},{1,2},{2,1},{3,4},{4,3},{5,6},{6,5},{7,8},{8,7},{9,10},{10... | collective-permute-start | bytes 1622024 | tf_op jit(solution)/shard_map/ppermute | solution.py:516
  28.5 60.2 %collective-permute-start.3 = (bf16[1056,256]{1,0:T(8,128)(2,1)S(1)}, bf16[1056,256]{1,0:T(8,128)(2,1)}, u32[]{:S(2)}, u32[]{:S(2)}) collective-permute-start(bf16[1056,256]{1,0:T(8,128)(2,1)S(1)} %get-tuple-element.9), channel_id=1, source_target_pairs={{0,1},{1,0},{2,3},{3,2},{4,5},{5,4},{6,7},{7,6},{8,9},{9,8},{10,11... | collective-permute-start | bytes 1622024 | tf_op jit(solution)/shard_map/ppermute | solution.py:522
  38.3 24.0 %all-to-all-start.1 = ((f32[16,8,128]{2,1,0:T(8,128)}), f32[16,8,128]{2,1,0:T(8,128)S(1)}, u32[]{:S(2)}, u32[]{:S(2)}) async-start(f32[16,8,128]{2,1,0:T(8,128)} %plane_sum.1), calls=%async_computation.1 | async-start | bytes 131072 | tf_op jit(solution)/shard_map/all_to_all | solution.py:525
  44.4 45.0 %copy-start = (bf16[1024,256]{1,0:T(8,128)(2,1)S(1)}, bf16[1024,256]{1,0:T(8,128)(2,1)}, u32[]{:S(2)}) copy-start(bf16[1024,256]{1,0:T(8,128)(2,1)} %embedding.3) | copy-start | bytes 1572868
  44.4 45.0 %copy-start.8 = (s32[24,2]{0,1:T(2,128)S(1)}, s32[24,2]{0,1:T(2,128)}, u32[]{:S(2)}) copy-start(s32[24,2]{0,1:T(2,128)} %param.12) | copy-start | bytes 580
  44.4 45.0 %copy-start.10 = (bf16[256,256]{1,0:T(8,128)(2,1)S(1)}, bf16[256,256]{1,0:T(8,128)(2,1)}, u32[]{:S(2)}) copy-start(bf16[256,256]{1,0:T(8,128)(2,1)} %weight.3) | copy-start | bytes 393220
  48.1 1.3 %copy-start.2 = (bf16[1024,1024]{1,0:T(8,128)(2,1)}, bf16[1024,1024]{1,0:T(8,128)(2,1)S(1)}, u32[]{:S(2)}) copy-start(bf16[1024,1024]{1,0:T(8,128)(2,1)S(1)} %get-tuple-element.7.table) | copy-start | bytes 6291460
  62.9 18.0 %all-to-all-start.2 = ((bf16[16,8,128]{2,1,0:T(8,128)(2,1)}), bf16[16,8,128]{2,1,0:T(8,128)(2,1)S(1)}, u32[]{:S(2)}, u32[]{:S(2)}) async-start(bf16[16,8,128]{2,1,0:T(8,128)(2,1)} %coefficients.1), calls=%async_computation.2 | async-start | bytes 65536 | tf_op jit(solution)/shard_map/all_to_all | solution.py:528
  81.8 16.1 %all-to-all-start.3 = ((bf16[16,16,8,128]{3,2,1,0:T(8,128)(2,1)}), bf16[16,16,8,128]{3,2,1,0:T(8,128)(2,1)S(1)}, u32[]{:S(2)}, u32[]{:S(2)}) async-start(bf16[16,16,8,128]{3,2,1,0:T(8,128)(2,1)} %copies.1), calls=%async_computation.3 | async-start | bytes 1048576 | tf_op jit(solution)/shard_map/all_to_all | solution.py:533
  88.6 17.2 %copy-start.1 = (bf16[1024,256]{1,0:T(8,128)(2,1)S(1)}, bf16[1024,256]{1,0:T(8,128)(2,1)}, u32[]{:S(2)}) copy-start(bf16[1024,256]{1,0:T(8,128)(2,1)} %cotangent.3) | copy-start | bytes 1572868
  88.6 0.8 copy-start.11
  94.7 1.0 copy-start.3
  97.9 18.5 %collective-permute-start.1 = (bf16[256,8,128]{2,1,0:T(8,128)(2,1)S(1)}, bf16[256,8,128]{2,1,0:T(8,128)(2,1)S(1)}, u32[]{:S(2)}, u32[]{:S(2)}) collective-permute-start(bf16[256,8,128]{2,1,0:T(8,128)(2,1)S(1)} %bitcast.6), channel_id=1, source_target_pairs={{0,1},{1,0},{2,3},{3,2},{4,5},{5,4},{6,7},{7,6},{8,9},{9,8},{10,11... | collective-permute-start | bytes 1572872 | tf_op jit(solution)/shard_map/ppermute | solution.py:534
  115.4 1.0 copy-start.4

commit v5 on v4

--- a/solution.py
+++ b/solution.py
@@ -193,7 +193,7 @@
     )(a)
 
 
-def table_kernel(seat, waves, places, wave_filter, table, scale, turns, *, atoms_all):
+def table_kernel(waves, places, table, turns):
     atoms, count = turns.shape
     half = count // 2
     turns[...] = dot(padded(places[...]).astype(BF16), padded(waves[...]).astype(BF16), ((0,), (0,)))
@@ -206,26 +206,19 @@
             table[rows, 2 * j * half : (2 * j + 1) * half] = c.astype(BF16)
             table[rows, (2 * j + 1) * half : (2 * j + 2) * half] = s.astype(BF16)
 
-    row, col = seat[1], seat[2]
-    tile = wave_filter[pl.ds(pl.multiple_of(row * 8, 8), 8), pl.ds(pl.multiple_of(col * 128, 128), 128)]
-    scale[...] = tile * (1.0 / math.sqrt(atoms_all))
-
-
-def tables(seat, waves, places, wave_filter, atoms_all):
+
+def tables(waves, places):
     atoms, count = places.shape[1], waves.shape[1]
     return pl.pallas_call(
-        functools.partial(table_kernel, atoms_all=atoms_all),
-        out_shape=(
-            jax.ShapeDtypeStruct((atoms, 2 * count), BF16),
-            jax.ShapeDtypeStruct((8, 128), F32),
-        ),
-        in_specs=[SMEM] + [VMEM] * 3,
-        out_specs=(VMEM, VMEM),
+        table_kernel,
+        out_shape=jax.ShapeDtypeStruct((atoms, 2 * count), BF16),
+        in_specs=[VMEM] * 2,
+        out_specs=VMEM,
         scratch_shapes=[pltpu.VMEM((atoms, count), F32)],
-        compiler_params=pltpu.CompilerParams(vmem_limit_bytes=12 << 20),
+        compiler_params=pltpu.CompilerParams(vmem_limit_bytes=8 << 20),
         cost_estimate=pl.CostEstimate(flops=6 << 30, bytes_accessed=2 << 20, transcendentals=0),
         name="table",
-    )(seat, waves, places, wave_filter)
+    )(waves, places)
 
 
 def thirds(value):
@@ -329,9 +322,16 @@
 
 
 def ahead_kernel(
-    seat, pairs, count, embedding, far, close, places, weight, ahead, above, projected, lefts, rights, far_places, sem
+    seat, pairs, count, embedding, far, close, places, weight, wave_filter,
+    ahead, scale,
+    above, projected, lefts, rights, far_places, tile, sem, tile_sem, *, atoms_all,
 ):
     atoms = embedding.shape[0]
+    mine = wave_filter.at[
+        pl.ds(pl.multiple_of(seat[1] * 8, 8), 8), pl.ds(pl.multiple_of(seat[2] * TILE, TILE), TILE)
+    ]
+    filtering = pltpu.make_async_copy(mine, tile, tile_sem)
+    filtering.start()
 
     @pl.when(seat[0] == 0)
     def _():
@@ -346,6 +346,8 @@
     lefts[...] = left.T.astype(BF16)
     store_tiles(rights, 0, right)
     ahead[...] = jnp.zeros_like(ahead)
+    filtering.wait()
+    scale[...] = tile[...] * (1.0 / math.sqrt(atoms_all))
     pltpu.make_async_copy(far, above, sem).wait()
     projected[pl.ds(atoms, atoms), :] = dot(above[pl.ds(0, atoms), :], weight[...]).astype(BF16)
     unpack_places(above, far_places)
@@ -368,71 +370,87 @@
 def behind_kernel(
     seat, pairs, count, pairs_below, count_below, cotangent, far, close, places, weight,
     mixed,
-    below, back, lefts, lefts_below, rights, far_places, sem,
+    sources, back, lefts, rights, far_places, listed, sem, own_sem,
 ):
     atoms = cotangent.shape[0]
     tiles = atoms // TILE
+    own = pltpu.make_async_copy(cotangent, sources.at[pl.ds(0, atoms)], own_sem)
+    own.start()
+    packed = sources.at[pl.ds(atoms, ROWS)]
 
     @pl.when(seat[0] == 0)
     def _():
-        pltpu.make_async_copy(far, below, sem).start()
+        pltpu.make_async_copy(far, packed, sem).start()
 
     @pl.when(seat[0] != 0)
     def _():
-        pltpu.make_async_copy(close, below, sem).start()
+        pltpu.make_async_copy(close, packed, sem).start()
+
+    live = jnp.int32(0)
+    for p in range(pairs.shape[1]):
+        u, v = pairs[0, p], pairs[1, p]
+        listed[0, live] = u
+        listed[1, live] = jnp.where(v < tiles, v, v - tiles)
+        live = live + jnp.where((p < count[0]) & (v < tiles), 1, 0)
+        u, v = pairs_below[0, p], pairs_below[1, p]
+        listed[0, live] = u + tiles
+        listed[1, live] = jnp.where(v < tiles, v, v - tiles)
+        live = live + jnp.where((p < count_below[0]) & (v >= tiles), 1, 0)
+    for j in range(GROUP):
+        listed[0, live + j] = jnp.int32(0)
+        listed[1, live + j] = jnp.int32(0)
 
     left, right = features(places[...])
-    lefts[...] = left.T.astype(BF16)
+    lefts[pl.ds(0, atoms), :] = left.T.astype(BF16)
     store_tiles(rights, 0, right)
     back[...] = jnp.zeros_like(back)
-    pltpu.make_async_copy(far, below, sem).wait()
-    unpack_places(below, far_places)
+    own.wait()
+    pltpu.make_async_copy(far, packed, sem).wait()
+    unpack_places(packed, far_places)
     left, _ = features(far_places[...])
-    lefts_below[...] = left.T.astype(BF16)
-
-    def own_of(v):
-        return jnp.where(v < tiles, v, v - tiles)
-
-    @pl.loop(0, pairs.shape[1] // GROUP)
+    lefts[pl.ds(atoms, atoms), :] = left.T.astype(BF16)
+
+    @pl.loop(0, lax.shift_right_logical(live + (GROUP - 1), 2))
     def _(g):
         parts = []
         for j in range(GROUP):
             p = g * GROUP + j
-            u, v = pairs[0, p], pairs[1, p]
-            k = jnp.exp(dot(lefts[rows_of(u), :], rights[own_of(v)]) + SHIFT)
-            k = jnp.where((p < count[0]) & (v < tiles), k, 0.0)
-            parts.append((own_of(v), dot(k.T.astype(BF16), cotangent[rows_of(u), :])))
-            u, v = pairs_below[0, p], pairs_below[1, p]
-            k = jnp.exp(dot(lefts_below[rows_of(u), :], rights[own_of(v)]) + SHIFT)
-            k = jnp.where((p < count_below[0]) & (v >= tiles), k, 0.0)
-            parts.append((own_of(v), dot(k.T.astype(BF16), below[rows_of(u), :])))
+            u, v = listed[0, p], listed[1, p]
+            k = jnp.exp(dot(lefts[rows_of(u), :], rights[v]) + SHIFT)
+            k = jnp.where(p < live, k, 0.0)
+            parts.append((v, dot(k.T.astype(BF16), sources[rows_of(u), :])))
         for t, part in parts:
             back[rows_of(t), :] += part
 
     mixed[...] = dot(back[...].astype(BF16), weight[...], ((1,), (1,)))
 
 
-def near_ahead(seat, pairs, count, embedding, far, close, places, weight):
+def near_ahead(seat, pairs, count, embedding, far, close, places, weight, wave_filter, atoms_all):
     atoms, channels = embedding.shape
     tiles = atoms // TILE
     hbm = pl.BlockSpec(memory_space=pltpu.HBM)
     return pl.pallas_call(
-        ahead_kernel,
-        out_shape=jax.ShapeDtypeStruct((atoms, channels), F32),
-        in_specs=[SMEM] * 3 + [VMEM, hbm, hbm, VMEM, VMEM],
-        out_specs=VMEM,
+        functools.partial(ahead_kernel, atoms_all=atoms_all),
+        out_shape=(
+            jax.ShapeDtypeStruct((atoms, channels), F32),
+            jax.ShapeDtypeStruct((8, TILE), F32),
+        ),
+        in_specs=[SMEM] * 3 + [VMEM, hbm, hbm, VMEM, VMEM, hbm],
+        out_specs=(VMEM, VMEM),
         scratch_shapes=[
             pltpu.VMEM((ROWS, channels), BF16),
             pltpu.VMEM((2 * atoms, channels), BF16),
             pltpu.VMEM((atoms, 96), BF16),
             pltpu.VMEM((2 * tiles, 96, TILE), BF16),
             pltpu.VMEM((3, atoms), F32),
+            pltpu.VMEM((8, TILE), F32),
+            pltpu.SemaphoreType.DMA(()),
             pltpu.SemaphoreType.DMA(()),
         ],
         compiler_params=pltpu.CompilerParams(vmem_limit_bytes=12 << 20),
         cost_estimate=pl.CostEstimate(flops=5 << 30, bytes_accessed=2 << 20, transcendentals=0),
         name="near_ahead",
-    )(seat, pairs, count, embedding, in_hbm(far), in_hbm(close), places, weight)
+    )(seat, pairs, count, embedding, in_hbm(far), in_hbm(close), places, weight, in_hbm(wave_filter))
 
 
 def near_behind(seat, pairs, count, pairs_below, count_below, cotangent, far, close, places, weight):
@@ -442,21 +460,24 @@
     return pl.pallas_call(
         behind_kernel,
         out_shape=jax.ShapeDtypeStruct((atoms, channels), F32),
-        in_specs=[SMEM] * 5 + [VMEM, hbm, hbm, VMEM, VMEM],
+        in_specs=[SMEM] * 5 + [hbm] * 3 + [VMEM, VMEM],
         out_specs=VMEM,
         scratch_shapes=[
-            pltpu.VMEM((ROWS, channels), BF16),
+            pltpu.VMEM((atoms + ROWS, channels), BF16),
             pltpu.VMEM((atoms, channels), F32),
-            pltpu.VMEM((atoms, 96), BF16),
-            pltpu.VMEM((atoms, 96), BF16),
+            pltpu.VMEM((2 * atoms, 96), BF16),
             pltpu.VMEM((tiles, 96, TILE), BF16),
             pltpu.VMEM((3, atoms), F32),
+            pltpu.SMEM((2, 2 * pairs.shape[1] + GROUP), jnp.int32),
+            pltpu.SemaphoreType.DMA(()),
             pltpu.SemaphoreType.DMA(()),
         ],
         compiler_params=pltpu.CompilerParams(vmem_limit_bytes=12 << 20),
         cost_estimate=pl.CostEstimate(flops=5 << 30, bytes_accessed=2 << 20, transcendentals=0),
         name="near_behind",
-    )(seat, pairs, count, pairs_below, count_below, cotangent, in_hbm(far), in_hbm(close), places, weight)
+    )(
+        seat, pairs, count, pairs_below, count_below, in_hbm(cotangent), in_hbm(far), in_hbm(close), places, weight
+    )
 
 
 def final_kernel(seat, own, other, table, ahead, mixed, message, grad, matrix):
@@ -497,7 +518,7 @@
         compiler_params=pltpu.CompilerParams(vmem_limit_bytes=16 << 20),
         cost_estimate=pl.CostEstimate(flops=1 << 30, bytes_accessed=4 << 20, transcendentals=0),
         name="final",
-    )(seat, own, other, *map(in_hbm, (table, ahead, mixed)))
+    )(seat, own, other, table, in_hbm(ahead), in_hbm(mixed))
 
 
 def body(
@@ -520,13 +541,15 @@
     total = add(kept, given)
     chip = lax.all_to_all(total, ("y", "x"), 0, 0, tiled=True)
     close = lax.ppermute(to_close, "core", swap)
-    table, scale = tables(seat, wave_index, fractional, wave_filter, atoms_all)
+    table = tables(wave_index, fractional)
     summed = gather_sum(chip)
     parts = lax.all_to_all(summed, ALONG_Z, 0, 0, tiled=True)
     tail = jnp.where(seat[0] == 0, far[PAIRS:ROWS, :TILE], close[PAIRS:ROWS, :TILE]).astype(jnp.int32)
     pairs_below, count_below = tail[0:2, : listed.shape[1]], tail[LIVE - PAIRS, 0:1]
+    ahead, scale = near_ahead(
+        seat, listed, counts, embedding, far, close, fractional, short_weight, wave_filter, atoms_all
+    )
     mine = lax.all_to_all(coefficients(parts, scale), ALONG_Z, 0, 0, tiled=True)
-    ahead = near_ahead(seat[:1], listed, counts, embedding, far, close, fractional, short_weight)
     mixed = near_behind(
         seat[:1], listed, counts, pairs_below, count_below, cotangent, far, close, fractional, short_weight
     )

time: 121 us -> 116 us (0.959)
  waiting for transfers between devices: 26.4 us -> 33.5 us
  Pallas kernels: 32.8 us -> 26.3 us
  starting transfers between devices: 54.2 us -> 49.9 us
  local copies, waits for them, and re-layouts: 4.6 us -> 3.29 us
    all_to_all x1, waiting for transfers between devices: 0.01 us -> 11.3 us  [body(): chip = lax.all_to_all(total, ('y', 'x'), 0, 0, tiled=True)]
    all_to_all x1, waiting for transfers between devices: 12.9 us -> 4.88 us  [body(): parts = lax.all_to_all(summed, ALONG_Z, 0, 0, tiled=True)]
    pallas_call x1, Pallas kernels: 9.64 us -> 4.26 us  [near_behind(): pl.pallas_call(behind_kernel, out_shape=jax.ShapeDtypeStruct((atoms, chan...]
    all_to_all x1, waiting for transfers between devices: 2.17 us -> 5.94 us  [body(): lax.all_to_all(copies(mine), ('y', 'x'), 0, 0, tiled=True)]
    ppermute x1, starting transfers between devices: 6.94 us -> 3.37 us  [body(): lax.ppermute(to_far, FINE, [(i, (i + (1 if i % 2 else -1)) % size) for i...]
    all_to_all x1, starting transfers between devices: 6.8 us -> 3.57 us  [body(): lax.all_to_all(copies(mine), ('y', 'x'), 0, 0, tiled=True)]
    all_to_all x1, starting transfers between devices: 6.11 us -> 8.49 us  [body(): parts = lax.all_to_all(summed, ALONG_Z, 0, 0, tiled=True)]
    unnamed x24 -> x16, local copies, waits for them, and re-layouts: 4.09 us -> 2.77 us
  transfers between devices with their start and end apart: 8 -> 8, of which waited for: 3 -> 4; matrix products, arithmetic and copies ran while one was open for 1% -> 1% of each run, Pallas kernels for 21% -> 16%
where the time goes in v5:
time: 116 us; the launch traced here: 115 us
  starting transfers between devices  49.9 us (43%)
  waiting for transfers between devices  33.5 us (29%)
  Pallas kernels  26.3 us (23%)
  local copies, waits for them, and re-layouts  3.29 us (3%)
  between operations  1.53 us (1%)
    all_to_all x1, waiting for transfers between devices, body(): mine = lax.all_to_all(coefficients(parts, scale), ALONG_Z, 0, 0, tiled=True)  11.3 us
    all_to_all x1, waiting for transfers between devices, body(): chip = lax.all_to_all(total, ('y', 'x'), 0, 0, tiled=True)  11.3 us
    ppermute x1, starting transfers between devices, body(): close = lax.ppermute(to_close, 'core', swap)  9.36 us
    ppermute x1, starting transfers between devices, body(): given = lax.ppermute(given, 'core', swap)  8.75 us
    all_to_all x1, starting transfers between devices, body(): parts = lax.all_to_all(summed, ALONG_Z, 0, 0, tiled=True)  8.49 us
    all_to_all x1, starting transfers between devices, body(): mine = lax.all_to_all(coefficients(parts, scale), ALONG_Z, 0, 0, tiled=True)  6.58 us
    ppermute x1, starting transfers between devices, body(): other = lax.ppermute(coeffs, 'core', swap)  6.15 us
    all_to_all x1, waiting for transfers between devices, body(): lax.all_to_all(copies(mine), ('y', 'x'), 0, 0, tiled=True)  5.94 us
  transfers between devices with their start and end apart: 8, of which 4 were waited for; matrix products, arithmetic and copies ran while one was open for 1% of the time, Pallas kernels for 16%

profile of v5, /device:TPU:1, one launch (start us, length us, event | category | flops | bytes accessed | tf_op | source)
XLA Modules:
  0.0 115.2 jit_solution(7106149076212548206)
XLA Ops:
  0.6 0.0 copy-start.3
  0.7 3.2 %sums.3 = f32[16,16,8,128]{3,2,1,0:T(8,128)S(1)} custom-call(s32[1]{0:T(128)S(6)} %sub.3.seat, s32[3,512]{1,0:T(4,128)} %waves.1, bf16[3,1024]{1,0:T(4,128)(2,1)} %places.5, bf16[1024,256]{1,0:T(8,128)(2,1)} %embedding.3, bf16[1024,256]{1,0:T(8,128)(2,1)} %cotangent.3), custom_call_target="tpu_custom_call" | custom-call | flops 536870912 | bytes 2097152 | tf_op jit(solution)/shard_map/sums/pallas_call | solution.py:97
  3.8 8.7 %collective-permute-start = (f32[16,16,8,128]{3,2,1,0:T(8,128)S(1)}, f32[16,16,8,128]{3,2,1,0:T(8,128)S(1)}, u32[]{:S(2)}, u32[]{:S(2)}) collective-permute-start(f32[16,16,8,128]{3,2,1,0:T(8,128)S(1)} %sums.3), channel_id=1, source_target_pairs={{0,1},{1,0},{2,3},{3,2},{4,5},{5,4},{6,7},{7,6},{8,9},{9,8},{10,11... | collective-permute-start | bytes 3145736 | tf_op jit(solution)/shard_map/ppermute | solution.py:539
  13.2 1.3 %pack.1 = (bf16[1056,256]{1,0:T(8,128)(2,1)S(1)}, bf16[1056,256]{1,0:T(8,128)(2,1)S(1)}) custom-call(s32[1]{0:T(128)} %bitcast.seat, bf16[1024,256]{1,0:T(8,128)(2,1)} %embedding.3, bf16[1024,256]{1,0:T(8,128)(2,1)} %cotangent.3, bf16[3,1024]{1,0:T(4,128)(2,1)} %places.5, s32[2,24]{1,0:T(2,128)} %bitcast.8, s32[1]{0:T(128)S(6)} %copy.10.count), custom_call_target="tpu_custom_call" | custom-call | tf_op jit(solution)/shard_map/pack/pallas_call | solution.py:284
  14.5 3.4 %collective-permute-start.1 = (bf16[1056,256]{1,0:T(8,128)(2,1)S(1)}, bf16[1056,256]{1,0:T(8,128)(2,1)S(1)}, u32[]{:S(2)}, u32[]{:S(2)}) collective-permute-start(bf16[1056,256]{1,0:T(8,128)(2,1)S(1)} %get-tuple-element.6), channel_id=1, source_target_pairs={{0,511},{1,2},{2,1},{3,4},{4,3},{5,6},{6,5},{7,8},{8,7},{9,10},{10... | collective-permute-start | bytes 1622024 | tf_op jit(solution)/shard_map/ppermute | solution.py:537
  17.9 9.4 %collective-permute-start.2 = (bf16[1056,256]{1,0:T(8,128)(2,1)S(1)}, bf16[1056,256]{1,0:T(8,128)(2,1)}, u32[]{:S(2)}, u32[]{:S(2)}) collective-permute-start(bf16[1056,256]{1,0:T(8,128)(2,1)S(1)} %get-tuple-element.7), channel_id=1, source_target_pairs={{0,1},{1,0},{2,3},{3,2},{4,5},{5,4},{6,7},{7,6},{8,9},{9,8},{10,11... | collective-permute-start | bytes 1622024 | tf_op jit(solution)/shard_map/ppermute | solution.py:543
  27.3 2.5 %sums.2.a = f32[16,16,8,128]{3,2,1,0:T(8,128)S(1)} custom-call(s32[1]{0:T(128)} %bitcast.seat, s32[3,512]{1,0:T(4,128)S(1)} %copy-done.4, bf16[3,1024]{1,0:T(4,128)(2,1)S(1)} %copy-done.3, bf16[1024,256]{1,0:T(8,128)(2,1)} %embedding.3, bf16[1024,256]{1,0:T(8,128)(2,1)} %cotangent.3), custom_call_target="tpu_custom_call" | custom-call | flops 536870912 | bytes 2097152 | tf_op jit(solution)/shard_map/sums/pallas_call | solution.py:97
  29.7 0.0 copy-start
  29.8 0.0 copy-start.5
  29.8 1.0 add.17
  30.7 3.6 %all-to-all-start = ((bf16[16,16,8,128]{3,2,1,0:T(8,128)(2,1)}), bf16[16,16,8,128]{3,2,1,0:T(8,128)(2,1)S(1)}, u32[]{:S(2)}, u32[]{:S(2)}) async-start(bf16[16,16,8,128]{3,2,1,0:T(8,128)(2,1)} %add.17), calls=%async_computation | async-start | bytes 1048576 | tf_op jit(solution)/shard_map/all_to_all | solution.py:542
  34.3 0.1 pad_add_fusion.seat
  34.4 11.3 %all-to-all-done.a = bf16[16,16,8,128]{3,2,1,0:T(8,128)(2,1)S(1)} async-done(((bf16[16,16,8,128]{3,2,1,0:T(8,128)(2,1)}), bf16[16,16,8,128]{3,2,1,0:T(8,128)(2,1)S(1)}, u32[]{:S(2)}, u32[]{:S(2)}) %all-to-all-start) | async-done | bytes 524320 | tf_op jit(solution)/shard_map/all_to_all | solution.py:542
  45.7 0.9 plane_sum.1
  46.7 8.5 %all-to-all-start.1 = ((f32[16,8,128]{2,1,0:T(8,128)}), f32[16,8,128]{2,1,0:T(8,128)S(1)}, u32[]{:S(2)}, u32[]{:S(2)}) async-start(f32[16,8,128]{2,1,0:T(8,128)} %plane_sum.1), calls=%async_computation.1 | async-start | bytes 131072 | tf_op jit(solution)/shard_map/all_to_all | solution.py:546
  55.2 0.8 copy-done.7
  56.0 5.0 %near_ahead.1 = (f32[1024,256]{1,0:T(8,128)S(1)}, f32[8,128]{1,0:T(8,128)S(1)}) custom-call(s32[3]{0:T(128)S(1)} %pad_add_fusion.seat, s32[2,24]{1,0:T(2,128)S(1)} %bitcast.9, s32[1]{0:T(128)S(6)} %copy.10.count, bf16[1024,256]{1,0:T(8,128)(2,1)S(1)} %copy-done, bf16[1056,256]{1,0:T(8,128)(2,1)} %copy-done.7, ...), custom_call_target="tpu_custom_call" | custom-call | flops 5368709120 | bytes 2097152 | tf_op jit(solution)/shard_map/near_ahead/pallas_call | solution.py:432
  61.0 1.0 copy-done.1
  62.0 4.9 %all-to-all-done.1.a = f32[16,8,128]{2,1,0:T(8,128)S(1)} async-done(((f32[16,8,128]{2,1,0:T(8,128)}), f32[16,8,128]{2,1,0:T(8,128)S(1)}, u32[]{:S(2)}, u32[]{:S(2)}) %all-to-all-start.1) | async-done | bytes 65568 | tf_op jit(solution)/shard_map/all_to_all | solution.py:546
  66.9 0.6 coefficients.1
  67.5 6.6 %all-to-all-start.2 = ((bf16[16,8,128]{2,1,0:T(8,128)(2,1)}), bf16[16,8,128]{2,1,0:T(8,128)(2,1)S(1)}, u32[]{:S(2)}, u32[]{:S(2)}) async-start(bf16[16,8,128]{2,1,0:T(8,128)(2,1)} %coefficients.1), calls=%async_computation.2 | async-start | bytes 65536 | tf_op jit(solution)/shard_map/all_to_all | solution.py:552
  74.1 11.3 %all-to-all-done.2.a = bf16[16,8,128]{2,1,0:T(8,128)(2,1)S(1)} async-done(((bf16[16,8,128]{2,1,0:T(8,128)(2,1)}), bf16[16,8,128]{2,1,0:T(8,128)(2,1)S(1)}, u32[]{:S(2)}, u32[]{:S(2)}) %all-to-all-start.2) | async-done | bytes 32800 | tf_op jit(solution)/shard_map/all_to_all | solution.py:552
  85.4 0.9 copies.1
  86.3 3.6 %all-to-all-start.3 = ((bf16[16,16,8,128]{3,2,1,0:T(8,128)(2,1)}), bf16[16,16,8,128]{3,2,1,0:T(8,128)(2,1)S(1)}, u32[]{:S(2)}, u32[]{:S(2)}) async-start(bf16[16,16,8,128]{3,2,1,0:T(8,128)(2,1)} %copies.1), calls=%async_computation.3 | async-start | bytes 1048576 | tf_op jit(solution)/shard_map/all_to_all | solution.py:556
  89.9 3.0 %table.1 = bf16[1024,1024]{1,0:T(8,128)(2,1)S(1)} custom-call(s32[3,512]{1,0:T(4,128)S(1)} %copy-done.4, bf16[3,1024]{1,0:T(4,128)(2,1)S(1)} %copy-done.3), custom_call_target="tpu_custom_call" | custom-call | flops 6442450944 | bytes 2097152 | tf_op jit(solution)/shard_map/table/pallas_call | solution.py:212
  92.9 5.9 %all-to-all-done.3 = bf16[16,16,8,128]{3,2,1,0:T(8,128)(2,1)S(1)} async-done(((bf16[16,16,8,128]{3,2,1,0:T(8,128)(2,1)}), bf16[16,16,8,128]{3,2,1,0:T(8,128)(2,1)S(1)}, u32[]{:S(2)}, u32[]{:S(2)}) %all-to-all-start.3) | async-done | bytes 524320 | tf_op jit(solution)/shard_map/all_to_all | solution.py:556
  98.9 6.2 %collective-permute-start.3 = (bf16[256,8,128]{2,1,0:T(8,128)(2,1)S(1)}, bf16[256,8,128]{2,1,0:T(8,128)(2,1)S(1)}, u32[]{:S(2)}, u32[]{:S(2)}) collective-permute-start(bf16[256,8,128]{2,1,0:T(8,128)(2,1)S(1)} %bitcast.6), channel_id=1, source_target_pairs={{0,1},{1,0},{2,3},{3,2},{4,5},{5,4},{6,7},{7,6},{8,9},{9,8},{10,11... | collective-permute-start | bytes 1572872 | tf_op jit(solution)/shard_map/ppermute | solution.py:557
  105.0 0.7 fusion
  105.7 0.5 slice.19
  106.2 4.3 %near_behind.1.mixed = f32[1024,256]{1,0:T(8,128)S(1)} custom-call(s32[1]{0:T(128)} %bitcast.seat, s32[2,24]{1,0:T(2,128)S(1)} %bitcast.10, s32[1]{0:T(128)S(6)} %copy.10.count, s32[2,24]{1,0:T(2,128)S(1)} %slice.18.pairs_below, s32[1]{0:T(128)} %bitcast.5.count_below, bf16[1024,256]{1,0:T(8,128)(2,1)} %cotangent.3, bf16[1056,256]{1,0:T(8,128)(2,1)} %copy-done.7, ...), custom_call_target="tpu_custom_call" | custom-call | flops 5368709120 | bytes 2097152 | tf_op jit(solution)/shard_map/near_behind/pallas_call | solution.py:460
  110.5 1.0 copy-done.2
  111.5 3.7 %final.1 = (bf16[1024,256]{1,0:T(8,128)(2,1)}, bf16[1024,256]{1,0:T(8,128)(2,1)}) custom-call(s32[3]{0:T(128)S(1)} %pad_add_fusion.seat, bf16[256,8,128]{2,1,0:T(8,128)(2,1)S(1)} %bitcast.7, bf16[256,8,128]{2,1,0:T(8,128)(2,1)S(1)} %collective-permute-done.3.other, bf16[1024,1024]{1,0:T(8,128)(2,1)S(1)} %table.1, f32[1024,256]{1,0:T(8,128)} %copy-done.1, ...), custom_call_target="tpu_custom_call" | custom-call | flops 1073741824 | bytes 4194304 | tf_op jit(solution)/shard_map/final/pallas_call | solution.py:504
  (15 shorter events, 0.0 us)
Async XLA Ops:
  0.6 26.6 %copy-start.3 = (bf16[3,1024]{1,0:T(4,128)(2,1)S(1)}, bf16[3,1024]{1,0:T(4,128)(2,1)}, u32[]{:S(2)}) copy-start(bf16[3,1024]{1,0:T(4,128)(2,1)} %places.5) | copy-start | bytes 18436
  0.6 26.6 %copy-start.4 = (s32[3,512]{1,0:T(4,128)S(1)}, s32[3,512]{1,0:T(4,128)}, u32[]{:S(2)}) copy-start(s32[3,512]{1,0:T(4,128)} %waves.1) | copy-start | bytes 18436
  3.8 26.0 %collective-permute-start = (f32[16,16,8,128]{3,2,1,0:T(8,128)S(1)}, f32[16,16,8,128]{3,2,1,0:T(8,128)S(1)}, u32[]{:S(2)}, u32[]{:S(2)}) collective-permute-start(f32[16,16,8,128]{3,2,1,0:T(8,128)S(1)} %sums.3), channel_id=1, source_target_pairs={{0,1},{1,0},{2,3},{3,2},{4,5},{5,4},{6,7},{7,6},{8,9},{9,8},{10,11... | collective-permute-start | bytes 3145736 | tf_op jit(solution)/shard_map/ppermute | solution.py:539
  14.5 40.7 %collective-permute-start.1 = (bf16[1056,256]{1,0:T(8,128)(2,1)S(1)}, bf16[1056,256]{1,0:T(8,128)(2,1)S(1)}, u32[]{:S(2)}, u32[]{:S(2)}) collective-permute-start(bf16[1056,256]{1,0:T(8,128)(2,1)S(1)} %get-tuple-element.6), channel_id=1, source_target_pairs={{0,511},{1,2},{2,1},{3,4},{4,3},{5,6},{6,5},{7,8},{8,7},{9,10},{10... | collective-permute-start | bytes 1622024 | tf_op jit(solution)/shard_map/ppermute | solution.py:537
  17.9 37.3 %collective-permute-start.2 = (bf16[1056,256]{1,0:T(8,128)(2,1)S(1)}, bf16[1056,256]{1,0:T(8,128)(2,1)}, u32[]{:S(2)}, u32[]{:S(2)}) collective-permute-start(bf16[1056,256]{1,0:T(8,128)(2,1)S(1)} %get-tuple-element.7), channel_id=1, source_target_pairs={{0,1},{1,0},{2,3},{3,2},{4,5},{5,4},{6,7},{7,6},{8,9},{9,8},{10,11... | collective-permute-start | bytes 1622024 | tf_op jit(solution)/shard_map/ppermute | solution.py:543
  29.7 26.2 %copy-start = (bf16[1024,256]{1,0:T(8,128)(2,1)S(1)}, bf16[1024,256]{1,0:T(8,128)(2,1)}, u32[]{:S(2)}) copy-start(bf16[1024,256]{1,0:T(8,128)(2,1)} %embedding.3) | copy-start | bytes 1572868
  29.8 26.2 %copy-start.5 = (s32[24,2]{0,1:T(2,128)S(1)}, s32[24,2]{0,1:T(2,128)}, u32[]{:S(2)}) copy-start(s32[24,2]{0,1:T(2,128)} %param.12) | copy-start | bytes 580
  29.8 26.2 %copy-start.6 = (bf16[256,256]{1,0:T(8,128)(2,1)S(1)}, bf16[256,256]{1,0:T(8,128)(2,1)}, u32[]{:S(2)}) copy-start(bf16[256,256]{1,0:T(8,128)(2,1)} %weight.3) | copy-start | bytes 393220
  30.7 15.0 %all-to-all-start = ((bf16[16,16,8,128]{3,2,1,0:T(8,128)(2,1)}), bf16[16,16,8,128]{3,2,1,0:T(8,128)(2,1)S(1)}, u32[]{:S(2)}, u32[]{:S(2)}) async-start(bf16[16,16,8,128]{3,2,1,0:T(8,128)(2,1)} %add.17), calls=%async_computation | async-start | bytes 1048576 | tf_op jit(solution)/shard_map/all_to_all | solution.py:542
  46.7 20.2 %all-to-all-start.1 = ((f32[16,8,128]{2,1,0:T(8,128)}), f32[16,8,128]{2,1,0:T(8,128)S(1)}, u32[]{:S(2)}, u32[]{:S(2)}) async-start(f32[16,8,128]{2,1,0:T(8,128)} %plane_sum.1), calls=%async_computation.1 | async-start | bytes 131072 | tf_op jit(solution)/shard_map/all_to_all | solution.py:546
  55.2 0.8 copy-start.7
  61.0 1.0 copy-start.1
  67.5 17.9 %all-to-all-start.2 = ((bf16[16,8,128]{2,1,0:T(8,128)(2,1)}), bf16[16,8,128]{2,1,0:T(8,128)(2,1)S(1)}, u32[]{:S(2)}, u32[]{:S(2)}) async-start(bf16[16,8,128]{2,1,0:T(8,128)(2,1)} %coefficients.1), calls=%async_computation.2 | async-start | bytes 65536 | tf_op jit(solution)/shard_map/all_to_all | solution.py:552
  86.3 12.5 %all-to-all-start.3 = ((bf16[16,16,8,128]{3,2,1,0:T(8,128)(2,1)}), bf16[16,16,8,128]{3,2,1,0:T(8,128)(2,1)S(1)}, u32[]{:S(2)}, u32[]{:S(2)}) async-start(bf16[16,16,8,128]{3,2,1,0:T(8,128)(2,1)} %copies.1), calls=%async_computation.3 | async-start | bytes 1048576 | tf_op jit(solution)/shard_map/all_to_all | solution.py:556
  98.9 12.6 %collective-permute-start.3 = (bf16[256,8,128]{2,1,0:T(8,128)(2,1)S(1)}, bf16[256,8,128]{2,1,0:T(8,128)(2,1)S(1)}, u32[]{:S(2)}, u32[]{:S(2)}) collective-permute-start(bf16[256,8,128]{2,1,0:T(8,128)(2,1)S(1)} %bitcast.6), channel_id=1, source_target_pairs={{0,1},{1,0},{2,3},{3,2},{4,5},{5,4},{6,7},{7,6},{8,9},{9,8},{10,11... | collective-permute-start | bytes 1572872 | tf_op jit(solution)/shard_map/ppermute | solution.py:557
  110.5 1.0 copy-start.2

commit v6 on v5

--- a/solution.py
+++ b/solution.py
@@ -480,41 +480,62 @@
     )
 
 
-def final_kernel(seat, own, other, table, ahead, mixed, message, grad, matrix):
+BLOCKS = 4
+
+
+def final_kernel(
+    seat, own, other, table, ahead_far, mixed_far, message_far, grad_far, ahead, mixed, message, grad, matrix, sems, load_sems
+):
     channels = message.shape[1]
-
-    @pl.when(pl.program_id(0) == 0)
-    def _():
-        for half, ref in ((seat[0], own), (1 - seat[0], other)):
-            for r in range(0, 64, 2):
-                rows = pl.ds(pl.multiple_of(half * 512 + 8 * r, 16), 16)
-                for q in range(4):
-                    pair = [ref[(r + d) * 4 + q].astype(F32) for d in range(2)]
-                    matrix[rows, 128 * q : 128 * q + 128] = jnp.concatenate(pair, axis=0).astype(BF16)
-
-    message[...] = (dot(table[...], matrix[:, :channels]) + ahead[...]).astype(BF16)
-    grad[...] = (dot(table[...], matrix[:, channels:]) + mixed[...]).astype(BF16)
-
-
-def final(seat, own, other, table, ahead, mixed, steps=2):
-    atoms, channels = ahead.shape
-    rows = atoms // steps
-    block = pl.BlockSpec((rows, channels), lambda i: (i, 0))
-    whole = pl.BlockSpec(own.shape, lambda i: (0, 0, 0), pipeline_mode=pl.Buffered(1))
+    size = message.shape[0] // BLOCKS
+    loads = [
+        [
+            pltpu.make_async_copy(far.at[pl.ds(i * size, size)], ref.at[pl.ds(i * size, size)], load_sems.at[side, i])
+            for side, (far, ref) in enumerate(((ahead_far, ahead), (mixed_far, mixed)))
+        ]
+        for i in range(BLOCKS)
+    ]
+    for both in loads:
+        for load in both:
+            load.start()
+    for half, ref in ((seat[0], own), (1 - seat[0], other)):
+        for r in range(0, 64, 2):
+            rows = pl.ds(pl.multiple_of(half * 512 + 8 * r, 16), 16)
+            for q in range(4):
+                pair = [ref[(r + d) * 4 + q].astype(F32) for d in range(2)]
+                matrix[rows, 128 * q : 128 * q + 128] = jnp.concatenate(pair, axis=0).astype(BF16)
+
+    stores = []
+    for i in range(BLOCKS):
+        rows = pl.ds(i * size, size)
+        for side, (near, out, far) in enumerate(((ahead, message, message_far), (mixed, grad, grad_far))):
+            part = dot(table[rows, :], matrix[:, side * channels : side * channels + channels])
+            loads[i][side].wait()
+            out[rows, :] = (part + near[rows, :]).astype(BF16)
+            store = pltpu.make_async_copy(out.at[rows], far.at[rows], sems.at[side, i])
+            store.start()
+            stores.append(store)
+    for store in stores:
+        store.wait()
+
+
+def final(seat, own, other, table, ahead, mixed):
+    shape = ahead.shape
+    hbm = pl.BlockSpec(memory_space=pltpu.HBM)
     return pl.pallas_call(
         final_kernel,
-        grid=(steps,),
-        out_shape=(jax.ShapeDtypeStruct((atoms, channels), BF16),) * 2,
-        in_specs=[
-            SMEM,
-            whole,
-            whole,
-            pl.BlockSpec((rows, table.shape[1]), lambda i: (i, 0)),
-            block,
-            block,
+        out_shape=(jax.ShapeDtypeStruct(shape, BF16),) * 2,
+        in_specs=[SMEM] + [VMEM] * 3 + [hbm] * 2,
+        out_specs=(hbm, hbm),
+        scratch_shapes=[
+            pltpu.VMEM(shape, F32),
+            pltpu.VMEM(shape, F32),
+            pltpu.VMEM(shape, BF16),
+            pltpu.VMEM(shape, BF16),
+            pltpu.VMEM((table.shape[1], 2 * shape[1]), BF16),
+            pltpu.SemaphoreType.DMA((2, BLOCKS)),
+            pltpu.SemaphoreType.DMA((2, BLOCKS)),
         ],
-        out_specs=(block, block),
-        scratch_shapes=[pltpu.VMEM((table.shape[1], 2 * channels), BF16)],
         compiler_params=pltpu.CompilerParams(vmem_limit_bytes=16 << 20),
         cost_estimate=pl.CostEstimate(flops=1 << 30, bytes_accessed=4 << 20, transcendentals=0),
         name="final",

time: 116 us -> 118 us (1.017)
  Pallas kernels: 26.3 us -> 28.3 us
    pallas_call x1, Pallas kernels: 3.67 us -> 5.66 us  [final(): pl.pallas_call(final_kernel, out_shape=(jax.ShapeDtypeStruct(shape, BF16)...]
  transfers between devices with their start and end apart: 8 -> 8, of which waited for: 4 -> 4; matrix products, arithmetic and copies ran while one was open for 1% -> 1% of each run, Pallas kernels for 16% -> 15%
where the time goes in v6:
time: 118 us; the launch traced here: 117 us
  starting transfers between devices  49.9 us (42%)
  waiting for transfers between devices  33.5 us (28%)
  Pallas kernels  28.3 us (24%)
  local copies, waits for them, and re-layouts  3.29 us (3%)
  between operations  1.53 us (1%)
    all_to_all x1, waiting for transfers between devices, body(): mine = lax.all_to_all(coefficients(parts, scale), ALONG_Z, 0, 0, tiled=True)  11.3 us
    all_to_all x1, waiting for transfers between devices, body(): chip = lax.all_to_all(total, ('y', 'x'), 0, 0, tiled=True)  11.3 us
    ppermute x1, starting transfers between devices, body(): close = lax.ppermute(to_close, 'core', swap)  9.36 us
    ppermute x1, starting transfers between devices, body(): given = lax.ppermute(given, 'core', swap)  8.75 us
    all_to_all x1, starting transfers between devices, body(): parts = lax.all_to_all(summed, ALONG_Z, 0, 0, tiled=True)  8.49 us
    all_to_all x1, starting transfers between devices, body(): mine = lax.all_to_all(coefficients(parts, scale), ALONG_Z, 0, 0, tiled=True)  6.58 us
    ppermute x1, starting transfers between devices, body(): other = lax.ppermute(coeffs, 'core', swap)  6.15 us
    all_to_all x1, waiting for transfers between devices, body(): lax.all_to_all(copies(mine), ('y', 'x'), 0, 0, tiled=True)  5.94 us
  transfers between devices with their start and end apart: 8, of which 4 were waited for; matrix products, arithmetic and copies ran while one was open for 1% of the time, Pallas kernels for 15%

profile of v6, /device:TPU:1, one launch (start us, length us, event | category | flops | bytes accessed | tf_op | source)
XLA Modules:
  0.0 117.2 jit_solution(8783912091547229931)
XLA Ops:
  0.6 0.0 copy-start.3
  0.7 3.2 %sums.3 = f32[16,16,8,128]{3,2,1,0:T(8,128)S(1)} custom-call(s32[1]{0:T(128)S(6)} %sub.3.seat, s32[3,512]{1,0:T(4,128)} %waves.1, bf16[3,1024]{1,0:T(4,128)(2,1)} %places.5, bf16[1024,256]{1,0:T(8,128)(2,1)} %embedding.3, bf16[1024,256]{1,0:T(8,128)(2,1)} %cotangent.3), custom_call_target="tpu_custom_call" | custom-call | flops 536870912 | bytes 2097152 | tf_op jit(solution)/shard_map/sums/pallas_call | solution.py:97
  3.8 8.7 %collective-permute-start = (f32[16,16,8,128]{3,2,1,0:T(8,128)S(1)}, f32[16,16,8,128]{3,2,1,0:T(8,128)S(1)}, u32[]{:S(2)}, u32[]{:S(2)}) collective-permute-start(f32[16,16,8,128]{3,2,1,0:T(8,128)S(1)} %sums.3), channel_id=1, source_target_pairs={{0,1},{1,0},{2,3},{3,2},{4,5},{5,4},{6,7},{7,6},{8,9},{9,8},{10,11... | collective-permute-start | bytes 3145736 | tf_op jit(solution)/shard_map/ppermute | solution.py:560
  13.2 1.3 %pack.1 = (bf16[1056,256]{1,0:T(8,128)(2,1)S(1)}, bf16[1056,256]{1,0:T(8,128)(2,1)S(1)}) custom-call(s32[1]{0:T(128)} %bitcast.seat, bf16[1024,256]{1,0:T(8,128)(2,1)} %embedding.3, bf16[1024,256]{1,0:T(8,128)(2,1)} %cotangent.3, bf16[3,1024]{1,0:T(4,128)(2,1)} %places.5, s32[2,24]{1,0:T(2,128)} %bitcast.8, s32[1]{0:T(128)S(6)} %copy.10.count), custom_call_target="tpu_custom_call" | custom-call | tf_op jit(solution)/shard_map/pack/pallas_call | solution.py:284
  14.5 3.4 %collective-permute-start.1 = (bf16[1056,256]{1,0:T(8,128)(2,1)S(1)}, bf16[1056,256]{1,0:T(8,128)(2,1)S(1)}, u32[]{:S(2)}, u32[]{:S(2)}) collective-permute-start(bf16[1056,256]{1,0:T(8,128)(2,1)S(1)} %get-tuple-element.6), channel_id=1, source_target_pairs={{0,511},{1,2},{2,1},{3,4},{4,3},{5,6},{6,5},{7,8},{8,7},{9,10},{10... | collective-permute-start | bytes 1622024 | tf_op jit(solution)/shard_map/ppermute | solution.py:558
  17.9 9.4 %collective-permute-start.2 = (bf16[1056,256]{1,0:T(8,128)(2,1)S(1)}, bf16[1056,256]{1,0:T(8,128)(2,1)}, u32[]{:S(2)}, u32[]{:S(2)}) collective-permute-start(bf16[1056,256]{1,0:T(8,128)(2,1)S(1)} %get-tuple-element.7), channel_id=1, source_target_pairs={{0,1},{1,0},{2,3},{3,2},{4,5},{5,4},{6,7},{7,6},{8,9},{9,8},{10,11... | collective-permute-start | bytes 1622024 | tf_op jit(solution)/shard_map/ppermute | solution.py:564
  27.3 2.5 %sums.2.a = f32[16,16,8,128]{3,2,1,0:T(8,128)S(1)} custom-call(s32[1]{0:T(128)} %bitcast.seat, s32[3,512]{1,0:T(4,128)S(1)} %copy-done.4, bf16[3,1024]{1,0:T(4,128)(2,1)S(1)} %copy-done.3, bf16[1024,256]{1,0:T(8,128)(2,1)} %embedding.3, bf16[1024,256]{1,0:T(8,128)(2,1)} %cotangent.3), custom_call_target="tpu_custom_call" | custom-call | flops 536870912 | bytes 2097152 | tf_op jit(solution)/shard_map/sums/pallas_call | solution.py:97
  29.7 0.0 copy-start
  29.8 0.0 copy-start.5
  29.8 1.0 add.17
  30.7 3.6 %all-to-all-start = ((bf16[16,16,8,128]{3,2,1,0:T(8,128)(2,1)}), bf16[16,16,8,128]{3,2,1,0:T(8,128)(2,1)S(1)}, u32[]{:S(2)}, u32[]{:S(2)}) async-start(bf16[16,16,8,128]{3,2,1,0:T(8,128)(2,1)} %add.17), calls=%async_computation | async-start | bytes 1048576 | tf_op jit(solution)/shard_map/all_to_all | solution.py:563
  34.3 0.1 pad_add_fusion.seat
  34.4 11.3 %all-to-all-done.a = bf16[16,16,8,128]{3,2,1,0:T(8,128)(2,1)S(1)} async-done(((bf16[16,16,8,128]{3,2,1,0:T(8,128)(2,1)}), bf16[16,16,8,128]{3,2,1,0:T(8,128)(2,1)S(1)}, u32[]{:S(2)}, u32[]{:S(2)}) %all-to-all-start) | async-done | bytes 524320 | tf_op jit(solution)/shard_map/all_to_all | solution.py:563
  45.7 0.9 plane_sum.1
  46.7 8.5 %all-to-all-start.1 = ((f32[16,8,128]{2,1,0:T(8,128)}), f32[16,8,128]{2,1,0:T(8,128)S(1)}, u32[]{:S(2)}, u32[]{:S(2)}) async-start(f32[16,8,128]{2,1,0:T(8,128)} %plane_sum.1), calls=%async_computation.1 | async-start | bytes 131072 | tf_op jit(solution)/shard_map/all_to_all | solution.py:567
  55.2 0.8 copy-done.7
  56.0 5.0 %near_ahead.1 = (f32[1024,256]{1,0:T(8,128)S(1)}, f32[8,128]{1,0:T(8,128)S(1)}) custom-call(s32[3]{0:T(128)S(1)} %pad_add_fusion.seat, s32[2,24]{1,0:T(2,128)S(1)} %bitcast.9, s32[1]{0:T(128)S(6)} %copy.10.count, bf16[1024,256]{1,0:T(8,128)(2,1)S(1)} %copy-done, bf16[1056,256]{1,0:T(8,128)(2,1)} %copy-done.7, ...), custom_call_target="tpu_custom_call" | custom-call | flops 5368709120 | bytes 2097152 | tf_op jit(solution)/shard_map/near_ahead/pallas_call | solution.py:432
  61.0 1.0 copy-done.1
  62.0 4.9 %all-to-all-done.1.a = f32[16,8,128]{2,1,0:T(8,128)S(1)} async-done(((f32[16,8,128]{2,1,0:T(8,128)}), f32[16,8,128]{2,1,0:T(8,128)S(1)}, u32[]{:S(2)}, u32[]{:S(2)}) %all-to-all-start.1) | async-done | bytes 65568 | tf_op jit(solution)/shard_map/all_to_all | solution.py:567
  66.9 0.6 coefficients.1
  67.5 6.6 %all-to-all-start.2 = ((bf16[16,8,128]{2,1,0:T(8,128)(2,1)}), bf16[16,8,128]{2,1,0:T(8,128)(2,1)S(1)}, u32[]{:S(2)}, u32[]{:S(2)}) async-start(bf16[16,8,128]{2,1,0:T(8,128)(2,1)} %coefficients.1), calls=%async_computation.2 | async-start | bytes 65536 | tf_op jit(solution)/shard_map/all_to_all | solution.py:573
  74.1 11.3 %all-to-all-done.2.a = bf16[16,8,128]{2,1,0:T(8,128)(2,1)S(1)} async-done(((bf16[16,8,128]{2,1,0:T(8,128)(2,1)}), bf16[16,8,128]{2,1,0:T(8,128)(2,1)S(1)}, u32[]{:S(2)}, u32[]{:S(2)}) %all-to-all-start.2) | async-done | bytes 32800 | tf_op jit(solution)/shard_map/all_to_all | solution.py:573
  85.4 0.9 copies.1
  86.3 3.6 %all-to-all-start.3 = ((bf16[16,16,8,128]{3,2,1,0:T(8,128)(2,1)}), bf16[16,16,8,128]{3,2,1,0:T(8,128)(2,1)S(1)}, u32[]{:S(2)}, u32[]{:S(2)}) async-start(bf16[16,16,8,128]{3,2,1,0:T(8,128)(2,1)} %copies.1), calls=%async_computation.3 | async-start | bytes 1048576 | tf_op jit(solution)/shard_map/all_to_all | solution.py:577
  89.9 3.0 %table.1 = bf16[1024,1024]{1,0:T(8,128)(2,1)S(1)} custom-call(s32[3,512]{1,0:T(4,128)S(1)} %copy-done.4, bf16[3,1024]{1,0:T(4,128)(2,1)S(1)} %copy-done.3), custom_call_target="tpu_custom_call" | custom-call | flops 6442450944 | bytes 2097152 | tf_op jit(solution)/shard_map/table/pallas_call | solution.py:212
  92.9 5.9 %all-to-all-done.3 = bf16[16,16,8,128]{3,2,1,0:T(8,128)(2,1)S(1)} async-done(((bf16[16,16,8,128]{3,2,1,0:T(8,128)(2,1)}), bf16[16,16,8,128]{3,2,1,0:T(8,128)(2,1)S(1)}, u32[]{:S(2)}, u32[]{:S(2)}) %all-to-all-start.3) | async-done | bytes 524320 | tf_op jit(solution)/shard_map/all_to_all | solution.py:577
  98.9 6.2 %collective-permute-start.3 = (bf16[256,8,128]{2,1,0:T(8,128)(2,1)S(1)}, bf16[256,8,128]{2,1,0:T(8,128)(2,1)S(1)}, u32[]{:S(2)}, u32[]{:S(2)}) collective-permute-start(bf16[256,8,128]{2,1,0:T(8,128)(2,1)S(1)} %bitcast.6), channel_id=1, source_target_pairs={{0,1},{1,0},{2,3},{3,2},{4,5},{5,4},{6,7},{7,6},{8,9},{9,8},{10,11... | collective-permute-start | bytes 1572872 | tf_op jit(solution)/shard_map/ppermute | solution.py:578
  105.0 0.7 fusion
  105.7 0.5 slice.19
  106.2 4.3 %near_behind.1.mixed_far = f32[1024,256]{1,0:T(8,128)S(1)} custom-call(s32[1]{0:T(128)} %bitcast.seat, s32[2,24]{1,0:T(2,128)S(1)} %bitcast.10, s32[1]{0:T(128)S(6)} %copy.10.count, s32[2,24]{1,0:T(2,128)S(1)} %slice.18.pairs_below, s32[1]{0:T(128)} %bitcast.5.count_below, bf16[1024,256]{1,0:T(8,128)(2,1)} %cotangent.3, bf16[1056,256]{1,0:T(8,128)(2,1)} %copy-done.7, ...), custom_call_target="tpu_custom_call" | custom-call | flops 5368709120 | bytes 2097152 | tf_op jit(solution)/shard_map/near_behind/pallas_call | solution.py:460
  110.5 1.0 copy-done.2
  111.5 5.7 %final.1 = (bf16[1024,256]{1,0:T(8,128)(2,1)}, bf16[1024,256]{1,0:T(8,128)(2,1)}) custom-call(s32[3]{0:T(128)S(1)} %pad_add_fusion.seat, bf16[256,8,128]{2,1,0:T(8,128)(2,1)S(1)} %bitcast.7, bf16[256,8,128]{2,1,0:T(8,128)(2,1)S(1)} %collective-permute-done.3.other, bf16[1024,1024]{1,0:T(8,128)(2,1)S(1)} %table.1, f32[1024,256]{1,0:T(8,128)} %copy-done.1, ...), custom_call_target="tpu_custom_call" | custom-call | flops 1073741824 | bytes 4194304 | tf_op jit(solution)/shard_map/final/pallas_call | solution.py:525
  (15 shorter events, 0.0 us)
Async XLA Ops:
  0.6 26.6 %copy-start.3 = (bf16[3,1024]{1,0:T(4,128)(2,1)S(1)}, bf16[3,1024]{1,0:T(4,128)(2,1)}, u32[]{:S(2)}) copy-start(bf16[3,1024]{1,0:T(4,128)(2,1)} %places.5) | copy-start | bytes 18436
  0.6 26.6 %copy-start.4 = (s32[3,512]{1,0:T(4,128)S(1)}, s32[3,512]{1,0:T(4,128)}, u32[]{:S(2)}) copy-start(s32[3,512]{1,0:T(4,128)} %waves.1) | copy-start | bytes 18436
  3.8 26.0 %collective-permute-start = (f32[16,16,8,128]{3,2,1,0:T(8,128)S(1)}, f32[16,16,8,128]{3,2,1,0:T(8,128)S(1)}, u32[]{:S(2)}, u32[]{:S(2)}) collective-permute-start(f32[16,16,8,128]{3,2,1,0:T(8,128)S(1)} %sums.3), channel_id=1, source_target_pairs={{0,1},{1,0},{2,3},{3,2},{4,5},{5,4},{6,7},{7,6},{8,9},{9,8},{10,11... | collective-permute-start | bytes 3145736 | tf_op jit(solution)/shard_map/ppermute | solution.py:560
  14.5 40.7 %collective-permute-start.1 = (bf16[1056,256]{1,0:T(8,128)(2,1)S(1)}, bf16[1056,256]{1,0:T(8,128)(2,1)S(1)}, u32[]{:S(2)}, u32[]{:S(2)}) collective-permute-start(bf16[1056,256]{1,0:T(8,128)(2,1)S(1)} %get-tuple-element.6), channel_id=1, source_target_pairs={{0,511},{1,2},{2,1},{3,4},{4,3},{5,6},{6,5},{7,8},{8,7},{9,10},{10... | collective-permute-start | bytes 1622024 | tf_op jit(solution)/shard_map/ppermute | solution.py:558
  17.9 37.3 %collective-permute-start.2 = (bf16[1056,256]{1,0:T(8,128)(2,1)S(1)}, bf16[1056,256]{1,0:T(8,128)(2,1)}, u32[]{:S(2)}, u32[]{:S(2)}) collective-permute-start(bf16[1056,256]{1,0:T(8,128)(2,1)S(1)} %get-tuple-element.7), channel_id=1, source_target_pairs={{0,1},{1,0},{2,3},{3,2},{4,5},{5,4},{6,7},{7,6},{8,9},{9,8},{10,11... | collective-permute-start | bytes 1622024 | tf_op jit(solution)/shard_map/ppermute | solution.py:564
  29.7 26.2 %copy-start = (bf16[1024,256]{1,0:T(8,128)(2,1)S(1)}, bf16[1024,256]{1,0:T(8,128)(2,1)}, u32[]{:S(2)}) copy-start(bf16[1024,256]{1,0:T(8,128)(2,1)} %embedding.3) | copy-start | bytes 1572868
  29.8 26.2 %copy-start.5 = (s32[24,2]{0,1:T(2,128)S(1)}, s32[24,2]{0,1:T(2,128)}, u32[]{:S(2)}) copy-start(s32[24,2]{0,1:T(2,128)} %param.12) | copy-start | bytes 580
  29.8 26.2 %copy-start.6 = (bf16[256,256]{1,0:T(8,128)(2,1)S(1)}, bf16[256,256]{1,0:T(8,128)(2,1)}, u32[]{:S(2)}) copy-start(bf16[256,256]{1,0:T(8,128)(2,1)} %weight.3) | copy-start | bytes 393220
  30.7 15.0 %all-to-all-start = ((bf16[16,16,8,128]{3,2,1,0:T(8,128)(2,1)}), bf16[16,16,8,128]{3,2,1,0:T(8,128)(2,1)S(1)}, u32[]{:S(2)}, u32[]{:S(2)}) async-start(bf16[16,16,8,128]{3,2,1,0:T(8,128)(2,1)} %add.17), calls=%async_computation | async-start | bytes 1048576 | tf_op jit(solution)/shard_map/all_to_all | solution.py:563
  46.7 20.2 %all-to-all-start.1 = ((f32[16,8,128]{2,1,0:T(8,128)}), f32[16,8,128]{2,1,0:T(8,128)S(1)}, u32[]{:S(2)}, u32[]{:S(2)}) async-start(f32[16,8,128]{2,1,0:T(8,128)} %plane_sum.1), calls=%async_computation.1 | async-start | bytes 131072 | tf_op jit(solution)/shard_map/all_to_all | solution.py:567
  55.2 0.8 copy-start.7
  61.0 1.0 copy-start.1
  67.5 17.9 %all-to-all-start.2 = ((bf16[16,8,128]{2,1,0:T(8,128)(2,1)}), bf16[16,8,128]{2,1,0:T(8,128)(2,1)S(1)}, u32[]{:S(2)}, u32[]{:S(2)}) async-start(bf16[16,8,128]{2,1,0:T(8,128)(2,1)} %coefficients.1), calls=%async_computation.2 | async-start | bytes 65536 | tf_op jit(solution)/shard_map/all_to_all | solution.py:573
  86.3 12.5 %all-to-all-start.3 = ((bf16[16,16,8,128]{3,2,1,0:T(8,128)(2,1)}), bf16[16,16,8,128]{3,2,1,0:T(8,128)(2,1)S(1)}, u32[]{:S(2)}, u32[]{:S(2)}) async-start(bf16[16,16,8,128]{3,2,1,0:T(8,128)(2,1)} %copies.1), calls=%async_computation.3 | async-start | bytes 1048576 | tf_op jit(solution)/shard_map/all_to_all | solution.py:577
  98.9 12.6 %collective-permute-start.3 = (bf16[256,8,128]{2,1,0:T(8,128)(2,1)S(1)}, bf16[256,8,128]{2,1,0:T(8,128)(2,1)S(1)}, u32[]{:S(2)}, u32[]{:S(2)}) collective-permute-start(bf16[256,8,128]{2,1,0:T(8,128)(2,1)S(1)} %bitcast.6), channel_id=1, source_target_pairs={{0,1},{1,0},{2,3},{3,2},{4,5},{5,4},{6,7},{7,6},{8,9},{9,8},{10,11... | collective-permute-start | bytes 1572872 | tf_op jit(solution)/shard_map/ppermute | solution.py:578
  110.5 1.0 copy-start.2

commit v7 on v5

--- a/solution.py
+++ b/solution.py
@@ -133,19 +133,20 @@
     )(a, b)
 
 
-def gather_sum_kernel(a, out):
-    @pl.loop(0, out.shape[0])
-    def _(i):
+def plane_sum_kernel(a, out):
+    for i in range(a.shape[1]):
         total = a[0, i].astype(F32)
         for k in range(1, a.shape[0]):
             total = total + a[k, i].astype(F32)
-        out[i] = total
-
-
-def gather_sum(a):
-    return pl.pallas_call(
-        gather_sum_kernel,
-        out_shape=jax.ShapeDtypeStruct(a.shape[1:], F32),
+        mine = total.astype(BF16)
+        for k in range(out.shape[0]):
+            out[k, i] = mine
+
+
+def plane_sum(a):
+    return pl.pallas_call(
+        plane_sum_kernel,
+        out_shape=jax.ShapeDtypeStruct(a.shape, BF16),
         in_specs=[VMEM],
         out_specs=VMEM,
         compiler_params=pltpu.CompilerParams(vmem_limit_bytes=4 << 20),
@@ -154,12 +155,13 @@
 
 
 def coefficients_kernel(a, scale, out):
-    total = a[0]
-    for k in range(1, a.shape[0]):
-        total = total + a[k]
-    mine = (total * scale[...]).astype(BF16)
-    for k in range(out.shape[0]):
-        out[k] = mine
+    for i in range(a.shape[1]):
+        total = a[0, i].astype(F32)
+        for k in range(1, a.shape[0]):
+            total = total + a[k, i].astype(F32)
+        mine = (total * scale[i]).astype(BF16)
+        for k in range(out.shape[0]):
+            out[k, i] = mine
 
 
 def coefficients(a, scale):
@@ -171,26 +173,6 @@
         compiler_params=pltpu.CompilerParams(vmem_limit_bytes=4 << 20),
         name="coefficients",
     )(a, scale)
-
-
-def copies_kernel(a, out):
-    for k in range(a.shape[0]):
-        mine = a[k]
-
-        @pl.loop(0, out.shape[0], unroll=True)
-        def _(i):
-            out[i, k] = mine
-
-
-def copies(a):
-    return pl.pallas_call(
-        copies_kernel,
-        out_shape=jax.ShapeDtypeStruct((16, *a.shape), BF16),
-        in_specs=[VMEM],
-        out_specs=VMEM,
-        compiler_params=pltpu.CompilerParams(vmem_limit_bytes=4 << 20),
-        name="copies",
-    )(a)
 
 
 def table_kernel(waves, places, table, turns):
@@ -327,9 +309,7 @@
     above, projected, lefts, rights, far_places, tile, sem, tile_sem, *, atoms_all,
 ):
     atoms = embedding.shape[0]
-    mine = wave_filter.at[
-        pl.ds(pl.multiple_of(seat[1] * 8, 8), 8), pl.ds(pl.multiple_of(seat[2] * TILE, TILE), TILE)
-    ]
+    mine = wave_filter.at[pl.ds(pl.multiple_of(seat[1] * 32, 32), 32)]
     filtering = pltpu.make_async_copy(mine, tile, tile_sem)
     filtering.start()
 
@@ -347,7 +327,9 @@
     store_tiles(rights, 0, right)
     ahead[...] = jnp.zeros_like(ahead)
     filtering.wait()
-    scale[...] = tile[...] * (1.0 / math.sqrt(atoms_all))
+    for i in range(scale.shape[0]):
+        rows, cols = i // 4 * 8, i % 2 * TILE
+        scale[i] = tile[rows : rows + 8, cols : cols + TILE] * (1.0 / math.sqrt(atoms_all))
     pltpu.make_async_copy(far, above, sem).wait()
     projected[pl.ds(atoms, atoms), :] = dot(above[pl.ds(0, atoms), :], weight[...]).astype(BF16)
     unpack_places(above, far_places)
@@ -433,7 +415,7 @@
         functools.partial(ahead_kernel, atoms_all=atoms_all),
         out_shape=(
             jax.ShapeDtypeStruct((atoms, channels), F32),
-            jax.ShapeDtypeStruct((8, TILE), F32),
+            jax.ShapeDtypeStruct((16, 8, TILE), F32),
         ),
         in_specs=[SMEM] * 3 + [VMEM, hbm, hbm, VMEM, VMEM, hbm],
         out_specs=(VMEM, VMEM),
@@ -443,7 +425,7 @@
             pltpu.VMEM((atoms, 96), BF16),
             pltpu.VMEM((2 * tiles, 96, TILE), BF16),
             pltpu.VMEM((3, atoms), F32),
-            pltpu.VMEM((8, TILE), F32),
+            pltpu.VMEM((32, channels), F32),
             pltpu.SemaphoreType.DMA(()),
             pltpu.SemaphoreType.DMA(()),
         ],
@@ -527,8 +509,7 @@
     devices = math.prod(lax.axis_size(name) for name in FINE)
     atoms_all = embedding.shape[0] * devices
     core, x, y = (lax.axis_index(name).astype(jnp.int32) for name in ("core", "x", "y"))
-    z_lo, z_hi = lax.axis_index("z_lo").astype(jnp.int32), lax.axis_index("z_hi").astype(jnp.int32)
-    seat = jnp.stack([core, core * 32 + (y & 1) * 16 + x * 4 + z_lo, z_hi & 1])
+    seat = jnp.stack([core, core * 8 + (y & 1) * 4 + x])
     swap = [(0, 1), (1, 0)]
 
     listed = tile_pairs.T
@@ -542,18 +523,17 @@
     chip = lax.all_to_all(total, ("y", "x"), 0, 0, tiled=True)
     close = lax.ppermute(to_close, "core", swap)
     table = tables(wave_index, fractional)
-    summed = gather_sum(chip)
+    summed = plane_sum(chip)
     parts = lax.all_to_all(summed, ALONG_Z, 0, 0, tiled=True)
     tail = jnp.where(seat[0] == 0, far[PAIRS:ROWS, :TILE], close[PAIRS:ROWS, :TILE]).astype(jnp.int32)
     pairs_below, count_below = tail[0:2, : listed.shape[1]], tail[LIVE - PAIRS, 0:1]
     ahead, scale = near_ahead(
         seat, listed, counts, embedding, far, close, fractional, short_weight, wave_filter, atoms_all
     )
-    mine = lax.all_to_all(coefficients(parts, scale), ALONG_Z, 0, 0, tiled=True)
     mixed = near_behind(
         seat[:1], listed, counts, pairs_below, count_below, cotangent, far, close, fractional, short_weight
     )
-    coeffs = lax.all_to_all(copies(mine), ("y", "x"), 0, 0, tiled=True).reshape(256, 8, 128)
+    coeffs = lax.all_to_all(coefficients(parts, scale), ("y", "x"), 0, 0, tiled=True).reshape(256, 8, 128)
     other = lax.ppermute(coeffs, "core", swap)
     return final(seat, coeffs, other, table, ahead, mixed)
 

time: 116 us -> 131 us (1.13)
  blocking collectives: 0 us -> 13.9 us
  waiting for transfers between devices: 33.5 us -> 47 us
  starting transfers between devices: 49.9 us -> 38.9 us
    ppermute x1, waiting for transfers between devices: 0.01 us -> 38.6 us  [body(): lax.ppermute(to_far, FINE, [(i, (i + (1 if i % 2 else -1)) % size) for i...]
    all_to_all x3 -> x1, waiting for transfers between devices: 28.6 us -> 8.38 us  [body(): lax.all_to_all(coefficients(parts, scale), ('y', 'x'), 0, 0, tiled=True)]
    all_to_all x0 -> x1, blocking collectives: none -> 13.9 us  [body(): chip = lax.all_to_all(total, ('y', 'x'), 0, 0, tiled=True)]
    all_to_all x3 -> x1, starting transfers between devices: 13.7 us -> 3.62 us  [body(): lax.all_to_all(coefficients(parts, scale), ('y', 'x'), 0, 0, tiled=True)]
    ppermute x1, starting transfers between devices: 9.36 us -> 1.92 us  [body(): close = lax.ppermute(to_close, 'core', swap)]
    ppermute x1, starting transfers between devices: 3.37 us -> 9.2 us  [body(): lax.ppermute(to_far, FINE, [(i, (i + (1 if i % 2 else -1)) % size) for i...]
    all_to_all x1, waiting for transfers between devices: 4.88 us -> 0.01 us  [body(): parts = lax.all_to_all(summed, ALONG_Z, 0, 0, tiled=True)]
    all_to_all x1, starting transfers between devices: 8.49 us -> 13.2 us  [body(): parts = lax.all_to_all(summed, ALONG_Z, 0, 0, tiled=True)]
  transfers between devices with their start and end apart: 8 -> 6, of which waited for: 4 -> 2; matrix products, arithmetic and copies ran while one was open for 1% -> 1% of each run, Pallas kernels for 16% -> 12%
where the time goes in v7:
time: 131 us; the launch traced here: 130 us
  waiting for transfers between devices  47 us (36%)
  starting transfers between devices  38.9 us (30%)
  Pallas kernels  25 us (19%)
  blocking collectives  13.9 us (11%)
  local copies, waits for them, and re-layouts  3.34 us (3%)
  between operations  1.5 us (1%)
    ppermute x1, waiting for transfers between devices, body(): lax.ppermute(to_far, FINE, [(i, (i + (1 if i % 2 else -1)) % size) for i...  38.6 us
    all_to_all x1, blocking collectives, body(): chip = lax.all_to_all(total, ('y', 'x'), 0, 0, tiled=True)  13.9 us
    all_to_all x1, starting transfers between devices, body(): parts = lax.all_to_all(summed, ALONG_Z, 0, 0, tiled=True)  13.2 us
    ppermute x1, starting transfers between devices, body(): lax.ppermute(to_far, FINE, [(i, (i + (1 if i % 2 else -1)) % size) for i...  9.2 us
    ppermute x1, starting transfers between devices, body(): given = lax.ppermute(given, 'core', swap)  8.75 us
    all_to_all x1, waiting for transfers between devices, body(): lax.all_to_all(coefficients(parts, scale), ('y', 'x'), 0, 0, tiled=True)  8.38 us
    pallas_call x2, Pallas kernels, partial_sums(): pl.pallas_call(sums_kernel, out_shape=jax.ShapeDtypeStruct((16, 16, 8, 12...  5.62 us
    pallas_call x1, Pallas kernels, near_ahead(): pl.pallas_call(functools.partial(ahead_kernel, atoms_all=atoms_all), out_...  5.21 us
  transfers between devices with their start and end apart: 6, of which 2 were waited for; matrix products, arithmetic and copies ran while one was open for 1% of the time, Pallas kernels for 12%

profile of v7, /device:TPU:1, one launch (start us, length us, event | category | flops | bytes accessed | tf_op | source)
XLA Modules:
  0.0 130.5 jit_solution(6135921728679315244)
XLA Ops:
  0.6 0.0 copy-start.3
  0.7 3.2 %sums.3 = f32[16,16,8,128]{3,2,1,0:T(8,128)S(1)} custom-call(s32[1]{0:T(128)S(6)} %sub.3.seat, s32[3,512]{1,0:T(4,128)} %waves.1, bf16[3,1024]{1,0:T(4,128)(2,1)} %places.5, bf16[1024,256]{1,0:T(8,128)(2,1)} %embedding.3, bf16[1024,256]{1,0:T(8,128)(2,1)} %cotangent.3), custom_call_target="tpu_custom_call" | custom-call | flops 536870912 | bytes 2097152 | tf_op jit(solution)/shard_map/sums/pallas_call | solution.py:97
  3.8 8.7 %collective-permute-start = (f32[16,16,8,128]{3,2,1,0:T(8,128)S(1)}, f32[16,16,8,128]{3,2,1,0:T(8,128)S(1)}, u32[]{:S(2)}, u32[]{:S(2)}) collective-permute-start(f32[16,16,8,128]{3,2,1,0:T(8,128)S(1)} %sums.3), channel_id=1, source_target_pairs={{0,1},{1,0},{2,3},{3,2},{4,5},{5,4},{6,7},{7,6},{8,9},{9,8},{10,11... | collective-permute-start | bytes 3145736 | tf_op jit(solution)/shard_map/ppermute | solution.py:520
  12.6 2.5 %sums.2.a = f32[16,16,8,128]{3,2,1,0:T(8,128)S(1)} custom-call(s32[1]{0:T(128)} %bitcast.seat, s32[3,512]{1,0:T(4,128)S(1)} %copy-done.5, bf16[3,1024]{1,0:T(4,128)(2,1)S(1)} %copy-done.3, bf16[1024,256]{1,0:T(8,128)(2,1)} %embedding.3, bf16[1024,256]{1,0:T(8,128)(2,1)} %cotangent.3), custom_call_target="tpu_custom_call" | custom-call | flops 536870912 | bytes 2097152 | tf_op jit(solution)/shard_map/sums/pallas_call | solution.py:97
  15.1 0.2 add.11
  15.2 0.0 copy-start
  15.3 0.0 copy-start.4
  15.3 0.0 copy-start.6
  15.3 0.0 copy-start.7
  15.3 13.9 %all_to_all.15.a = bf16[16,16,8,128]{3,2,1,0:T(8,128)(2,1)S(1)} all-to-all(bf16[16,16,8,128]{3,2,1,0:T(8,128)(2,1)S(1)} %add.11), channel_id=1, replica_groups=mesh['z_lo'=4,'y'=4,'x'=4,'z_hi'=4,'core'=2] {'y','x'}, dimensions={0} | all-to-all | bytes 1048576 | tf_op jit(solution)/shard_map/all_to_all | solution.py:523
  29.2 0.9 plane_sum.1
  30.2 13.2 %all-to-all-start.1 = ((bf16[16,16,8,128]{3,2,1,0:T(8,128)(2,1)}), bf16[16,16,8,128]{3,2,1,0:T(8,128)(2,1)S(1)}, u32[]{:S(2)}, u32[]{:S(2)}) async-start(bf16[16,16,8,128]{3,2,1,0:T(8,128)(2,1)} %plane_sum.1), calls=%async_computation.1 | async-start | bytes 1048576 | tf_op jit(solution)/shard_map/all_to_all | solution.py:527
  44.0 1.3 pack.1
  45.3 9.2 %collective-permute-start.1 = (bf16[1056,256]{1,0:T(8,128)(2,1)S(1)}, bf16[1056,256]{1,0:T(8,128)(2,1)S(1)}, u32[]{:S(2)}, u32[]{:S(2)}) collective-permute-start(bf16[1056,256]{1,0:T(8,128)(2,1)S(1)} %get-tuple-element.6), channel_id=1, source_target_pairs={{0,511},{1,2},{2,1},{3,4},{4,3},{5,6},{6,5},{7,8},{8,7},{9,10},{10... | collective-permute-start | bytes 1622024 | tf_op jit(solution)/shard_map/ppermute | solution.py:518
  54.5 1.9 %collective-permute-start.2 = (bf16[1056,256]{1,0:T(8,128)(2,1)S(1)}, bf16[1056,256]{1,0:T(8,128)(2,1)}, u32[]{:S(2)}, u32[]{:S(2)}) collective-permute-start(bf16[1056,256]{1,0:T(8,128)(2,1)S(1)} %get-tuple-element.7), channel_id=1, source_target_pairs={{0,1},{1,0},{2,3},{3,2},{4,5},{5,4},{6,7},{7,6},{8,9},{9,8},{10,11... | collective-permute-start | bytes 1622024 | tf_op jit(solution)/shard_map/ppermute | solution.py:524
  56.5 0.1 pad_add_fusion.seat
  56.5 38.6 %collective-permute-done.1.far = bf16[1056,256]{1,0:T(8,128)(2,1)S(1)} collective-permute-done((bf16[1056,256]{1,0:T(8,128)(2,1)S(1)}, bf16[1056,256]{1,0:T(8,128)(2,1)S(1)}, u32[]{:S(2)}, u32[]{:S(2)}) %collective-permute-start.1) | collective-permute-done | bytes 540704 | tf_op jit(solution)/shard_map/ppermute | solution.py:518
  95.1 0.0 collective-permute-done.2.close
  95.2 0.8 copy-done.8
  96.0 5.2 %near_ahead.1 = (f32[1024,256]{1,0:T(8,128)S(1)}, f32[16,8,128]{2,1,0:T(8,128)S(1)}) custom-call(s32[2]{0:T(128)S(1)} %pad_add_fusion.seat, s32[2,24]{1,0:T(2,128)S(1)} %bitcast.8, s32[1]{0:T(128)S(6)} %copy.10.count, bf16[1024,256]{1,0:T(8,128)(2,1)S(1)} %copy-done, bf16[1056,256]{1,0:T(8,128)(2,1)} %copy-done.8, ...), custom_call_target="tpu_custom_call" | custom-call | flops 5368709120 | bytes 2097152 | tf_op jit(solution)/shard_map/near_ahead/pallas_call | solution.py:414
  101.2 1.0 copy-done.1
  102.2 0.9 coefficients.1
  103.1 3.6 %all-to-all-start.2 = ((bf16[16,16,8,128]{3,2,1,0:T(8,128)(2,1)}), bf16[16,16,8,128]{3,2,1,0:T(8,128)(2,1)S(1)}, u32[]{:S(2)}, u32[]{:S(2)}) async-start(bf16[16,16,8,128]{3,2,1,0:T(8,128)(2,1)} %coefficients.1), calls=%async_computation.2 | async-start | bytes 1048576 | tf_op jit(solution)/shard_map/all_to_all | solution.py:536
  106.7 3.0 %table.1 = bf16[1024,1024]{1,0:T(8,128)(2,1)S(1)} custom-call(s32[3,512]{1,0:T(4,128)S(1)} %copy-done.5, bf16[3,1024]{1,0:T(4,128)(2,1)S(1)} %copy-done.4), custom_call_target="tpu_custom_call" | custom-call | flops 6442450944 | bytes 2097152 | tf_op jit(solution)/shard_map/table/pallas_call | solution.py:194
  109.8 8.4 %all-to-all-done.2 = bf16[16,16,8,128]{3,2,1,0:T(8,128)(2,1)S(1)} async-done(((bf16[16,16,8,128]{3,2,1,0:T(8,128)(2,1)}), bf16[16,16,8,128]{3,2,1,0:T(8,128)(2,1)S(1)}, u32[]{:S(2)}, u32[]{:S(2)}) %all-to-all-start.2) | async-done | bytes 524320 | tf_op jit(solution)/shard_map/all_to_all | solution.py:536
  118.1 2.2 %collective-permute-start.3 = (bf16[256,8,128]{2,1,0:T(8,128)(2,1)S(1)}, bf16[256,8,128]{2,1,0:T(8,128)(2,1)S(1)}, u32[]{:S(2)}, u32[]{:S(2)}) collective-permute-start(bf16[256,8,128]{2,1,0:T(8,128)(2,1)S(1)} %bitcast.5), channel_id=1, source_target_pairs={{0,1},{1,0},{2,3},{3,2},{4,5},{5,4},{6,7},{7,6},{8,9},{9,8},{10,11... | collective-permute-start | bytes 1572872 | tf_op jit(solution)/shard_map/ppermute | solution.py:537
  120.3 0.7 fusion
  121.0 0.5 slice.19
  121.5 4.3 %near_behind.1.mixed = f32[1024,256]{1,0:T(8,128)S(1)} custom-call(s32[1]{0:T(128)} %bitcast.seat, s32[2,24]{1,0:T(2,128)S(1)} %bitcast.9, s32[1]{0:T(128)S(6)} %copy.10.count, s32[2,24]{1,0:T(2,128)S(1)} %slice.18.pairs_below, s32[1]{0:T(128)} %bitcast.4.count_below, bf16[1024,256]{1,0:T(8,128)(2,1)} %cotangent.3, bf16[1056,256]{1,0:T(8,128)(2,1)} %copy-done.8, ...), custom_call_target="tpu_custom_call" | custom-call | flops 5368709120 | bytes 2097152 | tf_op jit(solution)/shard_map/near_behind/pallas_call | solution.py:442
  125.8 1.0 copy-done.2
  126.8 0.0 collective-permute-done.3.other
  126.8 3.7 %final.1 = (bf16[1024,256]{1,0:T(8,128)(2,1)}, bf16[1024,256]{1,0:T(8,128)(2,1)}) custom-call(s32[2]{0:T(128)S(1)} %pad_add_fusion.seat, bf16[256,8,128]{2,1,0:T(8,128)(2,1)S(1)} %bitcast.6, bf16[256,8,128]{2,1,0:T(8,128)(2,1)S(1)} %collective-permute-done.3.other, bf16[1024,1024]{1,0:T(8,128)(2,1)S(1)} %table.1, f32[1024,256]{1,0:T(8,128)} %copy-done.1, ...), custom_call_target="tpu_custom_call" | custom-call | flops 1073741824 | bytes 4194304 | tf_op jit(solution)/shard_map/final/pallas_call | solution.py:486
  (13 shorter events, 0.0 us)
Async XLA Ops:
  0.6 12.0 %copy-start.3 = (bf16[3,1024]{1,0:T(4,128)(2,1)S(1)}, bf16[3,1024]{1,0:T(4,128)(2,1)}, u32[]{:S(2)}) copy-start(bf16[3,1024]{1,0:T(4,128)(2,1)} %places.5) | copy-start | bytes 18436
  0.6 12.0 %copy-start.5 = (s32[3,512]{1,0:T(4,128)S(1)}, s32[3,512]{1,0:T(4,128)}, u32[]{:S(2)}) copy-start(s32[3,512]{1,0:T(4,128)} %waves.1) | copy-start | bytes 18436
  3.8 11.2 %collective-permute-start = (f32[16,16,8,128]{3,2,1,0:T(8,128)S(1)}, f32[16,16,8,128]{3,2,1,0:T(8,128)S(1)}, u32[]{:S(2)}, u32[]{:S(2)}) collective-permute-start(f32[16,16,8,128]{3,2,1,0:T(8,128)S(1)} %sums.3), channel_id=1, source_target_pairs={{0,1},{1,0},{2,3},{3,2},{4,5},{5,4},{6,7},{7,6},{8,9},{9,8},{10,11... | collective-permute-start | bytes 3145736 | tf_op jit(solution)/shard_map/ppermute | solution.py:520
  15.2 80.7 %copy-start = (bf16[1024,256]{1,0:T(8,128)(2,1)S(1)}, bf16[1024,256]{1,0:T(8,128)(2,1)}, u32[]{:S(2)}) copy-start(bf16[1024,256]{1,0:T(8,128)(2,1)} %embedding.3) | copy-start | bytes 1572868
  15.3 80.7 %copy-start.4 = (bf16[3,1024]{1,0:T(4,128)(2,1)S(1)}, bf16[3,1024]{1,0:T(4,128)(2,1)}, u32[]{:S(2)}) copy-start(bf16[3,1024]{1,0:T(4,128)(2,1)} %places.5) | copy-start | bytes 18436
  15.3 80.7 %copy-start.6 = (s32[24,2]{0,1:T(2,128)S(1)}, s32[24,2]{0,1:T(2,128)}, u32[]{:S(2)}) copy-start(s32[24,2]{0,1:T(2,128)} %param.12) | copy-start | bytes 580
  15.3 80.7 %copy-start.7 = (bf16[256,256]{1,0:T(8,128)(2,1)S(1)}, bf16[256,256]{1,0:T(8,128)(2,1)}, u32[]{:S(2)}) copy-start(bf16[256,256]{1,0:T(8,128)(2,1)} %weight.3) | copy-start | bytes 393220
  30.2 72.0 %all-to-all-start.1 = ((bf16[16,16,8,128]{3,2,1,0:T(8,128)(2,1)}), bf16[16,16,8,128]{3,2,1,0:T(8,128)(2,1)S(1)}, u32[]{:S(2)}, u32[]{:S(2)}) async-start(bf16[16,16,8,128]{3,2,1,0:T(8,128)(2,1)} %plane_sum.1), calls=%async_computation.1 | async-start | bytes 1048576 | tf_op jit(solution)/shard_map/all_to_all | solution.py:527
  45.3 49.8 %collective-permute-start.1 = (bf16[1056,256]{1,0:T(8,128)(2,1)S(1)}, bf16[1056,256]{1,0:T(8,128)(2,1)S(1)}, u32[]{:S(2)}, u32[]{:S(2)}) collective-permute-start(bf16[1056,256]{1,0:T(8,128)(2,1)S(1)} %get-tuple-element.6), channel_id=1, source_target_pairs={{0,511},{1,2},{2,1},{3,4},{4,3},{5,6},{6,5},{7,8},{8,7},{9,10},{10... | collective-permute-start | bytes 1622024 | tf_op jit(solution)/shard_map/ppermute | solution.py:518
  54.5 40.6 %collective-permute-start.2 = (bf16[1056,256]{1,0:T(8,128)(2,1)S(1)}, bf16[1056,256]{1,0:T(8,128)(2,1)}, u32[]{:S(2)}, u32[]{:S(2)}) collective-permute-start(bf16[1056,256]{1,0:T(8,128)(2,1)S(1)} %get-tuple-element.7), channel_id=1, source_target_pairs={{0,1},{1,0},{2,3},{3,2},{4,5},{5,4},{6,7},{7,6},{8,9},{9,8},{10,11... | collective-permute-start | bytes 1622024 | tf_op jit(solution)/shard_map/ppermute | solution.py:524
  95.1 0.8 copy-start.8
  101.2 1.0 copy-start.1
  103.1 15.0 %all-to-all-start.2 = ((bf16[16,16,8,128]{3,2,1,0:T(8,128)(2,1)}), bf16[16,16,8,128]{3,2,1,0:T(8,128)(2,1)S(1)}, u32[]{:S(2)}, u32[]{:S(2)}) async-start(bf16[16,16,8,128]{3,2,1,0:T(8,128)(2,1)} %coefficients.1), calls=%async_computation.2 | async-start | bytes 1048576 | tf_op jit(solution)/shard_map/all_to_all | solution.py:536
  118.1 8.7 %collective-permute-start.3 = (bf16[256,8,128]{2,1,0:T(8,128)(2,1)S(1)}, bf16[256,8,128]{2,1,0:T(8,128)(2,1)S(1)}, u32[]{:S(2)}, u32[]{:S(2)}) collective-permute-start(bf16[256,8,128]{2,1,0:T(8,128)(2,1)S(1)} %bitcast.5), channel_id=1, source_target_pairs={{0,1},{1,0},{2,3},{3,2},{4,5},{5,4},{6,7},{7,6},{8,9},{9,8},{10,11... | collective-permute-start | bytes 1572872 | tf_op jit(solution)/shard_map/ppermute | solution.py:537
  125.8 1.0 copy-start.2

commit v8 on v7

--- a/solution.py
+++ b/solution.py
@@ -221,31 +221,24 @@
 PLACES, PAIRS, LIVE, ROWS = 1024, 1040, 1048, 1056
 
 
-def pack_kernel(seat, embedding, cotangent, places_far, pairs_far, count, far, close, places, pairs, sems):
+def pack_kernel(which, embedding, cotangent, places_far, pairs_far, count, out, places, pairs, sems):
     atoms = embedding.shape[0]
     small = [
-        pltpu.make_async_copy(places_far, places, sems.at[2]),
-        pltpu.make_async_copy(pairs_far, pairs, sems.at[3]),
+        pltpu.make_async_copy(places_far, places, sems.at[1]),
+        pltpu.make_async_copy(pairs_far, pairs, sems.at[2]),
     ]
     for load in small:
         load.start()
 
-    def both(forward, backward):
-        a = pltpu.make_async_copy(embedding, backward.at[pl.ds(0, atoms)], sems.at[0])
-        b = pltpu.make_async_copy(cotangent, forward.at[pl.ds(0, atoms)], sems.at[1])
-        a.start()
-        b.start()
-        return a, b
-
-    @pl.when(seat[0] == 0)
-    def _():
-        both(close, far)
-
-    @pl.when(seat[0] != 0)
-    def _():
-        both(far, close)
-
-    width = far.shape[1]
+    @pl.when(which[0] == 0)
+    def _():
+        pltpu.make_async_copy(embedding, out.at[pl.ds(0, atoms)], sems.at[0]).start()
+
+    @pl.when(which[0] != 0)
+    def _():
+        pltpu.make_async_copy(cotangent, out.at[pl.ds(0, atoms)], sems.at[0]).start()
+
+    width = out.shape[1]
     for load in small:
         load.wait()
     coords = places[...].astype(F32)
@@ -254,28 +247,26 @@
     listed = jnp.concatenate([pairs[...].astype(F32), jnp.zeros((2, width - pairs.shape[1]), F32)], axis=1)
     listed = jnp.concatenate([listed, jnp.zeros((6, width), F32)], axis=0)
     tail = jnp.concatenate([listed, jnp.full((8, width), count[0], jnp.int32).astype(F32)], axis=0).astype(BF16)
-    for ref in (far, close):
-        ref[PLACES:PAIRS, :] = rows
-        ref[PAIRS:ROWS, :] = tail
-    pltpu.make_async_copy(embedding, far.at[pl.ds(0, atoms)], sems.at[0]).wait()
-    pltpu.make_async_copy(cotangent, close.at[pl.ds(0, atoms)], sems.at[1]).wait()
-
-
-def pack(seat, embedding, cotangent, places, pairs, count):
+    out[PLACES:PAIRS, :] = rows
+    out[PAIRS:ROWS, :] = tail
+    pltpu.make_async_copy(embedding, out.at[pl.ds(0, atoms)], sems.at[0]).wait()
+
+
+def pack(which, embedding, cotangent, places, pairs, count):
     hbm = pl.BlockSpec(memory_space=pltpu.HBM)
     return pl.pallas_call(
         pack_kernel,
-        out_shape=(jax.ShapeDtypeStruct((ROWS, embedding.shape[1]), BF16),) * 2,
+        out_shape=jax.ShapeDtypeStruct((ROWS, embedding.shape[1]), BF16),
         in_specs=[SMEM, hbm, hbm, hbm, hbm, SMEM],
-        out_specs=(VMEM, VMEM),
+        out_specs=VMEM,
         scratch_shapes=[
             pltpu.VMEM(places.shape, BF16),
             pltpu.VMEM(pairs.shape, pairs.dtype),
-            pltpu.SemaphoreType.DMA((4,)),
+            pltpu.SemaphoreType.DMA((3,)),
         ],
         compiler_params=pltpu.CompilerParams(vmem_limit_bytes=4 << 20),
         name="pack",
-    )(seat, *map(in_hbm, (embedding, cotangent, places, pairs)), count)
+    )(which, *map(in_hbm, (embedding, cotangent, places, pairs)), count)
 
 
 def in_hbm(value):
@@ -513,7 +504,7 @@
     swap = [(0, 1), (1, 0)]
 
     listed = tile_pairs.T
-    to_far, to_close = pack(seat[:1], embedding, cotangent, fractional, listed, counts)
+    to_far = pack(seat[:1], embedding, cotangent, fractional, listed, counts)
     size = math.prod(lax.axis_size(name) for name in FINE)
     far = lax.ppermute(to_far, FINE, [(i, (i + (1 if i % 2 else -1)) % size) for i in range(size)])
     given = partial_sums(1 - seat[:1], wave_index, fractional, embedding, cotangent, True)
@@ -521,6 +512,7 @@
     kept = partial_sums(seat[:1], wave_index, fractional, embedding, cotangent, False)
     total = add(kept, given)
     chip = lax.all_to_all(total, ("y", "x"), 0, 0, tiled=True)
+    to_close = pack(1 - seat[:1], embedding, cotangent, fractional, listed, counts)
     close = lax.ppermute(to_close, "core", swap)
     table = tables(wave_index, fractional)
     summed = plane_sum(chip)

time: 131 us -> 131 us (level)
  transfers between devices with their start and end apart: 6 -> 6, of which waited for: 2 -> 2; matrix products, arithmetic and copies ran while one was open for 1% -> 1% of each run, Pallas kernels for 12% -> 13%
where the time goes in v8:
time: 131 us; the launch traced here: 130 us
  waiting for transfers between devices  46 us (35%)
  starting transfers between devices  39 us (30%)
  Pallas kernels  26 us (20%)
  blocking collectives  13.8 us (11%)
  local copies, waits for them, and re-layouts  3.34 us (3%)
  between operations  1.48 us (1%)
    ppermute x1, waiting for transfers between devices, body(): lax.ppermute(to_far, FINE, [(i, (i + (1 if i % 2 else -1)) % size) for i...  37.6 us
    all_to_all x1, blocking collectives, body(): chip = lax.all_to_all(total, ('y', 'x'), 0, 0, tiled=True)  13.8 us
    all_to_all x1, starting transfers between devices, body(): parts = lax.all_to_all(summed, ALONG_Z, 0, 0, tiled=True)  13.4 us
    ppermute x1, starting transfers between devices, body(): lax.ppermute(to_far, FINE, [(i, (i + (1 if i % 2 else -1)) % size) for i...  9.2 us
    ppermute x1, starting transfers between devices, body(): given = lax.ppermute(given, 'core', swap)  8.75 us
    all_to_all x1, waiting for transfers between devices, body(): lax.all_to_all(coefficients(parts, scale), ('y', 'x'), 0, 0, tiled=True)  8.38 us
    pallas_call x2, Pallas kernels, partial_sums(): pl.pallas_call(sums_kernel, out_shape=jax.ShapeDtypeStruct((16, 16, 8, 12...  5.62 us
    pallas_call x1, Pallas kernels, near_ahead(): pl.pallas_call(functools.partial(ahead_kernel, atoms_all=atoms_all), out_...  5.21 us
  transfers between devices with their start and end apart: 6, of which 2 were waited for; matrix products, arithmetic and copies ran while one was open for 1% of the time, Pallas kernels for 13%

profile of v8, /device:TPU:1, one launch (start us, length us, event | category | flops | bytes accessed | tf_op | source)
XLA Modules:
  0.0 130.5 jit_solution(17168374900264382226)
XLA Ops:
  0.6 0.0 copy-start.3
  0.6 0.0 copy-start.5
  0.7 3.2 %sums.3 = f32[16,16,8,128]{3,2,1,0:T(8,128)S(1)} custom-call(s32[1]{0:T(128)S(6)} %sub.4.seat.which, s32[3,512]{1,0:T(4,128)} %waves.1, bf16[3,1024]{1,0:T(4,128)(2,1)} %places.5, bf16[1024,256]{1,0:T(8,128)(2,1)} %embedding.5, bf16[1024,256]{1,0:T(8,128)(2,1)} %cotangent.5), custom_call_target="tpu_custom_call" | custom-call | flops 536870912 | bytes 2097152 | tf_op jit(solution)/shard_map/sums/pallas_call | solution.py:97
  3.8 8.7 %collective-permute-start = (f32[16,16,8,128]{3,2,1,0:T(8,128)S(1)}, f32[16,16,8,128]{3,2,1,0:T(8,128)S(1)}, u32[]{:S(2)}, u32[]{:S(2)}) collective-permute-start(f32[16,16,8,128]{3,2,1,0:T(8,128)S(1)} %sums.3), channel_id=1, source_target_pairs={{0,1},{1,0},{2,3},{3,2},{4,5},{5,4},{6,7},{7,6},{8,9},{9,8},{10,11... | collective-permute-start | bytes 3145736 | tf_op jit(solution)/shard_map/ppermute | solution.py:511
  12.6 2.5 %sums.2.a = f32[16,16,8,128]{3,2,1,0:T(8,128)S(1)} custom-call(s32[1]{0:T(128)} %bitcast.seat.which, s32[3,512]{1,0:T(4,128)S(1)} %copy-done.5, bf16[3,1024]{1,0:T(4,128)(2,1)S(1)} %copy-done.3, bf16[1024,256]{1,0:T(8,128)(2,1)} %embedding.5, bf16[1024,256]{1,0:T(8,128)(2,1)} %cotangent.5), custom_call_target="tpu_custom_call" | custom-call | flops 536870912 | bytes 2097152 | tf_op jit(solution)/shard_map/sums/pallas_call | solution.py:97
  15.1 0.0 collective-permute-done.b
  15.1 0.2 add.11
  15.2 13.8 %all_to_all.15.a = bf16[16,16,8,128]{3,2,1,0:T(8,128)(2,1)S(1)} all-to-all(bf16[16,16,8,128]{3,2,1,0:T(8,128)(2,1)S(1)} %add.11), channel_id=1, replica_groups=mesh['z_lo'=4,'y'=4,'x'=4,'z_hi'=4,'core'=2] {'y','x'}, dimensions={0} | all-to-all | bytes 1048576 | tf_op jit(solution)/shard_map/all_to_all | solution.py:514
  29.1 0.9 plane_sum.1
  30.0 13.4 %all-to-all-start.1 = ((bf16[16,16,8,128]{3,2,1,0:T(8,128)(2,1)}), bf16[16,16,8,128]{3,2,1,0:T(8,128)(2,1)S(1)}, u32[]{:S(2)}, u32[]{:S(2)}) async-start(bf16[16,16,8,128]{3,2,1,0:T(8,128)(2,1)} %plane_sum.1), calls=%async_computation.1 | async-start | bytes 1048576 | tf_op jit(solution)/shard_map/all_to_all | solution.py:519
  44.0 1.1 pack.2
  45.1 9.2 %collective-permute-start.1 = (bf16[1056,256]{1,0:T(8,128)(2,1)S(1)}, bf16[1056,256]{1,0:T(8,128)(2,1)S(1)}, u32[]{:S(2)}, u32[]{:S(2)}) collective-permute-start(bf16[1056,256]{1,0:T(8,128)(2,1)S(1)} %pack.2), channel_id=1, source_target_pairs={{0,511},{1,2},{2,1},{3,4},{4,3},{5,6},{6,5},{7,8},{8,7},{9,10},{10... | collective-permute-start | bytes 1622024 | tf_op jit(solution)/shard_map/ppermute | solution.py:509
  54.3 1.1 pack.3
  55.5 1.9 %collective-permute-start.2 = (bf16[1056,256]{1,0:T(8,128)(2,1)S(1)}, bf16[1056,256]{1,0:T(8,128)(2,1)}, u32[]{:S(2)}, u32[]{:S(2)}) collective-permute-start(bf16[1056,256]{1,0:T(8,128)(2,1)S(1)} %pack.3), channel_id=1, source_target_pairs={{0,1},{1,0},{2,3},{3,2},{4,5},{5,4},{6,7},{7,6},{8,9},{9,8},{10,11... | collective-permute-start | bytes 1622024 | tf_op jit(solution)/shard_map/ppermute | solution.py:516
  57.4 0.1 pad_add_fusion.seat
  57.5 37.6 %collective-permute-done.1.far = bf16[1056,256]{1,0:T(8,128)(2,1)S(1)} collective-permute-done((bf16[1056,256]{1,0:T(8,128)(2,1)S(1)}, bf16[1056,256]{1,0:T(8,128)(2,1)S(1)}, u32[]{:S(2)}, u32[]{:S(2)}) %collective-permute-start.1) | collective-permute-done | bytes 540704 | tf_op jit(solution)/shard_map/ppermute | solution.py:509
  95.1 0.0 collective-permute-done.2.close
  95.1 0.8 copy-done.8
  96.0 5.2 %near_ahead.1 = (f32[1024,256]{1,0:T(8,128)S(1)}, f32[16,8,128]{2,1,0:T(8,128)S(1)}) custom-call(s32[2]{0:T(128)S(1)} %pad_add_fusion.seat, s32[2,24]{1,0:T(2,128)S(1)} %bitcast.9, s32[1]{0:T(128)S(6)} %copy.10.count, bf16[1024,256]{1,0:T(8,128)(2,1)S(1)} %copy-done, bf16[1056,256]{1,0:T(8,128)(2,1)} %copy-done.8, ...), custom_call_target="tpu_custom_call" | custom-call | flops 5368709120 | bytes 2097152 | tf_op jit(solution)/shard_map/near_ahead/pallas_call | solution.py:405
  101.2 1.0 copy-done.1
  102.2 0.0 all-to-all-done.1.a
  102.2 0.9 coefficients.1
  103.1 3.6 %all-to-all-start.2 = ((bf16[16,16,8,128]{3,2,1,0:T(8,128)(2,1)}), bf16[16,16,8,128]{3,2,1,0:T(8,128)(2,1)S(1)}, u32[]{:S(2)}, u32[]{:S(2)}) async-start(bf16[16,16,8,128]{3,2,1,0:T(8,128)(2,1)} %coefficients.1), calls=%async_computation.2 | async-start | bytes 1048576 | tf_op jit(solution)/shard_map/all_to_all | solution.py:528
  106.7 3.0 %table.1 = bf16[1024,1024]{1,0:T(8,128)(2,1)S(1)} custom-call(s32[3,512]{1,0:T(4,128)S(1)} %copy-done.5, bf16[3,1024]{1,0:T(4,128)(2,1)S(1)} %copy-done.4), custom_call_target="tpu_custom_call" | custom-call | flops 6442450944 | bytes 2097152 | tf_op jit(solution)/shard_map/table/pallas_call | solution.py:194
  109.7 8.4 %all-to-all-done.2 = bf16[16,16,8,128]{3,2,1,0:T(8,128)(2,1)S(1)} async-done(((bf16[16,16,8,128]{3,2,1,0:T(8,128)(2,1)}), bf16[16,16,8,128]{3,2,1,0:T(8,128)(2,1)S(1)}, u32[]{:S(2)}, u32[]{:S(2)}) %all-to-all-start.2) | async-done | bytes 524320 | tf_op jit(solution)/shard_map/all_to_all | solution.py:528
  118.1 2.2 %collective-permute-start.3 = (bf16[256,8,128]{2,1,0:T(8,128)(2,1)S(1)}, bf16[256,8,128]{2,1,0:T(8,128)(2,1)S(1)}, u32[]{:S(2)}, u32[]{:S(2)}) collective-permute-start(bf16[256,8,128]{2,1,0:T(8,128)(2,1)S(1)} %bitcast.5), channel_id=1, source_target_pairs={{0,1},{1,0},{2,3},{3,2},{4,5},{5,4},{6,7},{7,6},{8,9},{9,8},{10,11... | collective-permute-start | bytes 1572872 | tf_op jit(solution)/shard_map/ppermute | solution.py:529
  120.3 0.7 fusion
  121.0 0.5 slice.19
  121.5 4.3 %near_behind.1.mixed = f32[1024,256]{1,0:T(8,128)S(1)} custom-call(s32[1]{0:T(128)} %bitcast.seat.which, s32[2,24]{1,0:T(2,128)S(1)} %bitcast.10, s32[1]{0:T(128)S(6)} %copy.10.count, s32[2,24]{1,0:T(2,128)S(1)} %slice.18.pairs_below, s32[1]{0:T(128)} %bitcast.4.count_below, bf16[1024,256]{1,0:T(8,128)(2,1)} %cotangent.5, bf16[1056,256]{1,0:T(8,128)(2,1)} %copy-done.8, ...), custom_call_target="tpu_custom_call" | custom-call | flops 5368709120 | bytes 2097152 | tf_op jit(solution)/shard_map/near_behind/pallas_call | solution.py:433
  125.8 1.0 copy-done.2
  126.8 0.0 collective-permute-done.3.other
  126.8 3.7 %final.1 = (bf16[1024,256]{1,0:T(8,128)(2,1)}, bf16[1024,256]{1,0:T(8,128)(2,1)}) custom-call(s32[2]{0:T(128)S(1)} %pad_add_fusion.seat, bf16[256,8,128]{2,1,0:T(8,128)(2,1)S(1)} %bitcast.6, bf16[256,8,128]{2,1,0:T(8,128)(2,1)S(1)} %collective-permute-done.3.other, bf16[1024,1024]{1,0:T(8,128)(2,1)S(1)} %table.1, f32[1024,256]{1,0:T(8,128)} %copy-done.1, ...), custom_call_target="tpu_custom_call" | custom-call | flops 1073741824 | bytes 4194304 | tf_op jit(solution)/shard_map/final/pallas_call | solution.py:477
  (14 shorter events, 0.0 us)
Async XLA Ops:
  0.6 12.0 %copy-start.3 = (bf16[3,1024]{1,0:T(4,128)(2,1)S(1)}, bf16[3,1024]{1,0:T(4,128)(2,1)}, u32[]{:S(2)}) copy-start(bf16[3,1024]{1,0:T(4,128)(2,1)} %places.5) | copy-start | bytes 18436
  0.6 12.0 %copy-start.5 = (s32[3,512]{1,0:T(4,128)S(1)}, s32[3,512]{1,0:T(4,128)}, u32[]{:S(2)}) copy-start(s32[3,512]{1,0:T(4,128)} %waves.1) | copy-start | bytes 18436
  3.8 11.2 %collective-permute-start = (f32[16,16,8,128]{3,2,1,0:T(8,128)S(1)}, f32[16,16,8,128]{3,2,1,0:T(8,128)S(1)}, u32[]{:S(2)}, u32[]{:S(2)}) collective-permute-start(f32[16,16,8,128]{3,2,1,0:T(8,128)S(1)} %sums.3), channel_id=1, source_target_pairs={{0,1},{1,0},{2,3},{3,2},{4,5},{5,4},{6,7},{7,6},{8,9},{9,8},{10,11... | collective-permute-start | bytes 3145736 | tf_op jit(solution)/shard_map/ppermute | solution.py:511
  30.0 66.0 %copy-start = (bf16[1024,256]{1,0:T(8,128)(2,1)S(1)}, bf16[1024,256]{1,0:T(8,128)(2,1)}, u32[]{:S(2)}) copy-start(bf16[1024,256]{1,0:T(8,128)(2,1)} %embedding.5) | copy-start | bytes 1572868
  30.0 66.0 %copy-start.4 = (bf16[3,1024]{1,0:T(4,128)(2,1)S(1)}, bf16[3,1024]{1,0:T(4,128)(2,1)}, u32[]{:S(2)}) copy-start(bf16[3,1024]{1,0:T(4,128)(2,1)} %places.5) | copy-start | bytes 18436
  30.0 66.0 %copy-start.6 = (s32[24,2]{0,1:T(2,128)S(1)}, s32[24,2]{0,1:T(2,128)}, u32[]{:S(2)}) copy-start(s32[24,2]{0,1:T(2,128)} %param.12) | copy-start | bytes 580
  30.0 66.0 %copy-start.7 = (bf16[256,256]{1,0:T(8,128)(2,1)S(1)}, bf16[256,256]{1,0:T(8,128)(2,1)}, u32[]{:S(2)}) copy-start(bf16[256,256]{1,0:T(8,128)(2,1)} %weight.3) | copy-start | bytes 393220
  30.0 72.2 %all-to-all-start.1 = ((bf16[16,16,8,128]{3,2,1,0:T(8,128)(2,1)}), bf16[16,16,8,128]{3,2,1,0:T(8,128)(2,1)S(1)}, u32[]{:S(2)}, u32[]{:S(2)}) async-start(bf16[16,16,8,128]{3,2,1,0:T(8,128)(2,1)} %plane_sum.1), calls=%async_computation.1 | async-start | bytes 1048576 | tf_op jit(solution)/shard_map/all_to_all | solution.py:519
  45.1 50.0 %collective-permute-start.1 = (bf16[1056,256]{1,0:T(8,128)(2,1)S(1)}, bf16[1056,256]{1,0:T(8,128)(2,1)S(1)}, u32[]{:S(2)}, u32[]{:S(2)}) collective-permute-start(bf16[1056,256]{1,0:T(8,128)(2,1)S(1)} %pack.2), channel_id=1, source_target_pairs={{0,511},{1,2},{2,1},{3,4},{4,3},{5,6},{6,5},{7,8},{8,7},{9,10},{10... | collective-permute-start | bytes 1622024 | tf_op jit(solution)/shard_map/ppermute | solution.py:509
  55.5 39.7 %collective-permute-start.2 = (bf16[1056,256]{1,0:T(8,128)(2,1)S(1)}, bf16[1056,256]{1,0:T(8,128)(2,1)}, u32[]{:S(2)}, u32[]{:S(2)}) collective-permute-start(bf16[1056,256]{1,0:T(8,128)(2,1)S(1)} %pack.3), channel_id=1, source_target_pairs={{0,1},{1,0},{2,3},{3,2},{4,5},{5,4},{6,7},{7,6},{8,9},{9,8},{10,11... | collective-permute-start | bytes 1622024 | tf_op jit(solution)/shard_map/ppermute | solution.py:516
  95.1 0.8 copy-start.8
  101.2 1.0 copy-start.1
  103.1 15.0 %all-to-all-start.2 = ((bf16[16,16,8,128]{3,2,1,0:T(8,128)(2,1)}), bf16[16,16,8,128]{3,2,1,0:T(8,128)(2,1)S(1)}, u32[]{:S(2)}, u32[]{:S(2)}) async-start(bf16[16,16,8,128]{3,2,1,0:T(8,128)(2,1)} %coefficients.1), calls=%async_computation.2 | async-start | bytes 1048576 | tf_op jit(solution)/shard_map/all_to_all | solution.py:528
  118.1 8.7 %collective-permute-start.3 = (bf16[256,8,128]{2,1,0:T(8,128)(2,1)S(1)}, bf16[256,8,128]{2,1,0:T(8,128)(2,1)S(1)}, u32[]{:S(2)}, u32[]{:S(2)}) collective-permute-start(bf16[256,8,128]{2,1,0:T(8,128)(2,1)S(1)} %bitcast.5), channel_id=1, source_target_pairs={{0,1},{1,0},{2,3},{3,2},{4,5},{5,4},{6,7},{7,6},{8,9},{9,8},{10,11... | collective-permute-start | bytes 1572872 | tf_op jit(solution)/shard_map/ppermute | solution.py:529
  125.8 1.0 copy-start.2
